TPU v7x, 128 devices: a whole 4x4x4 slice. The times are simulated.
128 devices in a mesh: row: 8 (over x, core), col: 16 (over z, y).
Axes of the slice: x: 4, y: 4, z: 4, core: 2. Of those that a mesh axis runs over, the one named last changes fastest.
Arguments:
- send_cells: int32 [128, 128, 512], P(('row', 'col')), may hold values from 0 to 65535, as said below
- send_species: int32 [128, 128, 512], P(('row', 'col')), may hold values from 0 to 5
- send_mix: bfloat16 [128, 6, 128, 512], P(('row', 'col')), may hold values from 0 to 0.5
- send_counts: int32 [128, 128], P(('row', 'col')), may hold values from 64 to 512, as said below
- chi: float32 [6, 6], replicated, may hold values from 0 to 8
Outputs:
- forces: float32 [128, 3, 128, 512], P(('row', 'col'))
Inputs may be any that keep to these rules, and one draw needn't show every extreme that they name: `send_cells`: local cell (x * 16 + y) * 256 + z in the destination brick; domain s (flat index) holds particles with z from s * 2 to (s + 1) * 2 - 1 only. `send_counts`: slots at or beyond the count are unused. At most 512 particles go from one domain to one brick; in every draw some domain fills a slot list, and one brick receives 512 from every domain.
All inputs are finite; a program needn't handle non-finite values.
Results may differ from a plain program's by a relative error of at most 0.0023.
Values may be sent and summed in bfloat16 or wider, within the bound.
No kernel may reach another device: no remote copies, remote signals or barrier semaphores. Data moves between devices by JAX's collectives and lax.ppermute only.
A program may use at most 256 MiB of HBM per device.

v0:
```python
import jax
import jax.numpy as jnp
from jax import lax
from jax.sharding import PartitionSpec as P

SPECIES = 6
BX = 16
BY = 16
NZ = 256


raw_taps = (0.1353352832366127, 0.6065306597126334, 1.0, 0.6065306597126334, 0.1353352832366127)
tap_total = sum(raw_taps)
taps = tuple((t / tap_total for t in raw_taps))
rho_ref = 2.0
inv_kappa = 1.0


def cut_along(value, dim, count):
    before, after = (value.shape[:dim], value.shape[dim + 1 :])
    return jnp.moveaxis(value.reshape(*before, count, -1, *after), dim, 0)


def laid_out(blocks, dim):
    blocks = jnp.moveaxis(blocks, 0, dim)
    lengths = blocks.shape
    return blocks.reshape(*lengths[:dim], lengths[dim] * lengths[dim + 1], *lengths[dim + 2 :])


def exchange_both(value, axis, axes, splits, concats):
    sizes = [lax.axis_size(a) for a in axes]
    blocks = cut_along(value, splits[0], sizes[0])
    blocks = jnp.moveaxis(cut_along(blocks, splits[1] + 1, sizes[1]), 0, 1)
    inside = blocks.shape[2:]
    blocks = blocks.reshape(-1, *inside)
    blocks = lax.all_to_all(blocks, axis, split_axis=0, concat_axis=0, tiled=True)
    blocks = laid_out(blocks.reshape(*sizes, *inside), concats[0] + 1)
    return laid_out(blocks, concats[1])


def extended_2(value, sides, width):
    for axis, dim in sides:
        count, length = (lax.axis_size(axis), value.shape[dim])
        up = [(i, (i + 1) % count) for i in range(count)]
        down = [(j, i) for i, j in up]
        last = lax.slice_in_dim(value, length - width, length, axis=dim)
        first = lax.slice_in_dim(value, 0, width, axis=dim)
        before = lax.ppermute(last, axis, up)
        after = lax.ppermute(first, axis, down)
        value = jnp.concatenate([before, value, after], axis=dim)
    return value


def padded_2(value, sides, width):
    edges = {}
    for axis, dim in sides:
        count, length = (lax.axis_size(axis), value.shape[dim])
        up = [(i, (i + 1) % count) for i in range(count)]
        last = lax.slice_in_dim(value, length - width, length, axis=dim)
        first = lax.slice_in_dim(value, 0, width, axis=dim)
        edges[dim] = (
            lax.ppermute(last, axis, up),
            lax.ppermute(first, axis, [(b, a) for a, b in up]),
        )
    done = []
    for _, dim in sides:
        low, high = edges[dim]
        around = [(width, width) if d in done else (0, 0) for d in range(value.ndim)]
        value = jnp.concatenate([jnp.pad(low, around), value, jnp.pad(high, around)], axis=dim)
        done.append(dim)
    return value


def smooth(padded):
    width_x = padded.shape[1] - 4
    width_y = padded.shape[2] - 4
    along_x = taps[0] * padded[:, 0:width_x]
    for t in range(1, 5):
        along_x = along_x + taps[t] * padded[:, t : t + width_x]
    along_y = taps[0] * along_x[:, :, 0:width_y]
    for t in range(1, 5):
        along_y = along_y + taps[t] * along_x[:, :, t : t + width_y]
    along_z = taps[0] * jnp.roll(along_y, 2, axis=3)
    for t in range(1, 5):
        along_z = along_z + taps[t] * jnp.roll(along_y, 2 - t, axis=3)
    return along_z


def potential_of(filtered, chi):
    count = chi.shape[0]
    chis = 0.5 * (chi + chi.T) * (1.0 - jnp.eye(count, dtype=jnp.float32))
    mixing = jnp.einsum("kl,lxyz->kxyz", chis, filtered, precision=lax.Precision.HIGHEST) / rho_ref
    total = jnp.sum(filtered, axis=0) / rho_ref
    return mixing + inv_kappa * (total[None] - 1.0)


def deposit(weights, plane_idx, z_offset, plane, band, blocks):
    sources = plane_idx.shape[0]
    rows = plane_idx.shape[1]
    per = sources // blocks
    w_blocks = jnp.moveaxis(weights.reshape(SPECIES, blocks, per, rows), 1, 0)
    i_blocks = plane_idx.reshape(blocks, per, rows)
    z_blocks = z_offset.reshape(blocks, per, rows)
    plane_ids = jnp.arange(plane, dtype=jnp.int32)
    band_ids = jnp.arange(band, dtype=jnp.int32)

    def deposit_one_block(carry, item):
        w_b, i_b, z_b = item
        table = (i_b[:, :, None] == plane_ids[None, None, :]).astype(jnp.bfloat16)
        banded = jnp.where(
            z_b[None, :, :, None] == band_ids[None, None, None, :],
            w_b[:, :, :, None],
            jnp.zeros((), jnp.bfloat16),
        )
        return (
            carry,
            jnp.einsum("kbpz,bpc->bkzc", banded, table, preferred_element_type=jnp.float32),
        )

    unused, tiles = lax.scan(deposit_one_block, 0, (w_blocks, i_blocks, z_blocks))
    tiles = tiles.reshape(sources, SPECIES, band, plane)
    return jnp.transpose(tiles, (1, 3, 0, 2)).reshape(SPECIES, plane, sources * band)


def pick_forces(grads, plane_idx, z_offset, weights_f, blocks):
    sources = plane_idx.shape[0]
    rows = plane_idx.shape[1]
    plane = grads.shape[2]
    band = grads.shape[3] // sources
    per = sources // blocks
    tiles = jnp.transpose(grads.reshape(3 * SPECIES, plane, sources, band), (2, 0, 3, 1))
    g_blocks = tiles.reshape(blocks, per, 3 * SPECIES, band, plane)
    i_blocks = plane_idx.reshape(blocks, per, rows)
    z_blocks = z_offset.reshape(blocks, per, rows)
    w_blocks = jnp.moveaxis(weights_f.reshape(SPECIES, blocks, per, rows), 0, 2)
    plane_ids = jnp.arange(plane, dtype=jnp.int32)
    band_ids = jnp.arange(band, dtype=jnp.int32)

    def pick_one_block(carry, item):
        g_b, i_b, z_b, w_b = item
        table = (i_b[:, :, None] == plane_ids[None, None, :]).astype(jnp.float32)
        values = jnp.einsum("bjzc,bpc->bjzp", g_b, table, precision=lax.Precision.HIGHEST)
        chosen = jnp.sum(
            jnp.where(z_b[:, None, None, :] == band_ids[None, None, :, None], values, 0.0), axis=2
        )
        chosen = chosen.reshape(per, 3, SPECIES, rows)
        return (carry, -jnp.sum(w_b[:, None] * chosen, axis=2))

    unused, result = lax.scan(pick_one_block, 0, (g_blocks, i_blocks, z_blocks, w_blocks))
    return jnp.transpose(result.reshape(sources, 3, rows), (1, 0, 2))


def body(send_cells, send_species, send_mix, send_counts, chi):
    species = send_species[0]
    mixture = send_mix[0]
    counts = send_counts[0]
    domains = mixture.shape[1]
    slots = mixture.shape[2]
    row_size = lax.axis_size("row")
    col_size = lax.axis_size("col")
    band = NZ // domains
    valid = jnp.arange(slots, dtype=jnp.int32)[None, :] < counts[:, None]
    onehot = (species[None] == jnp.arange(SPECIES, dtype=jnp.int32)[:, None, None]).astype(
        jnp.float32
    )
    weights = jnp.where(valid[None], onehot + mixture.astype(jnp.float32), 0.0).astype(jnp.bfloat16)
    split_w = weights.reshape(SPECIES, row_size, col_size, slots)
    split_c = send_cells.reshape(1, row_size, col_size, slots)
    got_w4, got_c4 = (
        exchange_both(split_w, ("row", "col"), ("row", "col"), (1, 2), (1, 2)),
        exchange_both(split_c, ("row", "col"), ("row", "col"), (1, 2), (1, 2)),
    )
    got_weights = got_w4.reshape(SPECIES, domains, slots)
    got_cells = got_c4.reshape(1, domains, slots)
    place = got_cells.reshape(domains, slots)
    density = deposit(
        got_weights, place // NZ, place % NZ % band, BX * BY, band, max(1, domains // 8)
    )
    density = density.reshape(SPECIES, BX, BY, NZ)
    flat_w = got_weights.astype(jnp.float32)
    padded = extended_2(density, (("row", 1), ("col", 2)), 2)
    potential = potential_of(smooth(padded), chi)
    extended = padded_2(potential, (("row", 1), ("col", 2)), 1)
    center = extended[:, 1:-1, 1:-1]
    grad_x = 0.5 * (extended[:, 2:, 1:-1] - extended[:, :-2, 1:-1])
    grad_y = 0.5 * (extended[:, 1:-1, 2:] - extended[:, 1:-1, :-2])
    grad_z = 0.5 * (jnp.roll(center, -1, axis=3) - jnp.roll(center, 1, axis=3))
    grads = jnp.stack((grad_x, grad_y, grad_z), axis=0).reshape(3, SPECIES, BX * BY, NZ)
    slot_forces = pick_forces(grads, place // NZ, place % NZ % band, flat_w, max(1, domains // 8))
    split_f = slot_forces.reshape(3, row_size, col_size, slots)
    returned = exchange_both(split_f, ("row", "col"), ("row", "col"), (1, 2), (1, 2)).reshape(
        3, domains, slots
    )
    return returned[None]


def solution(mesh):
    return jax.shard_map(
        body,
        mesh=mesh,
        in_specs=(
            P(("row", "col"), None, None),
            P(("row", "col"), None, None),
            P(("row", "col"), None, None, None),
            P(("row", "col"), None),
            P(),
        ),
        out_specs=P(("row", "col"), None, None, None),
        check_vma=False,
    )
```

profile of v0, /device:TPU:1, one launch (start us, length us, event | category | flops | bytes accessed | tf_op | source)
XLA Modules:
  0.0 312.3 jit_solution(3904315143548767812)
XLA Ops:
  0.0 1.9 reshape_transpose_transpose_reshape_transpose_reshape_reshape.3
  1.9 11.5 %all-to-all-start.1 = ((s32[128,1,1,1,512]{4,3,2,1,0:T(1,128)}), s32[128,1,1,1,512]{4,3,2,1,0:T(1,128)S(1)}, u32[]{:S(2)}, u32[]{:S(2)}) async-start(s32[128,1,1,1,512]{4,3,2,1,0:T(1,128)} %reshape_transpose_transpose_reshape_transpose_reshape_reshape.3), calls=%async_computation.1 | async-start | bytes 524288 | tf_op jit(solution)/shard_map/all_to_all | solution.py:36
  15.4 1.3 convert.2
  16.8 2.5 fusion.49
  19.3 5.5 %all-to-all-done.1 = s32[128,1,1,1,512]{4,3,2,1,0:T(1,128)S(1)} async-done(((s32[128,1,1,1,512]{4,3,2,1,0:T(1,128)}), s32[128,1,1,1,512]{4,3,2,1,0:T(1,128)S(1)}, u32[]{:S(2)}, u32[]{:S(2)}) %all-to-all-start.1) | async-done | bytes 262176 | tf_op jit(solution)/shard_map/all_to_all | solution.py:36
  24.8 4.3 %all-to-all-start = ((bf16[128,6,1,1,512]{4,1,3,2,0:T(8,128)(2,1)}), bf16[128,6,1,1,512]{4,1,3,2,0:T(8,128)(2,1)S(1)}, u32[]{:S(2)}, u32[]{:S(2)}) async-start(bf16[128,6,1,1,512]{4,1,3,2,0:T(8,128)(2,1)} %bitcast.5), calls=%async_computation | async-start | bytes 2097152 | tf_op jit(solution)/shard_map/all_to_all | solution.py:36
  29.4 18.5 %all-to-all-done = bf16[128,6,1,1,512]{4,1,3,2,0:T(8,128)(2,1)S(1)} async-done(((bf16[128,6,1,1,512]{4,1,3,2,0:T(8,128)(2,1)}), bf16[128,6,1,1,512]{4,1,3,2,0:T(8,128)(2,1)S(1)}, u32[]{:S(2)}, u32[]{:S(2)}) %all-to-all-start) | async-done | bytes 786464 | tf_op jit(solution)/shard_map/all_to_all | solution.py:36
  48.0 28.4 %while.22 = (s32[]{:T(128)}, f32[16,8,6,2,256]{4,2,3,1,0:T(8,128)}, s32[16,8,512]{2,1,0:T(8,128)S(1)}, bf16[16,6,8,512]{3,1,2,0:T(8,128)(2,1)S(1)}, s32[16,8,512]{2,1,0:T(8,128)S(1)}, /*index=5*/s32[]{:T(128)}) while((s32[]{:T(128)}, f32[16,8,6,2,256]{4,2,3,1,0:T(8,128)}, s32[16,8,512]{2,1,0:T(8,128)S(1)}, ...), condition=%wide.region_1.2_spmd.clone, body=%wide.region_0.1_spmd.clone.sunk | while | flops 26271744 | bytes 393805 | solution.py:120
  48.0 1.7 fusion.90
  49.8 1.7 fusion.90
  51.6 1.7 fusion.90
  53.3 1.7 fusion.90
  55.1 1.7 fusion.90
  56.9 1.7 fusion.90
  58.7 1.7 fusion.90
  60.4 1.7 fusion.90
  62.2 1.7 fusion.90
  64.0 1.7 fusion.90
  65.8 1.7 fusion.90
  67.5 1.7 fusion.90
  69.3 1.7 fusion.90
  71.1 1.7 fusion.90
  72.9 1.7 fusion.90
  74.6 1.7 fusion.90
  77.5 2.4 copy.195
  79.9 7.0 %reshape_reshape.11 = f32[6,16,16,256]{2,1,3,0:T(8,128)} reshape(f32[6,256,128,2]{1,3,2,0:T(2,128)S(1)} %bitcast.156) | data formatting | bytes 3145728 | tf_op jit(solution)/shard_map/reshape;reshape | solution.py:179
  86.8 5.9 %fusion.75 = (f32[6,2,16,256]{2,1,3,0:T(2,128)S(1)}, f32[6,2,16,256]{2,1,3,0:T(2,128)S(1)}) fusion(f32[6,16,16,256]{2,1,3,0:T(8,128)} %reshape_reshape.11), kind=kLoop, calls=%fused_computation.122 | loop fusion | bytes 786432 | tf_op jit(solution)/shard_map/slice | solution.py:46
  92.7 1.7 copy.150
  94.4 1.5 collective-permute-start
  96.6 8.9 %copy.152 = f32[6,16,16,256]{3,2,1,0:T(8,128)S(1)} copy(f32[6,16,16,256]{2,1,3,0:T(8,128)} %reshape_reshape.11) | data formatting | bytes 3145728 | tf_op jit(solution)/shard_map/reshape;reshape | solution.py:179
  106.1 4.4 %collective-permute-start.3 = (f32[6,20,2,256]{3,2,1,0:T(2,128)S(1)}, f32[6,20,2,256]{3,2,1,0:T(2,128)S(1)}, u32[]{:S(2)}, u32[]{:S(2)}) collective-permute-start(f32[6,20,2,256]{3,2,1,0:T(2,128)S(1)} %get-tuple-element.243), channel_id=1, source_target_pairs={{1,0},{2,1},{3,2},{4,3},{5,4},{6,5},{7,6},{8,7},{9,8},{10,9},{11,1... | collective-permute-start | bytes 737288 | tf_op jit(solution)/shard_map/ppermute | solution.py:49
  110.5 1.4 convert_bitcast_fusion
  111.9 2.2 collective-permute-done.2
  117.8 2.2 fusion.73
  120.0 2.9 multiply_add_fusion
  124.3 2.7 slice_bitcast_fusion
  128.3 3.8 %collective-permute-start.4 = (f32[6,1,16,256]{3,0,2,1:T(8,128)}, f32[6,1,16,256]{3,0,2,1:T(8,128)}, u32[]{:S(2)}, u32[]{:S(2)}) collective-permute-start(f32[6,1,16,256]{3,0,2,1:T(8,128)} %get-tuple-element.237), channel_id=1, source_target_pairs={{16,0},{32,16},{48,32},{64,48},{80,64},{96,80},{112,96},{0,112},{1... | collective-permute-start | bytes 294920 | tf_op jit(solution)/shard_map/ppermute | solution.py:63
  132.1 5.1 %collective-permute-start.6 = (f32[6,16,1,256]{3,0,2,1:T(8,128)}, f32[6,16,1,256]{3,0,2,1:T(8,128)}, u32[]{:S(2)}, u32[]{:S(2)}) collective-permute-start(f32[6,16,1,256]{3,0,2,1:T(8,128)} %get-tuple-element.234), channel_id=1, source_target_pairs={{1,0},{2,1},{3,2},{4,3},{5,4},{6,5},{7,6},{8,7},{9,8},{10,9},{11,1... | collective-permute-start | bytes 294920 | tf_op jit(solution)/shard_map/ppermute | solution.py:63
  137.2 1.9 copy.156
  139.0 1.6 copy.157
  142.0 3.5 %fusion.45 = f32[1,6,16,16,256]{4,1,3,2,0:T(8,128)S(1)} fusion(f32[1,6,16,16,1]{4,1,3,2,0:T(8,128)} %copy.157, f32[1,6,16,16,255]{4,1,3,2,0:T(8,128)} %get-tuple-element.241, f32[1,6,16,16,255]{4,1,3,2,0:T(8,128)} %get-tuple-element.240, f32[1,6,16,16,1]{4,1,3,2,0:T(8,128)S(1)} %copy.159), kind=kLoop, calls=%fused_computation.65 | loop fusion | flops 1572864 | bytes 4718592 | tf_op jit(solution)/shard_map/mul | solution.py:187
  145.5 2.0 fusion.44
  147.5 3.4 %pad_maximum_fusion = f32[3,6,16,16,256]{4,1,3,2,0:T(8,128)} fusion(f32[1,6,16,16,256]{4,1,3,2,0:T(8,128)S(1)} %fusion.45, f32[1,6,16,16,256]{4,1,3,2,0:T(8,128)S(1)} %get-tuple-element.233, f32[1,6,16,16,256]{4,1,3,2,0:T(8,128)S(1)} %get-tuple-element.232), kind=kLoop, calls=%fused_computation.33 | loop fusion | flops 2359296 | bytes 9437184 | tf_op jit(solution)/shard_map/stack | solution.py:188
  150.9 18.7 %copy.160 = f32[3,6,16,16,256]{3,2,4,1,0:T(8,128)} copy(f32[3,6,16,16,256]{4,1,3,2,0:T(8,128)} %pad_maximum_fusion) | data formatting | bytes 9437184 | tf_op jit(solution)/shard_map/stack | solution.py:188
  169.6 28.1 %reshape_reshape.12 = f32[18,256,128,2]{1,3,2,0:T(2,128)} reshape(f32[3,6,16,16,256]{3,2,4,1,0:T(8,128)} %copy.160) | data formatting | bytes 9437184 | tf_op jit(solution)/shard_map/reshape;reshape | solution.py:131
  197.7 86.5 %while.23 = (s32[]{:T(128)}, f32[16,8,3,512]{3,1,0,2:T(8,128)S(1)}, f32[16,8,6,512]{3,1,0,2:T(8,128)}, s32[16,8,512]{2,1,0:T(8,128)}, f32[16,8,18,2,256]{4,3,1,0...) while((s32[]{:T(128)}, f32[16,8,3,512]{3,1,0,2:T(8,128)S(1)}, f32[16,8,6,512]{3,1,0,2:T(8,128)}, ...), condition=%wide.region_6.7_spmd.clone, body=%wide.region_3.6_spmd.clone.sunk | while | flops 454410240 | bytes 2621533 | solution.py:149
  199.4 2.5 fusion.92
  204.8 2.5 fusion.92
  210.2 2.5 fusion.92
  215.7 2.5 fusion.92
  221.1 2.5 fusion.92
  226.5 2.5 fusion.92
  231.9 2.5 fusion.92
  237.3 2.5 fusion.92
  242.7 2.5 fusion.92
  248.1 2.5 fusion.92
  253.5 2.5 fusion.92
  258.9 2.5 fusion.92
  264.3 2.5 fusion.92
  269.7 2.5 fusion.92
  275.1 2.5 fusion.92
  280.5 2.5 fusion.92
  285.0 25.5 %all_to_all.15 = f32[128,3,1,1,512]{4,3,2,1,0:T(1,128)S(1)} all-to-all(f32[128,3,1,1,512]{4,3,2,1,0:T(1,128)S(1)} %bitcast.159), channel_id=1, replica_groups=mesh['row'=8,'col'=16] {'row','col'}, dimensions={0} | all-to-all | bytes 1572864 | tf_op jit(solution)/shard_map/all_to_all | solution.py:36
  311.0 1.3 copy.167
  (210 shorter events, 60.6 us)
Async XLA Ops:
  0.0 16.8 %copy-start.4 = (s32[1,128,512]{2,1,0:T(8,128)S(1)}, s32[1,128,512]{2,1,0:T(8,128)}, u32[]{:S(2)}) copy-start(s32[1,128,512]{2,1,0:T(8,128)} %param.10) | copy-start | bytes 786436
  1.9 22.9 %all-to-all-start.1 = ((s32[128,1,1,1,512]{4,3,2,1,0:T(1,128)}), s32[128,1,1,1,512]{4,3,2,1,0:T(1,128)S(1)}, u32[]{:S(2)}, u32[]{:S(2)}) async-start(s32[128,1,1,1,512]{4,3,2,1,0:T(1,128)} %reshape_transpose_transpose_reshape_transpose_reshape_reshape.3), calls=%async_computation.1 | async-start | bytes 524288 | tf_op jit(solution)/shard_map/all_to_all | solution.py:36
  24.8 23.2 %all-to-all-start = ((bf16[128,6,1,1,512]{4,1,3,2,0:T(8,128)(2,1)}), bf16[128,6,1,1,512]{4,1,3,2,0:T(8,128)(2,1)S(1)}, u32[]{:S(2)}, u32[]{:S(2)}) async-start(bf16[128,6,1,1,512]{4,1,3,2,0:T(8,128)(2,1)} %bitcast.5), calls=%async_computation | async-start | bytes 2097152 | tf_op jit(solution)/shard_map/all_to_all | solution.py:36
  76.4 1.0 copy-start
  76.4 1.1 copy-start.3
  92.7 3.8 %copy-start.5 = (f32[6,6]{1,0:T(8,128)S(1)}, f32[6,6]{1,0:T(8,128)}, u32[]{:S(2)}) copy-start(f32[6,6]{1,0:T(8,128)} %param.13) | copy-start | bytes 436
  94.4 11.1 %collective-permute-start = (f32[6,2,16,256]{3,2,1,0:T(8,128)}, f32[6,2,16,256]{3,2,1,0:T(8,128)S(1)}, u32[]{:S(2)}, u32[]{:S(2)}) collective-permute-start(f32[6,2,16,256]{3,2,1,0:T(8,128)} %copy.150), channel_id=1, source_target_pairs={{0,16},{16,32},{32,48},{48,64},{64,80},{80,96},{96,112},{112,0},{1... | collective-permute-start | bytes 589832 | tf_op jit(solution)/shard_map/ppermute | solution.py:48
  96.5 9.0 %collective-permute-start.1 = (f32[6,2,16,256]{3,2,1,0:T(8,128)S(1)}, f32[6,2,16,256]{3,2,1,0:T(8,128)S(1)}, u32[]{:S(2)}, u32[]{:S(2)}) collective-permute-start(f32[6,2,16,256]{3,2,1,0:T(8,128)S(1)} %copy.151), channel_id=1, source_target_pairs={{16,0},{32,16},{48,32},{64,48},{80,64},{96,80},{112,96},{0,112},{1... | collective-permute-start | bytes 589832 | tf_op jit(solution)/shard_map/ppermute | solution.py:49
  105.5 5.1 %copy-start.1 = (bf16[16,6,8,512]{3,1,2,0:T(8,128)(2,1)S(1)}, bf16[16,6,8,512]{3,1,2,0:T(8,128)(2,1)}, u32[]{:S(2)}) copy-start(bf16[16,6,8,512]{3,1,2,0:T(8,128)(2,1)} %copy-done) | copy-start | bytes 2359300
  105.7 8.4 %collective-permute-start.2 = (f32[6,20,2,256]{3,2,1,0:T(2,128)S(1)}, f32[6,20,2,256]{3,2,1,0:T(2,128)S(1)}, u32[]{:S(2)}, u32[]{:S(2)}) collective-permute-start(f32[6,20,2,256]{3,2,1,0:T(2,128)S(1)} %get-tuple-element.242), channel_id=1, source_target_pairs={{0,1},{1,2},{2,3},{3,4},{4,5},{5,6},{6,7},{7,8},{8,9},{9,10},{10,1... | collective-permute-start | bytes 737288 | tf_op jit(solution)/shard_map/ppermute | solution.py:48
  106.1 8.0 %collective-permute-start.3 = (f32[6,20,2,256]{3,2,1,0:T(2,128)S(1)}, f32[6,20,2,256]{3,2,1,0:T(2,128)S(1)}, u32[]{:S(2)}, u32[]{:S(2)}) collective-permute-start(f32[6,20,2,256]{3,2,1,0:T(2,128)S(1)} %get-tuple-element.243), channel_id=1, source_target_pairs={{1,0},{2,1},{3,2},{4,3},{5,4},{6,5},{7,6},{8,7},{9,8},{10,9},{11,1... | collective-permute-start | bytes 737288 | tf_op jit(solution)/shard_map/ppermute | solution.py:49
  128.3 17.2 %collective-permute-start.4 = (f32[6,1,16,256]{3,0,2,1:T(8,128)}, f32[6,1,16,256]{3,0,2,1:T(8,128)}, u32[]{:S(2)}, u32[]{:S(2)}) collective-permute-start(f32[6,1,16,256]{3,0,2,1:T(8,128)} %get-tuple-element.237), channel_id=1, source_target_pairs={{16,0},{32,16},{48,32},{64,48},{80,64},{96,80},{112,96},{0,112},{1... | collective-permute-start | bytes 294920 | tf_op jit(solution)/shard_map/ppermute | solution.py:63
  132.1 13.4 %collective-permute-start.5 = (f32[6,1,16,256]{3,0,2,1:T(8,128)}, f32[6,1,16,256]{3,0,2,1:T(8,128)}, u32[]{:S(2)}, u32[]{:S(2)}) collective-permute-start(f32[6,1,16,256]{3,0,2,1:T(8,128)} %get-tuple-element.236), channel_id=1, source_target_pairs={{0,16},{16,32},{32,48},{48,64},{64,80},{80,96},{96,112},{112,0},{1... | collective-permute-start | bytes 294920 | tf_op jit(solution)/shard_map/ppermute | solution.py:62
  132.1 13.4 %collective-permute-start.6 = (f32[6,16,1,256]{3,0,2,1:T(8,128)}, f32[6,16,1,256]{3,0,2,1:T(8,128)}, u32[]{:S(2)}, u32[]{:S(2)}) collective-permute-start(f32[6,16,1,256]{3,0,2,1:T(8,128)} %get-tuple-element.234), channel_id=1, source_target_pairs={{1,0},{2,1},{3,2},{4,3},{5,4},{6,5},{7,6},{8,7},{9,8},{10,9},{11,1... | collective-permute-start | bytes 294920 | tf_op jit(solution)/shard_map/ppermute | solution.py:63
  137.2 8.3 %collective-permute-start.7 = (f32[6,16,1,256]{3,0,2,1:T(8,128)}, f32[6,16,1,256]{3,0,2,1:T(8,128)}, u32[]{:S(2)}, u32[]{:S(2)}) collective-permute-start(f32[6,16,1,256]{3,0,2,1:T(8,128)} %get-tuple-element.235), channel_id=1, source_target_pairs={{0,1},{1,2},{2,3},{3,4},{4,5},{5,6},{6,7},{7,8},{8,9},{9,10},{10,1... | collective-permute-start | bytes 294920 | tf_op jit(solution)/shard_map/ppermute | solution.py:62
  169.6 28.1 %copy-start.2 = (f32[16,8,3,512]{3,1,0,2:T(8,128)S(1)}, f32[16,8,3,512]{3,1,0,2:T(8,128)}, u32[]{:S(2)}) copy-start(f32[16,8,3,512]{3,1,0,2:T(8,128)} %custom-call.1) | copy-start | bytes 2359300
where the time goes:
time: 315 us; the launch traced here: 312 us
  local copies, waits for them, and re-layouts  137 us (43%)
  matrix products  70.1 us (22%)
  starting transfers between devices  31 us (10%)
  waiting for transfers between devices  26.2 us (8%)
  blocking collectives  25.5 us (8%)
  other arithmetic  21.6 us (7%)
    dot_general x16, matrix products, pick_one_block(): jnp.einsum('bjzc,bpc->bjzp', g_b, table, precision=lax.Precision.HIGHEST)  39.7 us
    another operation x1, local copies, waits for them, and re-layouts, pick_forces(): grads.reshape(3 * SPECIES, plane, sources, band)  28.1 us
    dot_general x16, matrix products, deposit_one_block(): jnp.einsum('kbpz,bpc->bkzc', banded, table, preferred_element_type=jnp.fl...  27.5 us
    all_to_all x1, blocking collectives, exchange_both(): lax.all_to_all(blocks, axis, split_axis=0, concat_axis=0, tiled=True)  25.5 us
    all_to_all x2, waiting for transfers between devices, exchange_both(): lax.all_to_all(blocks, axis, split_axis=0, concat_axis=0, tiled=True)  24 us
    another operation x1, local copies, waits for them, and re-layouts, body(): jnp.stack((grad_x, grad_y, grad_z), axis=0).reshape(3, SPECIES, BX * BY, NZ)  18.7 us
    dynamic_slice x16, local copies, waits for them, and re-layouts, pick_forces(): lax.scan(pick_one_block, 0, (g_blocks, i_blocks, z_blocks, w_blocks))  16.1 us
    another operation x2, local copies, waits for them, and re-layouts, body(): density = density.reshape(SPECIES, BX, BY, NZ)  15.8 us
  transfers between devices with their start and end apart: 10, of which 3 were waited for; matrix products, arithmetic and copies ran while one was open for 8% of the time, Pallas kernels for 0%

commit v1 on v0

v1 whole, which is shorter than its diff:
```python
import functools

import jax
import jax.numpy as jnp
from jax import lax
from jax.experimental import pallas as pl
from jax.experimental.pallas import tpu as pltpu
from jax.sharding import PartitionSpec as P

SPECIES = 6
ROWS = 8
COLS = 16
HALVES = 16
LANES = 128
SLOTS = 512

raw_taps = (0.1353352832366127, 0.6065306597126334, 1.0)
tap_total = raw_taps[2] + 2.0 * (raw_taps[0] + raw_taps[1])
T2, T1, T0 = (t / tap_total for t in raw_taps)

f32 = jnp.float32
bf16 = jnp.bfloat16


def onehot_of(plane_row):
    ids = lax.broadcasted_iota(jnp.int32, (256, SLOTS), 0)
    return jnp.where(ids == plane_row, 1.0, 0.0).astype(bf16)


def deposit_kernel(counts, mix_matrix, cells, species, mix, own, low, high, mixed, w_s, v_s, d_s):
    r = pl.program_id(0)
    rows = lax.broadcasted_iota(jnp.int32, (COLS, LANES), 0)
    limit = jnp.zeros((COLS, LANES), jnp.int32)
    for i in range(COLS):
        limit = jnp.where(rows == i, counts[r * COLS + i], limit)
    lane = lax.broadcasted_iota(jnp.int32, (COLS, LANES), 1)
    zero = jnp.zeros((COLS, LANES), f32)
    for t in range(4):
        part = pl.ds(t * LANES, LANES)
        valid = (lane + t * LANES) < limit
        kind = species[:, part]
        upper = (cells[:, part] & 1) == 1
        ws = []
        for k in range(SPECIES):
            w = jnp.where(kind == k, 1.0, 0.0) + mix[k, :, part].astype(f32)
            w = jnp.where(valid, w, 0.0).astype(bf16).astype(f32)
            ws.append(w)
            w_s[t, k * COLS:(k + 1) * COLS] = jnp.where(upper, 0.0, w)
            w_s[t, (8 + k) * COLS:(9 + k) * COLS] = jnp.where(upper, w, 0.0)
        for k in (6, 7):
            w_s[t, k * COLS:(k + 1) * COLS] = zero
            w_s[t, (8 + k) * COLS:(9 + k) * COLS] = zero
            v_s[t, k * COLS:(k + 1) * COLS] = zero
        for l in range(SPECIES):
            v = mix_matrix[l, 0] * ws[0]
            for k in range(1, SPECIES):
                v = v + mix_matrix[l, k] * ws[k]
            v_s[t, l * COLS:(l + 1) * COLS] = v

    def one_brick(b, carry):
        table = onehot_of(cells[pl.ds(b, 1), :] >> 8)
        w = jnp.concatenate([w_s[t, pl.ds(b, 16, stride=COLS)] for t in range(4)], axis=1)
        dens = lax.dot_general(
            w.astype(bf16), table, (((1,), (1,)), ((), ())), preferred_element_type=f32
        )
        d_s[0, pl.ds(b, 16, stride=COLS)] = dens[:, :LANES]
        d_s[1, pl.ds(b, 16, stride=COLS)] = dens[:, LANES:]
        for t in range(4):
            mixed[b, :, t * LANES:(t + 1) * LANES] = v_s[t, pl.ds(b, 8, stride=COLS)]
        return carry

    lax.fori_loop(0, COLS, one_brick, 0, unroll=2)
    for z in range(2):
        for k in range(SPECIES):
            for h in range(2):
                value = d_s[h, (z * 8 + k) * COLS:(z * 8 + k + 1) * COLS]
                own[z, k, h] = value
                (low, high)[z][k, h] = value.astype(bf16)


def deposit(counts, mix_matrix, cells, species, mix):
    plane = (SPECIES, HALVES, COLS, LANES)
    return pl.pallas_call(
        deposit_kernel,
        name="deposit",
        grid_spec=pltpu.PrefetchScalarGridSpec(
            num_scalar_prefetch=2,
            grid=(ROWS,),
            in_specs=[
                pl.BlockSpec((COLS, SLOTS), lambda r, *_: (r, 0)),
                pl.BlockSpec((COLS, SLOTS), lambda r, *_: (r, 0)),
                pl.BlockSpec((SPECIES, COLS, SLOTS), lambda r, *_: (0, r, 0)),
            ],
            out_specs=[
                pl.BlockSpec((2, SPECIES, 2, COLS, LANES), lambda r, *_: (0, 0, r, 0, 0)),
                pl.BlockSpec((SPECIES, 2, COLS, LANES), lambda r, *_: (0, r, 0, 0)),
                pl.BlockSpec((SPECIES, 2, COLS, LANES), lambda r, *_: (0, r, 0, 0)),
                pl.BlockSpec((COLS, 8, SLOTS), lambda r, *_: (r, 0, 0)),
            ],
            scratch_shapes=[
                pltpu.VMEM((4, 16 * COLS, LANES), f32),
                pltpu.VMEM((4, 8 * COLS, LANES), f32),
                pltpu.VMEM((2, 16 * COLS, LANES), f32),
            ],
        ),
        out_shape=[
            jax.ShapeDtypeStruct((2,) + plane, f32),
            jax.ShapeDtypeStruct(plane, bf16),
            jax.ShapeDtypeStruct(plane, bf16),
            jax.ShapeDtypeStruct((ROWS * COLS, 8, SLOTS), f32),
        ],
        compiler_params=pltpu.CompilerParams(dimension_semantics=("arbitrary",)),
    )(counts, mix_matrix, cells, species, mix)


def shift_y(v, step, col):
    a = pltpu.roll(v, (-step) % LANES, 1)
    if step > 0:
        b = pltpu.roll(pltpu.roll(v, COLS - 1, 0), 16 - step, 1)
        return jnp.where(col < 16 - step, a, b)
    b = pltpu.roll(pltpu.roll(v, 1, 0), (-16 - step) % LANES, 1)
    return jnp.where(col >= -step, a, b)


def shift_x(here, beyond, step, lane):
    amount = (-16 * step) % LANES
    a = pltpu.roll(here, amount, 1)
    b = pltpu.roll(beyond, amount, 1)
    if step > 0:
        return jnp.where(lane < LANES - 16 * step, a, b)
    return jnp.where(lane >= -16 * step, a, b)


def force_kernel(cells, own, far_low, near_low0, near_low1, near_high0, near_high1, far_high, mixed,
                 forces, y_s, s_s, g_s):
    lane = lax.broadcasted_iota(jnp.int32, (COLS, LANES), 1)
    col = lane & 15

    def one_species(k, carry):
        def along_zy(h, c):
            l2 = far_low[k, h].astype(f32)
            a = near_low0[k, h].astype(f32)
            b = near_low1[k, h].astype(f32)
            o0 = own[0, k, h]
            o1 = own[1, k, h]
            r0 = near_high0[k, h].astype(f32)
            r1 = near_high1[k, h].astype(f32)
            r2 = far_high[k, h].astype(f32)
            um = T2 * (l2 + o1) + T1 * (a + o0) + T0 * b
            u0 = T2 * (a + r0) + T1 * (b + o1) + T0 * o0
            u1 = T2 * (b + r1) + T1 * (o0 + r0) + T0 * o1
            up = T2 * (o0 + r2) + T1 * (o1 + r1) + T0 * r0
            for i, v in enumerate((u0, u1, 0.5 * (u1 - um), 0.5 * (up - u0))):
                y_s[i, h] = (
                    T2 * (shift_y(v, -2, col) + shift_y(v, 2, col))
                    + T1 * (shift_y(v, -1, col) + shift_y(v, 1, col))
                    + T0 * v
                )
            return c

        lax.fori_loop(0, HALVES, along_zy, 0)

        def along_x(h, c):
            before = lax.rem(h + HALVES - 1, HALVES)
            after = lax.rem(h + 1, HALVES)
            for i in range(4):
                m, v, n = y_s[i, before], y_s[i, h], y_s[i, after]
                out = (
                    T2 * (shift_x(v, m, -2, lane) + shift_x(v, n, 2, lane))
                    + T1 * (shift_x(v, m, -1, lane) + shift_x(v, n, 1, lane))
                    + T0 * v
                )
                if i < 2:
                    s_s[i, h] = out
                    gy = 0.5 * (shift_y(out, 1, col) - shift_y(out, -1, col))
                    g_s[h, pl.ds(pl.multiple_of(((2 + i) * 8 + k) * COLS, COLS), COLS)] = gy
                else:
                    g_s[h, pl.ds(pl.multiple_of(((2 + i) * 8 + k) * COLS, COLS), COLS)] = out
            return c

        lax.fori_loop(0, HALVES, along_x, 0)

        def slope_x(h, c):
            before = lax.rem(h + HALVES - 1, HALVES)
            after = lax.rem(h + 1, HALVES)
            for i in range(2):
                m, v, n = s_s[i, before], s_s[i, h], s_s[i, after]
                gx = 0.5 * (shift_x(v, n, 1, lane) - shift_x(v, m, -1, lane))
                g_s[h, pl.ds(pl.multiple_of((i * 8 + k) * COLS, COLS), COLS)] = gx
            return c

        lax.fori_loop(0, HALVES, slope_x, 0)
        return carry

    lax.fori_loop(0, SPECIES, one_species, 0)
    zero = jnp.zeros((COLS, LANES), f32)
    for h in range(HALVES):
        for j in range(6):
            for k in (6, 7):
                g_s[h, (j * 8 + k) * COLS:(j * 8 + k + 1) * COLS] = zero

    def one_brick(d, carry):
        r = lax.div(d, COLS)
        q = lax.rem(d, COLS)
        row = cells[pl.ds(d, 1), :]
        table = onehot_of(row >> 8)
        g = jnp.concatenate(
            [g_s[2 * r + h, pl.ds(q, 48, stride=COLS)] for h in range(2)], axis=1
        )
        top = g.astype(bf16)
        rest = (g - top.astype(f32)).astype(bf16)
        got = jnp.dot(jnp.concatenate([top, rest], axis=0), table, preferred_element_type=f32)
        got = got[:48] + got[48:]
        upper = (row & 1) == 1
        v = mixed[d]
        for a in range(3):
            value = jnp.where(upper, got[(2 * a + 1) * 8:(2 * a + 2) * 8], got[2 * a * 8:(2 * a + 1) * 8])
            forces[a, pl.ds(d, 1), :] = jnp.sum(value * v, axis=0, keepdims=True)
        return carry

    lax.fori_loop(0, ROWS * COLS, one_brick, 0, unroll=2)


def pick(*args):
    return pl.pallas_call(
        force_kernel,
        name="force",
        out_shape=jax.ShapeDtypeStruct((3, ROWS * COLS, SLOTS), f32),
        in_specs=[pl.BlockSpec(memory_space=pltpu.VMEM)] * len(args),
        out_specs=pl.BlockSpec(memory_space=pltpu.VMEM),
        scratch_shapes=[
            pltpu.VMEM((4, HALVES, COLS, LANES), f32),
            pltpu.VMEM((2, HALVES, COLS, LANES), f32),
            pltpu.VMEM((HALVES, 48 * COLS, LANES), f32),
        ],
    )(*args)


def body(send_cells, send_species, send_mix, send_counts, chi):
    axes = ("row", "col")
    count = lax.axis_size("row") * lax.axis_size("col")
    up = [(i, (i + 1) % count) for i in range(count)]
    down = [(j, i) for i, j in up]
    chis = 0.5 * (chi + chi.T) * (1.0 - jnp.eye(SPECIES, dtype=f32))
    mix_matrix = -0.5 * (chis + 1.0)
    cells = send_cells[0]
    own, low, high, mixed = deposit(send_counts[0], mix_matrix, cells, send_species[0], send_mix[0])
    near_low1 = lax.ppermute(high, axes, up)
    near_high0 = lax.ppermute(low, axes, down)
    near_low0 = lax.ppermute(low, axes, up)
    near_high1 = lax.ppermute(high, axes, down)
    far_low = lax.ppermute(near_low1, axes, up)
    far_high = lax.ppermute(near_high0, axes, down)
    forces = pick(cells, own, far_low, near_low0, near_low1, near_high0, near_high1, far_high, mixed)
    return forces[None]


def solution(mesh):
    return jax.shard_map(
        body,
        mesh=mesh,
        in_specs=(
            P(("row", "col"), None, None),
            P(("row", "col"), None, None),
            P(("row", "col"), None, None, None),
            P(("row", "col"), None),
            P(),
        ),
        out_specs=P(("row", "col"), None, None, None),
        check_vma=False,
    )
```

time: 315 us -> 121 us (0.38)
  local copies, waits for them, and re-layouts: 137 us -> 1.52 us
  Pallas kernels: 0 us -> 82 us
  matrix products: 70.1 us -> 0 us
  blocking collectives: 25.5 us -> 0 us
  other arithmetic: 21.6 us -> 1.28 us
  starting transfers between devices: 31 us -> 19.5 us
  waiting for transfers between devices: 26.2 us -> 16.2 us
    pallas_call x0 -> x2, Pallas kernels: none -> 82 us  [the longest x1 60 us: pick(): pl.pallas_call(force_kernel, name='force', out_shape=jax.ShapeDtypeStruct...]
    dot_general x33 -> x0, matrix products: 70.1 us -> none  [the longest x16 39.7 us: pick_one_block(): jnp.einsum('bjzc,bpc->bjzp', g_b, table, precision=lax.Precision.HIGHEST)]
    another operation x6 -> x0, local copies, waits for them, and re-layouts: 65.3 us -> none  [the longest x1 28.1 us: pick_forces(): grads.reshape(3 * SPECIES, plane, sources, band)]
    all_to_all x1 -> x0, blocking collectives: 25.5 us -> none  [exchange_both(): lax.all_to_all(blocks, axis, split_axis=0, concat_axis=0, tiled=True)]
    all_to_all x2 -> x0, waiting for transfers between devices: 24 us -> none  [exchange_both(): lax.all_to_all(blocks, axis, split_axis=0, concat_axis=0, tiled=True)]
    dynamic_slice x16 -> x0, local copies, waits for them, and re-layouts: 16.1 us -> none  [pick_forces(): lax.scan(pick_one_block, 0, (g_blocks, i_blocks, z_blocks, w_blocks))]
    all_to_all x2 -> x0, starting transfers between devices: 15.8 us -> none  [exchange_both(): lax.all_to_all(blocks, axis, split_axis=0, concat_axis=0, tiled=True)]
    slice x12 -> x0, local copies, waits for them, and re-layouts: 15.1 us -> none  [the longest x2 7.51 us: extended_2(): last = lax.slice_in_dim(value, length - width, length, axis=dim)]
  transfers between devices with their start and end apart: 10 -> 6, of which waited for: 3 -> 4; matrix products, arithmetic and copies ran while one was open for 8% -> 0% of each run, Pallas kernels for 0% -> 0%
where the time goes in v1:
time: 121 us
  Pallas kernels  82 us (68%)
  starting transfers between devices  19.5 us (16%)
  waiting for transfers between devices  16.2 us (13%)
  local copies, waits for them, and re-layouts  1.52 us (1%)
  other arithmetic  1.28 us (1%)
    pallas_call x1, Pallas kernels, pick(): pl.pallas_call(force_kernel, name='force', out_shape=jax.ShapeDtypeStruct...  60 us
    pallas_call x1, Pallas kernels, deposit(): pl.pallas_call(deposit_kernel, name='deposit', grid_spec=pltpu.PrefetchSc...  22.1 us
    ppermute x1, starting transfers between devices, body(): far_high = lax.ppermute(near_high0, axes, down)  9.86 us
    ppermute x1, waiting for transfers between devices, body(): near_low1 = lax.ppermute(high, axes, up)  7.85 us
    ppermute x1, starting transfers between devices, body(): near_high0 = lax.ppermute(low, axes, down)  5.54 us
    ppermute x1, waiting for transfers between devices, body(): near_high0 = lax.ppermute(low, axes, down)  3.69 us
    ppermute x1, waiting for transfers between devices, body(): far_low = lax.ppermute(near_low1, axes, up)  3.27 us
  transfers between devices with their start and end apart: 6, of which 4 were waited for; matrix products, arithmetic and copies ran while one was open for 0% of the time, Pallas kernels for 0%

profile of v1, /device:TPU:1, one launch (start us, length us, event | category | flops | bytes accessed | tf_op | source)
XLA Modules:
  0.0 120.6 jit_solution(2431542751471392770)
XLA Ops:
  0.0 0.8 copy.6
  0.8 1.3 %fusion.3.mix_matrix = f32[6,6]{1,0:T(8,128)} fusion(f32[6,6]{1,0:T(8,128)} %param.9, f32[6,6]{0,1:T(8,128)S(1)} %copy.6), kind=kLoop, calls=%fused_computation.4 | loop fusion | flops 288 | bytes 432 | tf_op jit(solution)/shard_map/mul | solution.py:245
  2.0 22.1 %deposit.1 = (f32[2,6,16,16,128]{4,3,2,1,0:T(8,128)}, bf16[6,16,16,128]{3,2,1,0:T(8,128)(2,1)}, bf16[6,16,16,128]{3,2,1,0:T(8,128)(2,1)}, f32[128,8,512]{2,1,0:T(8,128)}) custom-call(s32[128]{0:T(128)} %bitcast.19, f32[6,6]{1,0:T(8,128)} %fusion.3.mix_matrix, s32[128,512]{1,0:T(8,128)} %bitcast.15, s32[128,512]{1,0:T(8,128)} %bitcast.18, ...), custom_call_target="tpu_custom_call" | custom-call | tf_op jit(solution)/shard_map/deposit/pallas_call | solution.py:83
  24.1 2.1 %collective-permute-start = (bf16[6,16,16,128]{3,2,1,0:T(8,128)(2,1)}, bf16[6,16,16,128]{3,2,1,0:T(8,128)(2,1)S(1)}, u32[]{:S(2)}, u32[]{:S(2)}) collective-permute-start(bf16[6,16,16,128]{3,2,1,0:T(8,128)(2,1)} %get-tuple-element.10), channel_id=1, source_target_pairs={{0,1},{1,2},{2,3},{3,4},{4,5},{5,6},{6,7},{7,8},{8,9},{9,10},{10,1... | collective-permute-start | bytes 1179656 | tf_op jit(solution)/shard_map/ppermute | solution.py:248
  26.2 5.5 %collective-permute-start.3 = (bf16[6,16,16,128]{3,2,1,0:T(8,128)(2,1)}, bf16[6,16,16,128]{3,2,1,0:T(8,128)(2,1)S(1)}, u32[]{:S(2)}, u32[]{:S(2)}) collective-permute-start(bf16[6,16,16,128]{3,2,1,0:T(8,128)(2,1)} %get-tuple-element.11), channel_id=1, source_target_pairs={{1,0},{2,1},{3,2},{4,3},{5,4},{6,5},{7,6},{8,7},{9,8},{10,9},{11,1... | collective-permute-start | bytes 1179656 | tf_op jit(solution)/shard_map/ppermute | solution.py:249
  31.8 2.0 %collective-permute-start.4 = (bf16[6,16,16,128]{3,2,1,0:T(8,128)(2,1)}, bf16[6,16,16,128]{3,2,1,0:T(8,128)(2,1)S(1)}, u32[]{:S(2)}, u32[]{:S(2)}) collective-permute-start(bf16[6,16,16,128]{3,2,1,0:T(8,128)(2,1)} %get-tuple-element.10), channel_id=1, source_target_pairs={{1,0},{2,1},{3,2},{4,3},{5,4},{6,5},{7,6},{8,7},{9,8},{10,9},{11,1... | collective-permute-start | bytes 1179656 | tf_op jit(solution)/shard_map/ppermute | solution.py:251
  33.7 0.0 collective-permute-start.2
  33.7 7.9 %collective-permute-done.near_low1 = bf16[6,16,16,128]{3,2,1,0:T(8,128)(2,1)S(1)} collective-permute-done((bf16[6,16,16,128]{3,2,1,0:T(8,128)(2,1)}, bf16[6,16,16,128]{3,2,1,0:T(8,128)(2,1)S(1)}, u32[]{:S(2)}, u32[]{:S(2)}) %collective-permute-start) | collective-permute-done | bytes 393248 | tf_op jit(solution)/shard_map/ppermute | solution.py:248
  41.6 0.0 copy-start
  41.6 0.0 collective-permute-start.1
  41.6 3.7 %collective-permute-done.3.near_high0 = bf16[6,16,16,128]{3,2,1,0:T(8,128)(2,1)S(1)} collective-permute-done((bf16[6,16,16,128]{3,2,1,0:T(8,128)(2,1)}, bf16[6,16,16,128]{3,2,1,0:T(8,128)(2,1)S(1)}, u32[]{:S(2)}, u32[]{:S(2)}) %collective-permute-start.3) | collective-permute-done | bytes 393248 | tf_op jit(solution)/shard_map/ppermute | solution.py:249
  45.3 0.0 copy-start.1
  45.3 9.9 %collective-permute-start.5 = (bf16[6,16,16,128]{3,2,1,0:T(8,128)(2,1)S(1)}, bf16[6,16,16,128]{3,2,1,0:T(8,128)(2,1)S(1)}, u32[]{:S(2)}, u32[]{:S(2)}) collective-permute-start(bf16[6,16,16,128]{3,2,1,0:T(8,128)(2,1)S(1)} %collective-permute-done.3.near_high0), channel_id=1, source_target_pairs={{1,0},{2,1},{3,2},{4,3},{5,4},{6,5},{7,6},{8,7},{9,8},{10,9},{11,1... | collective-permute-start | bytes 1179656 | tf_op jit(solution)/shard_map/ppermute | solution.py:253
  55.1 0.0 collective-permute-done.4.near_high1
  55.1 0.0 copy-start.2
  55.1 0.0 collective-permute-done.2.near_low0
  55.2 0.0 copy-start.3
  55.2 3.3 %collective-permute-done.1.far_low = bf16[6,16,16,128]{3,2,1,0:T(8,128)(2,1)S(1)} collective-permute-done((bf16[6,16,16,128]{3,2,1,0:T(8,128)(2,1)S(1)}, bf16[6,16,16,128]{3,2,1,0:T(8,128)(2,1)S(1)}, u32[]{:S(2)}, u32[]{:S(2)}) %collective-permute-start.1) | collective-permute-done | bytes 393248 | tf_op jit(solution)/shard_map/ppermute | solution.py:252
  58.4 0.0 copy-start.4
  58.4 1.4 %collective-permute-done.5.far_high = bf16[6,16,16,128]{3,2,1,0:T(8,128)(2,1)S(1)} collective-permute-done((bf16[6,16,16,128]{3,2,1,0:T(8,128)(2,1)S(1)}, bf16[6,16,16,128]{3,2,1,0:T(8,128)(2,1)S(1)}, u32[]{:S(2)}, u32[]{:S(2)}) %collective-permute-start.5) | collective-permute-done | bytes 393248 | tf_op jit(solution)/shard_map/ppermute | solution.py:253
  59.9 0.0 copy-start.5
  59.9 0.0 copy-done
  59.9 0.0 copy-done.1
  59.9 0.0 copy-done.2
  59.9 0.0 copy-done.3
  59.9 0.0 copy-done.4
  59.9 0.7 copy-done.5
  60.6 60.0 %force.1 = f32[3,128,512]{2,1,0:T(8,128)} custom-call(s32[128,512]{1,0:T(8,128)} %bitcast.16, f32[2,6,16,16,128]{4,3,2,1,0:T(8,128)} %get-tuple-element.9.own, bf16[6,16,16,128]{3,2,1,0:T(8,128)(2,1)} %copy-done.4, bf16[6,16,16,128]{3,2,1,0:T(8,128)(2,1)} %copy-done.3, bf16[6,16,16,128]{3,2,1,0:T(8,128)(2,1)} %copy-done, bf16[6,16,16,128]{3,2,1,0:T(8,128)(2,1)} %copy-done.1, ...), custom_call_target="tpu_custom_call" | custom-call | tf_op jit(solution)/shard_map/force/pallas_call | solution.py:225
Async XLA Ops:
  24.1 17.5 %collective-permute-start = (bf16[6,16,16,128]{3,2,1,0:T(8,128)(2,1)}, bf16[6,16,16,128]{3,2,1,0:T(8,128)(2,1)S(1)}, u32[]{:S(2)}, u32[]{:S(2)}) collective-permute-start(bf16[6,16,16,128]{3,2,1,0:T(8,128)(2,1)} %get-tuple-element.10), channel_id=1, source_target_pairs={{0,1},{1,2},{2,3},{3,4},{4,5},{5,6},{6,7},{7,8},{8,9},{9,10},{10,1... | collective-permute-start | bytes 1179656 | tf_op jit(solution)/shard_map/ppermute | solution.py:248
  26.2 19.1 %collective-permute-start.3 = (bf16[6,16,16,128]{3,2,1,0:T(8,128)(2,1)}, bf16[6,16,16,128]{3,2,1,0:T(8,128)(2,1)S(1)}, u32[]{:S(2)}, u32[]{:S(2)}) collective-permute-start(bf16[6,16,16,128]{3,2,1,0:T(8,128)(2,1)} %get-tuple-element.11), channel_id=1, source_target_pairs={{1,0},{2,1},{3,2},{4,3},{5,4},{6,5},{7,6},{8,7},{9,8},{10,9},{11,1... | collective-permute-start | bytes 1179656 | tf_op jit(solution)/shard_map/ppermute | solution.py:249
  31.8 23.4 %collective-permute-start.4 = (bf16[6,16,16,128]{3,2,1,0:T(8,128)(2,1)}, bf16[6,16,16,128]{3,2,1,0:T(8,128)(2,1)S(1)}, u32[]{:S(2)}, u32[]{:S(2)}) collective-permute-start(bf16[6,16,16,128]{3,2,1,0:T(8,128)(2,1)} %get-tuple-element.10), channel_id=1, source_target_pairs={{1,0},{2,1},{3,2},{4,3},{5,4},{6,5},{7,6},{8,7},{9,8},{10,9},{11,1... | collective-permute-start | bytes 1179656 | tf_op jit(solution)/shard_map/ppermute | solution.py:251
  33.7 21.4 %collective-permute-start.2 = (bf16[6,16,16,128]{3,2,1,0:T(8,128)(2,1)}, bf16[6,16,16,128]{3,2,1,0:T(8,128)(2,1)S(1)}, u32[]{:S(2)}, u32[]{:S(2)}) collective-permute-start(bf16[6,16,16,128]{3,2,1,0:T(8,128)(2,1)} %get-tuple-element.11), channel_id=1, source_target_pairs={{0,1},{1,2},{2,3},{3,4},{4,5},{5,6},{6,7},{7,8},{8,9},{9,10},{10,1... | collective-permute-start | bytes 1179656 | tf_op jit(solution)/shard_map/ppermute | solution.py:250
  41.6 18.3 %copy-start = (bf16[6,16,16,128]{3,2,1,0:T(8,128)(2,1)}, bf16[6,16,16,128]{3,2,1,0:T(8,128)(2,1)S(1)}, u32[]{:S(2)}) copy-start(bf16[6,16,16,128]{3,2,1,0:T(8,128)(2,1)S(1)} %collective-permute-done.near_low1) | copy-start | bytes 1179652
  41.6 16.9 %collective-permute-start.1 = (bf16[6,16,16,128]{3,2,1,0:T(8,128)(2,1)S(1)}, bf16[6,16,16,128]{3,2,1,0:T(8,128)(2,1)S(1)}, u32[]{:S(2)}, u32[]{:S(2)}) collective-permute-start(bf16[6,16,16,128]{3,2,1,0:T(8,128)(2,1)S(1)} %collective-permute-done.near_low1), channel_id=1, source_target_pairs={{0,1},{1,2},{2,3},{3,4},{4,5},{5,6},{6,7},{7,8},{8,9},{9,10},{10,1... | collective-permute-start | bytes 1179656 | tf_op jit(solution)/shard_map/ppermute | solution.py:252
  45.3 14.6 %copy-start.1 = (bf16[6,16,16,128]{3,2,1,0:T(8,128)(2,1)}, bf16[6,16,16,128]{3,2,1,0:T(8,128)(2,1)S(1)}, u32[]{:S(2)}) copy-start(bf16[6,16,16,128]{3,2,1,0:T(8,128)(2,1)S(1)} %collective-permute-done.3.near_high0) | copy-start | bytes 1179652
  45.3 14.6 %collective-permute-start.5 = (bf16[6,16,16,128]{3,2,1,0:T(8,128)(2,1)S(1)}, bf16[6,16,16,128]{3,2,1,0:T(8,128)(2,1)S(1)}, u32[]{:S(2)}, u32[]{:S(2)}) collective-permute-start(bf16[6,16,16,128]{3,2,1,0:T(8,128)(2,1)S(1)} %collective-permute-done.3.near_high0), channel_id=1, source_target_pairs={{1,0},{2,1},{3,2},{4,3},{5,4},{6,5},{7,6},{8,7},{9,8},{10,9},{11,1... | collective-permute-start | bytes 1179656 | tf_op jit(solution)/shard_map/ppermute | solution.py:253
  55.1 4.7 %copy-start.2 = (bf16[6,16,16,128]{3,2,1,0:T(8,128)(2,1)}, bf16[6,16,16,128]{3,2,1,0:T(8,128)(2,1)S(1)}, u32[]{:S(2)}) copy-start(bf16[6,16,16,128]{3,2,1,0:T(8,128)(2,1)S(1)} %collective-permute-done.4.near_high1) | copy-start | bytes 1179652
  55.2 4.7 %copy-start.3 = (bf16[6,16,16,128]{3,2,1,0:T(8,128)(2,1)}, bf16[6,16,16,128]{3,2,1,0:T(8,128)(2,1)S(1)}, u32[]{:S(2)}) copy-start(bf16[6,16,16,128]{3,2,1,0:T(8,128)(2,1)S(1)} %collective-permute-done.2.near_low0) | copy-start | bytes 1179652
  58.4 1.5 %copy-start.4 = (bf16[6,16,16,128]{3,2,1,0:T(8,128)(2,1)}, bf16[6,16,16,128]{3,2,1,0:T(8,128)(2,1)S(1)}, u32[]{:S(2)}) copy-start(bf16[6,16,16,128]{3,2,1,0:T(8,128)(2,1)S(1)} %collective-permute-done.1.far_low) | copy-start | bytes 1179652
  59.9 0.8 copy-start.5

commit v2 on v1

v2 whole, which is shorter than its diff:
```python
import jax
import jax.numpy as jnp
import numpy as np
from jax import lax
from jax.experimental import pallas as pl
from jax.experimental.pallas import tpu as pltpu
from jax.sharding import PartitionSpec as P

SPECIES = 6
ROWS = 8
COLS = 16
HALVES = 16
LANES = 128
SLOTS = 512

raw_taps = (0.1353352832366127, 0.6065306597126334, 1.0)
tap_total = raw_taps[2] + 2.0 * (raw_taps[0] + raw_taps[1])
T2, T1, T0 = (t / tap_total for t in raw_taps)

f32 = jnp.float32
bf16 = jnp.bfloat16


def onehot_of(plane_row):
    ids = lax.broadcasted_iota(jnp.int32, (16, SLOTS), 0)
    inner = jnp.where((plane_row & 15) == ids, 1.0, 0.0).astype(bf16)
    outer = (plane_row >> 4).astype(f32).astype(bf16)
    none = jnp.zeros((16, SLOTS), bf16)
    return jnp.concatenate(
        [jnp.where(outer == jnp.full((16, SLOTS), i, bf16), inner, none) for i in range(16)], axis=0
    )


def weights_of(limit, t, cells, species, mix):
    part = pl.ds(t * LANES, LANES)
    lane = lax.broadcasted_iota(jnp.int32, (COLS, LANES), 1)
    valid = (lane + t * LANES) < limit
    kind = species[:, part]
    found = []
    for k in range(SPECIES):
        w = jnp.where(kind == k, 1.0, 0.0) + mix[k, :, part].astype(f32)
        found.append(jnp.where(valid, w, 0.0).astype(bf16).astype(f32))
    return found


def limits_of(counts, first):
    rows = lax.broadcasted_iota(jnp.int32, (COLS, LANES), 0)
    limit = jnp.zeros((COLS, LANES), jnp.int32)
    for i in range(COLS):
        limit = jnp.where(rows == i, counts[first + i], limit)
    return limit


def deposit_kernel(counts, cells, species, mix, own, low, high, w_s, d_s):
    r = pl.program_id(0)
    limit = limits_of(counts, r * COLS)
    zero = jnp.zeros((COLS, LANES), f32)
    for t in range(4):
        upper = (cells[:, pl.ds(t * LANES, LANES)] & 1) == 1
        for k, w in enumerate(weights_of(limit, t, cells, species, mix)):
            w_s[t, k * COLS:(k + 1) * COLS] = jnp.where(upper, 0.0, w)
            w_s[t, (8 + k) * COLS:(9 + k) * COLS] = jnp.where(upper, w, 0.0)
        for k in (6, 7):
            w_s[t, k * COLS:(k + 1) * COLS] = zero
            w_s[t, (8 + k) * COLS:(9 + k) * COLS] = zero

    for b in range(COLS):
        table = onehot_of(jnp.broadcast_to(cells[b:b + 1, :] >> 8, (16, SLOTS)))
        w = jnp.concatenate([w_s[t, pl.ds(b, 16, stride=COLS)] for t in range(4)], axis=1)
        dens = lax.dot_general(
            w.astype(bf16), table, (((1,), (1,)), ((), ())), preferred_element_type=f32
        )
        d_s[0, pl.ds(b, 16, stride=COLS)] = dens[:, :LANES]
        d_s[1, pl.ds(b, 16, stride=COLS)] = dens[:, LANES:]

    for z in range(2):
        for k in range(SPECIES):
            for h in range(2):
                value = d_s[h, (z * 8 + k) * COLS:(z * 8 + k + 1) * COLS]
                own[z, k, h] = value
                (low, high)[z][k, h] = value.astype(bf16)


def deposit(counts, cells, species, mix):
    plane = (SPECIES, HALVES, COLS, LANES)
    return pl.pallas_call(
        deposit_kernel,
        name="deposit",
        grid_spec=pltpu.PrefetchScalarGridSpec(
            num_scalar_prefetch=1,
            grid=(ROWS,),
            in_specs=[
                pl.BlockSpec((COLS, SLOTS), lambda r, *_: (r, 0)),
                pl.BlockSpec((COLS, SLOTS), lambda r, *_: (r, 0)),
                pl.BlockSpec((SPECIES, COLS, SLOTS), lambda r, *_: (0, r, 0)),
            ],
            out_specs=[
                pl.BlockSpec((2, SPECIES, 2, COLS, LANES), lambda r, *_: (0, 0, r, 0, 0)),
                pl.BlockSpec((SPECIES, 2, COLS, LANES), lambda r, *_: (0, r, 0, 0)),
                pl.BlockSpec((SPECIES, 2, COLS, LANES), lambda r, *_: (0, r, 0, 0)),
            ],
            scratch_shapes=[
                pltpu.VMEM((4, 16 * COLS, LANES), f32),
                pltpu.VMEM((2, 16 * COLS, LANES), f32),
            ],
        ),
        out_shape=[
            jax.ShapeDtypeStruct((2,) + plane, f32),
            jax.ShapeDtypeStruct(plane, bf16),
            jax.ShapeDtypeStruct(plane, bf16),
        ],
        cost_estimate=pl.CostEstimate(flops=4 * 10**9, bytes_accessed=5 * 10**6, transcendentals=0),
    )(counts, cells, species, mix)


def mixing_kernel(counts, mix_matrix, cells, species, mix, mixed, v_s):
    r = pl.program_id(0)
    limit = limits_of(counts, r * COLS)
    zero = jnp.zeros((COLS, LANES), f32)
    for t in range(4):
        ws = weights_of(limit, t, cells, species, mix)
        for l in range(SPECIES):
            v = mix_matrix[l, 0] * ws[0]
            for k in range(1, SPECIES):
                v = v + mix_matrix[l, k] * ws[k]
            v_s[t, l * COLS:(l + 1) * COLS] = v
        for k in (6, 7):
            v_s[t, k * COLS:(k + 1) * COLS] = zero
    for b in range(COLS):
        for t in range(4):
            mixed[b, :, t * LANES:(t + 1) * LANES] = v_s[t, pl.ds(b, 8, stride=COLS)]


def mixing(counts, mix_matrix, cells, species, mix):
    return pl.pallas_call(
        mixing_kernel,
        name="mixing",
        grid_spec=pltpu.PrefetchScalarGridSpec(
            num_scalar_prefetch=2,
            grid=(ROWS,),
            in_specs=[
                pl.BlockSpec((COLS, SLOTS), lambda r, *_: (r, 0)),
                pl.BlockSpec((COLS, SLOTS), lambda r, *_: (r, 0)),
                pl.BlockSpec((SPECIES, COLS, SLOTS), lambda r, *_: (0, r, 0)),
            ],
            out_specs=pl.BlockSpec((COLS, 8, SLOTS), lambda r, *_: (r, 0, 0)),
            scratch_shapes=[pltpu.VMEM((4, 8 * COLS, LANES), f32)],
        ),
        out_shape=jax.ShapeDtypeStruct((ROWS * COLS, 8, SLOTS), f32),
        cost_estimate=pl.CostEstimate(flops=10**9, bytes_accessed=4 * 10**6, transcendentals=0),
    )(counts, mix_matrix, cells, species, mix)


def scaled_taps():
    smooth_scale, slope_scale = 1.6396387, 1.5596421
    smooth_taps = {0: T0, 1: T1, -1: T1, 2: T2, -2: T2}
    slope_taps = {1: 0.5 * (T0 - T2), 2: 0.5 * T1, 3: 0.5 * T2}
    slope_taps.update({-j: -v for j, v in slope_taps.items()})
    return (
        {j: smooth_scale * v for j, v in smooth_taps.items()},
        {j: slope_scale * v for j, v in slope_taps.items()},
        smooth_scale,
        slope_scale,
    )


SMOOTH, SLOPE, SMOOTH_SCALE, SLOPE_SCALE = scaled_taps()


def tap_matrices():
    lane = np.arange(LANES)
    x, y = lane // 16, lane % 16
    results = []
    for main, other, extent in ((y, x, 16), (x, y, 8)):
        source = np.concatenate([main, np.where(main < extent // 2, main + extent, main - extent)])
        same = np.concatenate([other, other])[:, None] == other[None, :]
        gap = source[:, None] - main[None, :]
        for taps in (SMOOTH, SLOPE):
            matrix = np.zeros((2 * LANES, LANES), np.float32)
            for j, value in taps.items():
                matrix += np.where(same & (gap == j), np.float32(value), np.float32(0))
            results.append(matrix)
    return jnp.asarray(np.concatenate(results, axis=1)).astype(bf16)


def split(v):
    top = v.astype(bf16)
    return top, (v - top.astype(f32)).astype(bf16)


def force_kernel(cells, taps, own, far_low, near_low0, near_low1, near_high0, near_high1, far_high, mixed_far,
                 forces, x_s, y_s, w_s, g_s, mixed, sem):
    k = pl.program_id(0)
    lane = lax.broadcasted_iota(jnp.int32, (COLS, LANES), 1)
    col = lane & 15
    fetch = pltpu.make_async_copy(mixed_far, mixed, sem)

    @pl.when(k == 0)
    def _():
        fetch.start()
        zero = jnp.zeros((HALVES, COLS, LANES), f32)
        for j in range(6):
            for i in (6, 7):
                g_s[:, (j * 8 + i) * COLS:(j * 8 + i + 1) * COLS] = zero

    cu = 1.0 / (SMOOTH_SCALE * SLOPE_SCALE)
    cz = 0.5 / (SMOOTH_SCALE * SMOOTH_SCALE)
    for h in range(HALVES):
        l2 = far_low[0, h].astype(f32)
        a = near_low0[0, h].astype(f32)
        b = near_low1[0, h].astype(f32)
        o0 = own[0, 0, h]
        o1 = own[1, 0, h]
        r0 = near_high0[0, h].astype(f32)
        r1 = near_high1[0, h].astype(f32)
        r2 = far_high[0, h].astype(f32)
        um = T2 * (l2 + o1) + T1 * (a + o0) + T0 * b
        u0 = T2 * (a + r0) + T1 * (b + o1) + T0 * o0
        u1 = T2 * (b + r1) + T1 * (o0 + r0) + T0 * o1
        up = T2 * (o0 + r2) + T1 * (o1 + r1) + T0 * r0
        for i, v in enumerate((cu * u0, cu * u1, cz * (u1 - um), cz * (up - u0))):
            around = jnp.where(col < 8, pltpu.roll(v, COLS - 1, 0), pltpu.roll(v, 1, 0))
            for part, value in ((0, v), (1, around)):
                for level, piece in enumerate(split(value)):
                    x_s[level, i, h * COLS:(h + 1) * COLS, part * LANES:(part + 1) * LANES] = piece
    for i in range(4):
        width = 2 * LANES if i < 2 else LANES
        table = taps[:, :width]
        out = jnp.dot(x_s[0, i], table, preferred_element_type=f32) + jnp.dot(
            x_s[1, i], table, preferred_element_type=f32
        )
        if i < 2:
            y_s[i] = out[:, :LANES]
            y_s[2 + i] = out[:, LANES:]
        else:
            y_s[2 + i] = out
    for p in range(6):
        for h in range(HALVES):
            before = (h + HALVES - 1) % HALVES
            after = (h + 1) % HALVES
            v = y_s[p, h * COLS:(h + 1) * COLS]
            around = jnp.where(
                lane < 64,
                y_s[p, after * COLS:(after + 1) * COLS],
                y_s[p, before * COLS:(before + 1) * COLS],
            )
            for part, value in ((0, v), (1, around)):
                for level, piece in enumerate(split(value)):
                    w_s[level, p, h * COLS:(h + 1) * COLS, part * LANES:(part + 1) * LANES] = piece
        table = taps[:, 3 * LANES:] if p < 2 else taps[:, 2 * LANES:3 * LANES]
        out = jnp.dot(w_s[0, p], table, preferred_element_type=f32) + jnp.dot(
            w_s[1, p], table, preferred_element_type=f32
        )
        for h in range(HALVES):
            g_s[h, pl.ds(pl.multiple_of((p * 8 + k) * COLS, COLS), COLS)] = out[h * COLS:(h + 1) * COLS]

    def one_brick(d):
        r = lax.div(d, COLS)
        q = lax.rem(d, COLS)
        row = cells[pl.ds(d, 1), :]
        table = onehot_of(jnp.broadcast_to(row >> 8, (16, SLOTS)))
        g = jnp.concatenate(
            [g_s[2 * r + h, pl.ds(q, 48, stride=COLS)] for h in range(2)], axis=1
        )
        got = jnp.dot(jnp.concatenate(split(g), axis=0), table, preferred_element_type=f32)
        got = got[:48] + got[48:]
        upper = (row & 1) == 1
        v = mixed[d]
        for a in range(3):
            value = jnp.where(upper, got[(2 * a + 1) * 8:(2 * a + 2) * 8], got[2 * a * 8:(2 * a + 1) * 8])
            forces[a, pl.ds(d, 1), :] = jnp.sum(value * v, axis=0, keepdims=True)

    @pl.when(k == SPECIES - 1)
    def _():
        fetch.wait()

        def some_bricks(i, carry):
            for j in range(8):
                one_brick(i * 8 + j)
            return carry

        lax.fori_loop(0, ROWS * COLS // 8, some_bricks, 0)


def pick(cells, taps, own, *others):
    plane = pl.BlockSpec((1, HALVES, COLS, LANES), lambda k: (k, 0, 0, 0))
    return pl.pallas_call(
        force_kernel,
        name="force",
        grid=(SPECIES,),
        out_shape=jax.ShapeDtypeStruct((3, ROWS * COLS, SLOTS), f32),
        in_specs=[
            pl.BlockSpec((ROWS * COLS, SLOTS), lambda k: (0, 0)),
            pl.BlockSpec((2 * LANES, 4 * LANES), lambda k: (0, 0)),
            pl.BlockSpec((2, 1, HALVES, COLS, LANES), lambda k: (0, k, 0, 0, 0)),
        ]
        + [plane] * 6
        + [pl.BlockSpec(memory_space=pl.ANY)],
        out_specs=pl.BlockSpec((3, ROWS * COLS, SLOTS), lambda k: (0, 0, 0)),
        scratch_shapes=[
            pltpu.VMEM((2, 4, HALVES * COLS, 2 * LANES), bf16),
            pltpu.VMEM((6, HALVES * COLS, LANES), f32),
            pltpu.VMEM((2, 6, HALVES * COLS, 2 * LANES), bf16),
            pltpu.VMEM((HALVES, 48 * COLS, LANES), f32),
            pltpu.VMEM((ROWS * COLS, 8, SLOTS), f32),
            pltpu.SemaphoreType.DMA,
        ],
    )(cells, taps, own, *others)


def body(send_cells, send_species, send_mix, send_counts, chi):
    axes = ("row", "col")
    count = lax.axis_size("row") * lax.axis_size("col")
    up = [(i, (i + 1) % count) for i in range(count)]
    down = [(j, i) for i, j in up]
    chis = 0.5 * (chi + chi.T) * (1.0 - jnp.eye(SPECIES, dtype=f32))
    mix_matrix = -0.5 * (chis + 1.0)
    cells, species, mix, counts = send_cells[0], send_species[0], send_mix[0], send_counts[0]
    own, low, high = deposit(counts, cells, species, mix)
    near_low1 = lax.ppermute(high, axes, up)
    near_high0 = lax.ppermute(low, axes, down)
    near_low0 = lax.ppermute(low, axes, up)
    near_high1 = lax.ppermute(high, axes, down)
    far_low = lax.ppermute(near_low1, axes, up)
    far_high = lax.ppermute(near_high0, axes, down)
    mixed = mixing(counts, mix_matrix, cells, species, mix)
    forces = pick(
        cells, tap_matrices(), own, far_low, near_low0, near_low1, near_high0, near_high1, far_high, mixed
    )
    return forces[None]


def solution(mesh):
    return jax.shard_map(
        body,
        mesh=mesh,
        in_specs=(
            P(("row", "col"), None, None),
            P(("row", "col"), None, None),
            P(("row", "col"), None, None, None),
            P(("row", "col"), None),
            P(),
        ),
        out_specs=P(("row", "col"), None, None, None),
        check_vma=False,
    )
```

time: 121 us -> 72.7 us (0.60)
  Pallas kernels: 82 us -> 39.4 us
  waiting for transfers between devices: 16.2 us -> 11.6 us
    pallas_call x1 -> x2, Pallas kernels: 60 us -> 26.5 us  [the longest x1 19.5 us: pick(): pl.pallas_call(force_kernel, name='force', grid=(SPECIES,), out_shape=jax...]
    pallas_call x1, Pallas kernels: 22.1 us -> 12.8 us  [deposit(): pl.pallas_call(deposit_kernel, name='deposit', grid_spec=pltpu.PrefetchSc...]
    ppermute x1, waiting for transfers between devices: 3.27 us -> 0.01 us  [body(): far_low = lax.ppermute(near_low1, axes, up)]
    ppermute x1, waiting for transfers between devices: 1.43 us -> 0.01 us  [body(): far_high = lax.ppermute(near_high0, axes, down)]
  transfers between devices with their start and end apart: 6 -> 6, of which waited for: 4 -> 2; matrix products, arithmetic and copies ran while one was open for 0% -> 1% of each run, Pallas kernels for 0% -> 10%
where the time goes in v2:
time: 72.7 us; the launch traced here: 72.3 us
  Pallas kernels  39.4 us (54%)
  starting transfers between devices  19.5 us (27%)
  waiting for transfers between devices  11.6 us (16%)
  local copies, waits for them, and re-layouts  1.19 us (2%)
    pallas_call x1, Pallas kernels, pick(): pl.pallas_call(force_kernel, name='force', grid=(SPECIES,), out_shape=jax...  19.5 us
    pallas_call x1, Pallas kernels, deposit(): pl.pallas_call(deposit_kernel, name='deposit', grid_spec=pltpu.PrefetchSc...  12.8 us
    ppermute x1, starting transfers between devices, body(): far_high = lax.ppermute(near_high0, axes, down)  9.86 us
    ppermute x1, waiting for transfers between devices, body(): near_low1 = lax.ppermute(high, axes, up)  7.85 us
    pallas_call x1, Pallas kernels, mixing(): pl.pallas_call(mixing_kernel, name='mixing', grid_spec=pltpu.PrefetchScal...  6.98 us
    ppermute x1, starting transfers between devices, body(): near_high0 = lax.ppermute(low, axes, down)  5.55 us
    ppermute x1, waiting for transfers between devices, body(): near_high0 = lax.ppermute(low, axes, down)  3.7 us
    ppermute x1, starting transfers between devices, body(): near_low1 = lax.ppermute(high, axes, up)  2.11 us
  transfers between devices with their start and end apart: 6, of which 2 were waited for; matrix products, arithmetic and copies ran while one was open for 1% of the time, Pallas kernels for 10%

profile of v2, /device:TPU:1, one launch (start us, length us, event | category | flops | bytes accessed | tf_op | source)
XLA Modules:
  0.0 72.3 jit_solution(2632909462542284189)
XLA Ops:
  0.0 0.0 copy-start.6
  0.0 12.8 %deposit.1 = (f32[2,6,16,16,128]{4,3,2,1,0:T(8,128)}, bf16[6,16,16,128]{3,2,1,0:T(8,128)(2,1)}, bf16[6,16,16,128]{3,2,1,0:T(8,128)(2,1)}) custom-call(s32[128]{0:T(128)} %bitcast.22, s32[128,512]{1,0:T(8,128)} %bitcast.15, s32[128,512]{1,0:T(8,128)} %bitcast.20, bf16[6,128,512]{2,1,0:T(8,128)(2,1)} %bitcast.18), custom_call_target="tpu_custom_call" | custom-call | flops 4000000000 | bytes 5000000 | tf_op jit(solution)/shard_map/deposit/pallas_call | solution.py:86
  12.9 2.1 %collective-permute-start = (bf16[6,16,16,128]{3,2,1,0:T(8,128)(2,1)}, bf16[6,16,16,128]{3,2,1,0:T(8,128)(2,1)S(1)}, u32[]{:S(2)}, u32[]{:S(2)}) collective-permute-start(bf16[6,16,16,128]{3,2,1,0:T(8,128)(2,1)} %get-tuple-element.9), channel_id=1, source_target_pairs={{0,1},{1,2},{2,3},{3,4},{4,5},{5,6},{6,7},{7,8},{8,9},{9,10},{10,1... | collective-permute-start | bytes 1179656 | tf_op jit(solution)/shard_map/ppermute | solution.py:320
  15.0 5.5 %collective-permute-start.3 = (bf16[6,16,16,128]{3,2,1,0:T(8,128)(2,1)}, bf16[6,16,16,128]{3,2,1,0:T(8,128)(2,1)S(1)}, u32[]{:S(2)}, u32[]{:S(2)}) collective-permute-start(bf16[6,16,16,128]{3,2,1,0:T(8,128)(2,1)} %get-tuple-element.10), channel_id=1, source_target_pairs={{1,0},{2,1},{3,2},{4,3},{5,4},{6,5},{7,6},{8,7},{9,8},{10,9},{11,1... | collective-permute-start | bytes 1179656 | tf_op jit(solution)/shard_map/ppermute | solution.py:321
  20.5 1.9 %collective-permute-start.4 = (bf16[6,16,16,128]{3,2,1,0:T(8,128)(2,1)}, bf16[6,16,16,128]{3,2,1,0:T(8,128)(2,1)S(1)}, u32[]{:S(2)}, u32[]{:S(2)}) collective-permute-start(bf16[6,16,16,128]{3,2,1,0:T(8,128)(2,1)} %get-tuple-element.9), channel_id=1, source_target_pairs={{1,0},{2,1},{3,2},{4,3},{5,4},{6,5},{7,6},{8,7},{9,8},{10,9},{11,1... | collective-permute-start | bytes 1179656 | tf_op jit(solution)/shard_map/ppermute | solution.py:323
  22.5 0.0 collective-permute-start.2
  22.5 7.9 %collective-permute-done.near_low1 = bf16[6,16,16,128]{3,2,1,0:T(8,128)(2,1)S(1)} collective-permute-done((bf16[6,16,16,128]{3,2,1,0:T(8,128)(2,1)}, bf16[6,16,16,128]{3,2,1,0:T(8,128)(2,1)S(1)}, u32[]{:S(2)}, u32[]{:S(2)}) %collective-permute-start) | collective-permute-done | bytes 393248 | tf_op jit(solution)/shard_map/ppermute | solution.py:320
  30.3 0.0 copy-start
  30.3 0.0 collective-permute-start.1
  30.3 3.7 %collective-permute-done.3.near_high0 = bf16[6,16,16,128]{3,2,1,0:T(8,128)(2,1)S(1)} collective-permute-done((bf16[6,16,16,128]{3,2,1,0:T(8,128)(2,1)}, bf16[6,16,16,128]{3,2,1,0:T(8,128)(2,1)S(1)}, u32[]{:S(2)}, u32[]{:S(2)}) %collective-permute-start.3) | collective-permute-done | bytes 393248 | tf_op jit(solution)/shard_map/ppermute | solution.py:321
  34.0 0.0 copy-start.1
  34.0 9.9 %collective-permute-start.5 = (bf16[6,16,16,128]{3,2,1,0:T(8,128)(2,1)S(1)}, bf16[6,16,16,128]{3,2,1,0:T(8,128)(2,1)S(1)}, u32[]{:S(2)}, u32[]{:S(2)}) collective-permute-start(bf16[6,16,16,128]{3,2,1,0:T(8,128)(2,1)S(1)} %collective-permute-done.3.near_high0), channel_id=1, source_target_pairs={{1,0},{2,1},{3,2},{4,3},{5,4},{6,5},{7,6},{8,7},{9,8},{10,9},{11,1... | collective-permute-start | bytes 1179656 | tf_op jit(solution)/shard_map/ppermute | solution.py:325
  43.9 0.0 copy-done.6
  43.9 0.1 copy.7
  44.0 0.6 fusion.3.mix_matrix
  44.6 7.0 %mixing.1.mixed_far = f32[128,8,512]{2,1,0:T(8,128)} custom-call(s32[128]{0:T(128)} %bitcast.23, f32[6,6]{1,0:T(8,128)} %fusion.3.mix_matrix, s32[128,512]{1,0:T(8,128)} %bitcast.16, s32[128,512]{1,0:T(8,128)} %bitcast.21, bf16[6,128,512]{2,1,0:T(8,128)(2,1)} %bitcast.19), custom_call_target="tpu_custom_call" | custom-call | flops 1000000000 | bytes 4000000 | tf_op jit(solution)/shard_map/mixing/pallas_call | solution.py:135
  51.6 0.0 collective-permute-done.4.near_high1
  51.6 0.0 copy-start.2
  51.6 0.0 collective-permute-done.2.near_low0
  51.6 0.0 copy-start.3
  51.6 0.0 collective-permute-done.1.far_low
  51.6 0.0 copy-start.4
  51.6 0.0 collective-permute-done.5.far_high
  51.6 0.0 copy-start.5
  51.6 0.0 copy-done
  51.6 0.0 copy-done.1
  51.6 0.7 copy-done.2
  52.3 0.1 copy-done.3
  52.5 0.2 copy-done.4
  52.6 0.1 copy-done.5
  52.7 19.5 %force.1 = f32[3,128,512]{2,1,0:T(8,128)} custom-call(s32[128,512]{1,0:T(8,128)} %bitcast.17, bf16[256,512]{1,0:T(8,128)(2,1)} %constant.13.taps, f32[2,6,16,16,128]{4,3,2,1,0:T(8,128)} %get-tuple-element.8.own, bf16[6,16,16,128]{3,2,1,0:T(8,128)(2,1)} %copy-done.4, bf16[6,16,16,128]{3,2,1,0:T(8,128)(2,1)} %copy-done.3, bf16[6,16,16,128]{3,2,1,0:T(8,128)(2,1)} %copy-done, ...), custom_call_target="tpu_custom_call" | custom-call | tf_op jit(solution)/shard_map/force/pallas_call | solution.py:287
Async XLA Ops:
  0.0 43.9 %copy-start.6 = (f32[6,6]{1,0:T(8,128)S(1)}, f32[6,6]{1,0:T(8,128)}, u32[]{:S(2)}) copy-start(f32[6,6]{1,0:T(8,128)} %param.10) | copy-start | bytes 436
  12.9 17.5 %collective-permute-start = (bf16[6,16,16,128]{3,2,1,0:T(8,128)(2,1)}, bf16[6,16,16,128]{3,2,1,0:T(8,128)(2,1)S(1)}, u32[]{:S(2)}, u32[]{:S(2)}) collective-permute-start(bf16[6,16,16,128]{3,2,1,0:T(8,128)(2,1)} %get-tuple-element.9), channel_id=1, source_target_pairs={{0,1},{1,2},{2,3},{3,4},{4,5},{5,6},{6,7},{7,8},{8,9},{9,10},{10,1... | collective-permute-start | bytes 1179656 | tf_op jit(solution)/shard_map/ppermute | solution.py:320
  15.0 19.1 %collective-permute-start.3 = (bf16[6,16,16,128]{3,2,1,0:T(8,128)(2,1)}, bf16[6,16,16,128]{3,2,1,0:T(8,128)(2,1)S(1)}, u32[]{:S(2)}, u32[]{:S(2)}) collective-permute-start(bf16[6,16,16,128]{3,2,1,0:T(8,128)(2,1)} %get-tuple-element.10), channel_id=1, source_target_pairs={{1,0},{2,1},{3,2},{4,3},{5,4},{6,5},{7,6},{8,7},{9,8},{10,9},{11,1... | collective-permute-start | bytes 1179656 | tf_op jit(solution)/shard_map/ppermute | solution.py:321
  20.5 31.0 %collective-permute-start.4 = (bf16[6,16,16,128]{3,2,1,0:T(8,128)(2,1)}, bf16[6,16,16,128]{3,2,1,0:T(8,128)(2,1)S(1)}, u32[]{:S(2)}, u32[]{:S(2)}) collective-permute-start(bf16[6,16,16,128]{3,2,1,0:T(8,128)(2,1)} %get-tuple-element.9), channel_id=1, source_target_pairs={{1,0},{2,1},{3,2},{4,3},{5,4},{6,5},{7,6},{8,7},{9,8},{10,9},{11,1... | collective-permute-start | bytes 1179656 | tf_op jit(solution)/shard_map/ppermute | solution.py:323
  22.5 29.1 %collective-permute-start.2 = (bf16[6,16,16,128]{3,2,1,0:T(8,128)(2,1)}, bf16[6,16,16,128]{3,2,1,0:T(8,128)(2,1)S(1)}, u32[]{:S(2)}, u32[]{:S(2)}) collective-permute-start(bf16[6,16,16,128]{3,2,1,0:T(8,128)(2,1)} %get-tuple-element.10), channel_id=1, source_target_pairs={{0,1},{1,2},{2,3},{3,4},{4,5},{5,6},{6,7},{7,8},{8,9},{9,10},{10,1... | collective-permute-start | bytes 1179656 | tf_op jit(solution)/shard_map/ppermute | solution.py:322
  30.3 21.3 %copy-start = (bf16[6,16,16,128]{3,2,1,0:T(8,128)(2,1)}, bf16[6,16,16,128]{3,2,1,0:T(8,128)(2,1)S(1)}, u32[]{:S(2)}) copy-start(bf16[6,16,16,128]{3,2,1,0:T(8,128)(2,1)S(1)} %collective-permute-done.near_low1) | copy-start | bytes 1179652
  30.3 21.3 %collective-permute-start.1 = (bf16[6,16,16,128]{3,2,1,0:T(8,128)(2,1)S(1)}, bf16[6,16,16,128]{3,2,1,0:T(8,128)(2,1)S(1)}, u32[]{:S(2)}, u32[]{:S(2)}) collective-permute-start(bf16[6,16,16,128]{3,2,1,0:T(8,128)(2,1)S(1)} %collective-permute-done.near_low1), channel_id=1, source_target_pairs={{0,1},{1,2},{2,3},{3,4},{4,5},{5,6},{6,7},{7,8},{8,9},{9,10},{10,1... | collective-permute-start | bytes 1179656 | tf_op jit(solution)/shard_map/ppermute | solution.py:324
  34.0 17.6 %copy-start.1 = (bf16[6,16,16,128]{3,2,1,0:T(8,128)(2,1)}, bf16[6,16,16,128]{3,2,1,0:T(8,128)(2,1)S(1)}, u32[]{:S(2)}) copy-start(bf16[6,16,16,128]{3,2,1,0:T(8,128)(2,1)S(1)} %collective-permute-done.3.near_high0) | copy-start | bytes 1179652
  34.0 17.6 %collective-permute-start.5 = (bf16[6,16,16,128]{3,2,1,0:T(8,128)(2,1)S(1)}, bf16[6,16,16,128]{3,2,1,0:T(8,128)(2,1)S(1)}, u32[]{:S(2)}, u32[]{:S(2)}) collective-permute-start(bf16[6,16,16,128]{3,2,1,0:T(8,128)(2,1)S(1)} %collective-permute-done.3.near_high0), channel_id=1, source_target_pairs={{1,0},{2,1},{3,2},{4,3},{5,4},{6,5},{7,6},{8,7},{9,8},{10,9},{11,1... | collective-permute-start | bytes 1179656 | tf_op jit(solution)/shard_map/ppermute | solution.py:325
  51.6 0.8 %copy-start.2 = (bf16[6,16,16,128]{3,2,1,0:T(8,128)(2,1)}, bf16[6,16,16,128]{3,2,1,0:T(8,128)(2,1)S(1)}, u32[]{:S(2)}) copy-start(bf16[6,16,16,128]{3,2,1,0:T(8,128)(2,1)S(1)} %collective-permute-done.4.near_high1) | copy-start | bytes 1179652
  51.6 0.9 %copy-start.3 = (bf16[6,16,16,128]{3,2,1,0:T(8,128)(2,1)}, bf16[6,16,16,128]{3,2,1,0:T(8,128)(2,1)S(1)}, u32[]{:S(2)}) copy-start(bf16[6,16,16,128]{3,2,1,0:T(8,128)(2,1)S(1)} %collective-permute-done.2.near_low0) | copy-start | bytes 1179652
  51.6 1.0 %copy-start.4 = (bf16[6,16,16,128]{3,2,1,0:T(8,128)(2,1)}, bf16[6,16,16,128]{3,2,1,0:T(8,128)(2,1)S(1)}, u32[]{:S(2)}) copy-start(bf16[6,16,16,128]{3,2,1,0:T(8,128)(2,1)S(1)} %collective-permute-done.1.far_low) | copy-start | bytes 1179652
  51.6 1.1 %copy-start.5 = (bf16[6,16,16,128]{3,2,1,0:T(8,128)(2,1)}, bf16[6,16,16,128]{3,2,1,0:T(8,128)(2,1)S(1)}, u32[]{:S(2)}) copy-start(bf16[6,16,16,128]{3,2,1,0:T(8,128)(2,1)S(1)} %collective-permute-done.5.far_high) | copy-start | bytes 1179652

commit v3 on v2

v3 whole, which is shorter than its diff:
```python
import jax
import jax.numpy as jnp
import numpy as np
from jax import lax
from jax.experimental import pallas as pl
from jax.experimental.pallas import tpu as pltpu
from jax.sharding import PartitionSpec as P

SPECIES = 6
ROWS = 8
COLS = 16
HALVES = 16
LANES = 128
SLOTS = 512
CHUNKS = 3
PER = SPECIES // CHUNKS
GROUP = 8
MIB = 1 << 20

raw_taps = (0.1353352832366127, 0.6065306597126334, 1.0)
tap_total = raw_taps[2] + 2.0 * (raw_taps[0] + raw_taps[1])
T2, T1, T0 = (t / tap_total for t in raw_taps)

f32 = jnp.float32
bf16 = jnp.bfloat16


def onehot_of(row, count):
    wide = jnp.broadcast_to(row, (16, SLOTS))
    ids = lax.broadcasted_iota(jnp.int32, (16, SLOTS), 0)
    inner = jnp.where((wide & 15) == ids, 1.0, 0.0).astype(bf16)
    outer = (wide >> 4).astype(f32).astype(bf16)
    none = jnp.zeros((16, SLOTS), bf16)
    return jnp.concatenate(
        [jnp.where(outer == jnp.full((16, SLOTS), i, bf16), inner, none) for i in range(count)], axis=0
    )


def weights_of(limit, t, rows, species, mix):
    part = pl.ds(t * LANES, LANES)
    lane = lax.broadcasted_iota(jnp.int32, (COLS, LANES), 1)
    valid = (lane + t * LANES) < limit
    kind = species[rows, part]
    found = []
    for k in range(SPECIES):
        w = jnp.where(kind == k, 1.0, 0.0) + mix[k, rows, part].astype(f32)
        found.append(jnp.where(valid, w, 0.0).astype(bf16).astype(f32))
    return found


def limits_of(counts, first):
    rows = lax.broadcasted_iota(jnp.int32, (COLS, LANES), 0)
    limit = jnp.zeros((COLS, LANES), jnp.int32)
    for i in range(COLS):
        limit = jnp.where(rows == i, counts[first + i], limit)
    return limit


def deposit_kernel(counts, cells_far, species_far, mix_far, own, sent0, sent1, sent2,
                   cells, species, mix, w_s, d_s, sems):
    sent = (sent0, sent1, sent2)

    def fetches(r):
        rows = pl.ds(pl.multiple_of(r * COLS, COLS), COLS)
        return (
            pltpu.make_async_copy(cells_far.at[rows], cells.at[rows], sems.at[0, r]),
            pltpu.make_async_copy(species_far.at[rows], species.at[rows], sems.at[1, r]),
            pltpu.make_async_copy(mix_far.at[:, rows], mix.at[:, rows], sems.at[2, r]),
        )

    for r in range(ROWS):
        for copy in fetches(r):
            copy.start()
    zero = jnp.zeros((COLS, LANES), f32)
    for t in range(4):
        for k in (6, 7):
            w_s[t, k * COLS:(k + 1) * COLS] = zero
            w_s[t, (8 + k) * COLS:(9 + k) * COLS] = zero

    def one_row(r, carry):
        for copy in fetches(r):
            copy.wait()
        first = pl.multiple_of(r * COLS, COLS)
        rows = pl.ds(first, COLS)
        limit = limits_of(counts, first)
        for t in range(4):
            upper = (cells[rows, pl.ds(t * LANES, LANES)] & 1) == 1
            for k, w in enumerate(weights_of(limit, t, rows, species, mix)):
                w_s[t, k * COLS:(k + 1) * COLS] = jnp.where(upper, 0.0, w)
                w_s[t, (8 + k) * COLS:(9 + k) * COLS] = jnp.where(upper, w, 0.0)
        for b in range(COLS):
            plane = cells[pl.ds(first + b, 1), :] >> 8
            table = onehot_of(plane & 127, 8)
            w = jnp.concatenate([w_s[t, pl.ds(b, 16, stride=COLS)] for t in range(4)], axis=1).astype(bf16)
            second = jnp.broadcast_to(plane >> 7, (16, SLOTS)).astype(f32).astype(bf16) > 0.5
            none = jnp.zeros((16, SLOTS), bf16)
            halves = jnp.concatenate([jnp.where(second, none, w), jnp.where(second, w, none)], axis=0)
            dens = lax.dot_general(halves, table, (((1,), (1,)), ((), ())), preferred_element_type=f32)
            d_s[0, pl.ds(b, 16, stride=COLS)] = dens[:16]
            d_s[1, pl.ds(b, 16, stride=COLS)] = dens[16:]
        for z in range(2):
            for k in range(SPECIES):
                for h in range(2):
                    value = d_s[h, (z * 8 + k) * COLS:(z * 8 + k + 1) * COLS]
                    own[z, k, 2 * r + h] = value
                    sent[k // PER][z, k % PER, 2 * r + h] = value.astype(bf16)
        return carry

    lax.fori_loop(0, ROWS, one_row, 0)


VM = pltpu.MemorySpace.VMEM
SM = pltpu.MemorySpace.SMEM


def deposit(counts, cells, species, mix):
    half = (HALVES, COLS, LANES)
    return pl.pallas_call(
        deposit_kernel,
        name="deposit",
        in_specs=[pl.BlockSpec(memory_space=SM)] + [pl.BlockSpec(memory_space=pl.ANY)] * 3,
        out_specs=[pl.BlockSpec(memory_space=VM)] * 4,
        scratch_shapes=[
            pltpu.VMEM((ROWS * COLS, SLOTS), jnp.int32),
            pltpu.VMEM((ROWS * COLS, SLOTS), jnp.int32),
            pltpu.VMEM((SPECIES, ROWS * COLS, SLOTS), bf16),
            pltpu.VMEM((4, 16 * COLS, LANES), f32),
            pltpu.VMEM((2, 16 * COLS, LANES), f32),
            pltpu.SemaphoreType.DMA((3, ROWS)),
        ],
        out_shape=[jax.ShapeDtypeStruct((2, SPECIES) + half, f32)]
        + [jax.ShapeDtypeStruct((2, PER) + half, bf16)] * CHUNKS,
        compiler_params=pltpu.CompilerParams(vmem_limit_bytes=16 * MIB),
        cost_estimate=pl.CostEstimate(flops=10**9, bytes_accessed=5 * 10**6, transcendentals=0),
    )(counts, cells, species, mix)


def mixing_kernel(counts, mix_matrix, species, mix, mixed):
    def one_row(r, carry):
        first = pl.multiple_of(r * COLS, COLS)
        rows = pl.ds(first, COLS)
        limit = limits_of(counts, first)
        for t in range(4):
            ws = weights_of(limit, t, rows, species, mix)
            for l in range(SPECIES):
                v = mix_matrix[l, 0] * ws[0]
                for k in range(1, SPECIES):
                    v = v + mix_matrix[l, k] * ws[k]
                mixed[l, rows, t * LANES:(t + 1) * LANES] = v
        return carry

    lax.fori_loop(0, ROWS, one_row, 0)


def mixing(counts, mix_matrix, species, mix):
    return pl.pallas_call(
        mixing_kernel,
        name="mixing",
        in_specs=[pl.BlockSpec(memory_space=SM)] * 2 + [pl.BlockSpec(memory_space=VM)] * 2,
        out_specs=pl.BlockSpec(memory_space=VM),
        out_shape=jax.ShapeDtypeStruct((SPECIES, ROWS * COLS, SLOTS), f32),
        compiler_params=pltpu.CompilerParams(vmem_limit_bytes=12 * MIB),
        cost_estimate=pl.CostEstimate(flops=10**9, bytes_accessed=4 * 10**6, transcendentals=0),
    )(counts, mix_matrix, species, mix)


def scaled_taps():
    smooth_scale, slope_scale = 1.6396387, 1.5596421
    smooth_taps = {0: T0, 1: T1, -1: T1, 2: T2, -2: T2}
    slope_taps = {1: 0.5 * (T0 - T2), 2: 0.5 * T1, 3: 0.5 * T2}
    slope_taps.update({-j: -v for j, v in slope_taps.items()})
    return (
        {j: smooth_scale * v for j, v in smooth_taps.items()},
        {j: slope_scale * v for j, v in slope_taps.items()},
        smooth_scale,
        slope_scale,
    )


SMOOTH, SLOPE, SMOOTH_SCALE, SLOPE_SCALE = scaled_taps()


def tap_matrices():
    lane = np.arange(LANES)
    x, y = lane // 16, lane % 16
    results = []
    for main, other, extent in ((y, x, 16), (x, y, 8)):
        source = np.concatenate([main, np.where(main < extent // 2, main + extent, main - extent)])
        same = np.concatenate([other, other])[:, None] == other[None, :]
        gap = source[:, None] - main[None, :]
        for taps in (SMOOTH, SLOPE):
            matrix = np.zeros((2 * LANES, LANES), np.float32)
            for j, value in taps.items():
                matrix += np.where(same & (gap == j), np.float32(value), np.float32(0))
            results.append(matrix)
    return jnp.asarray(np.concatenate(results, axis=1)).astype(bf16)


def split(v):
    top = v.astype(bf16)
    return top, (v - top.astype(f32)).astype(bf16)


def smooth_kernel(taps, own, near_low, near_high, far_low, far_high, ready, x_s, y_s, w_s, g_s):
    k = pl.program_id(0)
    lane = lax.broadcasted_iota(jnp.int32, (COLS, LANES), 1)
    col = lane & 15
    cu = 1.0 / (SMOOTH_SCALE * SLOPE_SCALE)
    cz = 0.5 / (SMOOTH_SCALE * SMOOTH_SCALE)
    for h in range(HALVES):
        l2 = far_low[0, h].astype(f32)
        a = near_low[0, 0, h].astype(f32)
        b = near_low[1, 0, h].astype(f32)
        o0 = own[0, 0, h]
        o1 = own[1, 0, h]
        r0 = near_high[0, 0, h].astype(f32)
        r1 = near_high[1, 0, h].astype(f32)
        r2 = far_high[0, h].astype(f32)
        um = T2 * (l2 + o1) + T1 * (a + o0) + T0 * b
        u0 = T2 * (a + r0) + T1 * (b + o1) + T0 * o0
        u1 = T2 * (b + r1) + T1 * (o0 + r0) + T0 * o1
        up = T2 * (o0 + r2) + T1 * (o1 + r1) + T0 * r0
        for i, v in enumerate((cu * u0, cu * u1, cz * (u1 - um), cz * (up - u0))):
            around = jnp.where(col < 8, pltpu.roll(v, COLS - 1, 0), pltpu.roll(v, 1, 0))
            for part, value in ((0, v), (1, around)):
                for level, piece in enumerate(split(value)):
                    x_s[level, i, h * COLS:(h + 1) * COLS, part * LANES:(part + 1) * LANES] = piece
    for i in range(4):
        width = 2 * LANES if i < 2 else LANES
        table = taps[:, :width]
        out = jnp.dot(x_s[0, i], table, preferred_element_type=f32) + jnp.dot(
            x_s[1, i], table, preferred_element_type=f32
        )
        if i < 2:
            y_s[i] = out[:, :LANES]
            y_s[2 + i] = out[:, LANES:]
        else:
            y_s[2 + i] = out
    for p in range(6):
        for h in range(HALVES):
            before = (h + HALVES - 1) % HALVES
            after = (h + 1) % HALVES
            v = y_s[p, h * COLS:(h + 1) * COLS]
            around = jnp.where(
                lane < 64,
                y_s[p, after * COLS:(after + 1) * COLS],
                y_s[p, before * COLS:(before + 1) * COLS],
            )
            for part, value in ((0, v), (1, around)):
                for level, piece in enumerate(split(value)):
                    w_s[level, p, h * COLS:(h + 1) * COLS, part * LANES:(part + 1) * LANES] = piece
        table = taps[:, 3 * LANES:] if p < 2 else taps[:, 2 * LANES:3 * LANES]
        out = jnp.dot(w_s[0, p], table, preferred_element_type=f32) + jnp.dot(
            w_s[1, p], table, preferred_element_type=f32
        )
        for h in range(HALVES):
            g_s[h, pl.ds(pl.multiple_of((k * 8 + p) * COLS, COLS), COLS)] = out[h * COLS:(h + 1) * COLS]

    @pl.when(k == 0)
    def _():
        zero = jnp.zeros((HALVES, 2 * COLS, LANES), f32)
        for i in range(PER):
            g_s[:, (i * 8 + 6) * COLS:(i * 8 + 8) * COLS] = zero

    @pl.when(k == PER - 1)
    def _():
        def one_row(r, carry):
            for q in range(COLS):
                for h in range(2):
                    top, rest = split(g_s[2 * r + h, pl.ds(q, 16, stride=COLS)])
                    ready[r * COLS + q, :16, h * LANES:(h + 1) * LANES] = top
                    ready[r * COLS + q, 16:, h * LANES:(h + 1) * LANES] = rest
            return carry

        lax.fori_loop(0, ROWS, one_row, 0)


def smooth(chunk, taps, own, near_low, near_high, far_low, far_high):
    half = (HALVES, COLS, LANES)
    two = pl.BlockSpec((2, 1) + half, lambda k: (0, k, 0, 0, 0))
    one = pl.BlockSpec((1,) + half, lambda k: (k, 0, 0, 0))
    return pl.pallas_call(
        smooth_kernel,
        name="smooth",
        grid=(PER,),
        in_specs=[
            pl.BlockSpec((2 * LANES, 4 * LANES), lambda k: (0, 0)),
            pl.BlockSpec((2, 1) + half, lambda k: (0, chunk * PER + k, 0, 0, 0)),
            two,
            two,
            one,
            one,
        ],
        out_specs=pl.BlockSpec((ROWS * COLS, 32, 2 * LANES), lambda k: (0, 0, 0)),
        out_shape=jax.ShapeDtypeStruct((ROWS * COLS, 32, 2 * LANES), bf16),
        scratch_shapes=[
            pltpu.VMEM((2, 4, HALVES * COLS, 2 * LANES), bf16),
            pltpu.VMEM((6, HALVES * COLS, LANES), f32),
            pltpu.VMEM((2, 6, HALVES * COLS, 2 * LANES), bf16),
            pltpu.VMEM((HALVES, PER * 8 * COLS, LANES), f32),
        ],
        compiler_params=pltpu.CompilerParams(vmem_limit_bytes=24 * MIB),
        cost_estimate=pl.CostEstimate(flops=10**9, bytes_accessed=4 * 10**6, transcendentals=0),
    )(taps, own, near_low, near_high, far_low, far_high)


def pick_kernel(cells, ready0, ready1, ready2, mixed, forces, got_s):
    def one_group(g, slot):
        first = pl.multiple_of(g * GROUP, GROUP)
        for b in range(GROUP):
            d = first + b
            table = onehot_of(cells[pl.ds(d, 1), :] >> 8, 16)
            parts = [ready[d] for ready in (ready0, ready1, ready2)]
            rows = jnp.concatenate([p[:16] for p in parts] + [p[16:] for p in parts], axis=0)
            got = jnp.dot(rows, table, preferred_element_type=f32)
            got = got[:48] + got[48:]
            for t in range(4):
                got_s[slot, t, pl.ds(b, 48, stride=GROUP)] = got[:, t * LANES:(t + 1) * LANES]
        for t in range(4):
            lanes = slice(t * LANES, (t + 1) * LANES)
            upper = (cells[pl.ds(first, GROUP), lanes] & 1) == 1
            vs = [mixed[k, pl.ds(first, GROUP), lanes] for k in range(SPECIES)]
            for a in range(3):
                total = None
                for k in range(SPECIES):
                    row = ((k // PER) * 16 + (k % PER) * 8 + 2 * a) * GROUP
                    value = jnp.where(
                        upper, got_s[slot, t, row + GROUP:row + 2 * GROUP], got_s[slot, t, row:row + GROUP]
                    )
                    total = vs[k] * value if total is None else total + vs[k] * value
                forces[a, pl.ds(first, GROUP), lanes] = total

    def two_groups(i, carry):
        one_group(2 * i, 0)
        one_group(2 * i + 1, 1)
        return carry

    lax.fori_loop(0, ROWS * COLS // GROUP // 2, two_groups, 0)


def pick(cells, ready, mixed):
    return pl.pallas_call(
        pick_kernel,
        name="pick",
        in_specs=[pl.BlockSpec(memory_space=VM)] * 5,
        out_specs=pl.BlockSpec(memory_space=VM),
        out_shape=jax.ShapeDtypeStruct((3, ROWS * COLS, SLOTS), f32),
        scratch_shapes=[pltpu.VMEM((2, 4, 48 * GROUP, LANES), f32)],
        compiler_params=pltpu.CompilerParams(vmem_limit_bytes=24 * MIB),
        cost_estimate=pl.CostEstimate(flops=6 * 10**9, bytes_accessed=10**7, transcendentals=0),
    )(cells, *ready, mixed)


def body(send_cells, send_species, send_mix, send_counts, chi):
    axes = ("row", "col")
    count = lax.axis_size("row") * lax.axis_size("col")
    up = [(i, (i + 1) % count) for i in range(count)]
    down = [(j, i) for i, j in up]
    chis = 0.5 * (chi + chi.T) * (1.0 - jnp.eye(SPECIES, dtype=f32))
    mix_matrix = -0.5 * (chis + 1.0)
    cells, species, mix, counts = send_cells[0], send_species[0], send_mix[0], send_counts[0]
    own, *sent = deposit(counts, cells, species, mix)
    taps = tap_matrices()
    ready = []
    for chunk in range(CHUNKS):
        near_low = lax.ppermute(sent[chunk], axes, up)
        near_high = lax.ppermute(sent[chunk], axes, down)
        far_low = lax.ppermute(near_low[1], axes, up)
        far_high = lax.ppermute(near_high[0], axes, down)
        ready.append(smooth(chunk, taps, own, near_low, near_high, far_low, far_high))
    mixed = mixing(counts, mix_matrix, species, mix)
    return pick(cells, ready, mixed)[None]


def solution(mesh):
    return jax.shard_map(
        body,
        mesh=mesh,
        in_specs=(
            P(("row", "col"), None, None),
            P(("row", "col"), None, None),
            P(("row", "col"), None, None, None),
            P(("row", "col"), None),
            P(),
        ),
        out_specs=P(("row", "col"), None, None, None),
        check_vma=False,
    )
```

time: 72.7 us -> 81.4 us (1.12)
  the two profiles are of different devices: /device:TPU:1 before, /device:TPU:0 now
where the time goes in v3:
time: 81.4 us; the launch traced here: 81.2 us
  starting transfers between devices  44.7 us (55%)
  Pallas kernels  31.2 us (38%)
  local copies, waits for them, and re-layouts  5.02 us (6%)
    ppermute x3, starting transfers between devices, body(): far_high = lax.ppermute(near_high[0], axes, down)  21.7 us
    ppermute x3, starting transfers between devices, body(): near_high = lax.ppermute(sent[chunk], axes, down)  21 us
    pallas_call x3, Pallas kernels, smooth(): pl.pallas_call(smooth_kernel, name='smooth', grid=(PER,), in_specs=[pl.Bl...  11.1 us
    pallas_call x1, Pallas kernels, deposit(): pl.pallas_call(deposit_kernel, name='deposit', in_specs=[pl.BlockSpec(mem...  9.49 us
    pallas_call x1, Pallas kernels, pick(): pl.pallas_call(pick_kernel, name='pick', in_specs=[pl.BlockSpec(memory_sp...  8.91 us
    unnamed x21, local copies, waits for them, and re-layouts  4.96 us
    ppermute x3, starting transfers between devices, body(): near_low = lax.ppermute(sent[chunk], axes, up)  1.77 us
    pallas_call x1, Pallas kernels, mixing(): pl.pallas_call(mixing_kernel, name='mixing', in_specs=[pl.BlockSpec(memor...  1.7 us
  transfers between devices with their start and end apart: 12, of which 0 were waited for; matrix products, arithmetic and copies ran while one was open for 0% of the time, Pallas kernels for 11%

profile of v3, /device:TPU:0, one launch (start us, length us, event | category | flops | bytes accessed | tf_op | source)
XLA Modules:
  0.0 81.2 jit_solution(10141538941540172964)
XLA Ops:
  0.0 0.0 copy-start.8
  0.0 0.0 copy-start.9
  0.0 0.0 copy-start.1
  0.0 1.2 %copy-done.1 = bf16[1,6,128,512]{3,2,1,0:T(8,128)(2,1)S(1)} copy-done((bf16[1,6,128,512]{3,2,1,0:T(8,128)(2,1)S(1)}, bf16[1,6,128,512]{3,2,1,0:T(8,128)(2,1)}, u32[]{:S(2)}) %copy-start.1) | copy-done | bytes 786456
  1.2 0.0 copy-start.3
  1.2 0.9 %copy-done.3 = s32[1,128,512]{2,1,0:T(8,128)S(1)} copy-done((s32[1,128,512]{2,1,0:T(8,128)S(1)}, s32[1,128,512]{2,1,0:T(8,128)}, u32[]{:S(2)}) %copy-start.3) | copy-done | bytes 262168
  2.1 0.0 copy-start.5
  2.1 0.9 %copy-done.5 = s32[1,128,512]{2,1,0:T(8,128)S(1)} copy-done((s32[1,128,512]{2,1,0:T(8,128)S(1)}, s32[1,128,512]{2,1,0:T(8,128)}, u32[]{:S(2)}) %copy-start.5) | copy-done | bytes 262168
  3.1 0.0 copy-start.7
  3.1 0.7 copy-done.7
  3.7 0.0 copy-start.4
  3.7 9.5 %deposit.1 = (f32[2,6,16,16,128]{4,3,2,1,0:T(8,128)S(1)}, bf16[2,2,16,16,128]{4,3,2,1,0:T(8,128)(2,1)S(1)}, bf16[2,2,16,16,128]{4,3,2,1,0:T(8,128)(2,1)}, bf16[2,2,16,16,128]{4,3,2,1,0:T(8,128)(2,1)}) custom-call(s32[128]{0:T(128)S(1)} %bitcast.33, s32[128,512]{1,0:T(8,128)S(1)} %bitcast.31, s32[128,512]{1,0:T(8,128)S(1)} %bitcast.29, ...), custom_call_target="tpu_custom_call" | custom-call | flops 1000000000 | bytes 5000000 | tf_op jit(solution)/shard_map/deposit/pallas_call | solution.py:118
  13.2 1.8 %collective-permute-start.8 = (bf16[2,2,16,16,128]{4,3,2,1,0:T(8,128)(2,1)}, bf16[2,2,16,16,128]{4,3,2,1,0:T(8,128)(2,1)S(1)}, u32[]{:S(2)}, u32[]{:S(2)}) collective-permute-start(bf16[2,2,16,16,128]{4,3,2,1,0:T(8,128)(2,1)} %get-tuple-element.12), channel_id=1, source_target_pairs={{0,1},{1,2},{2,3},{3,4},{4,5},{5,6},{6,7},{7,8},{8,9},{9,10},{10,1... | collective-permute-start | bytes 786440 | tf_op jit(solution)/shard_map/ppermute | solution.py:366
  15.0 6.6 %collective-permute-start.9 = (bf16[2,2,16,16,128]{4,3,2,1,0:T(8,128)(2,1)}, bf16[2,2,16,16,128]{4,3,2,1,0:T(8,128)(2,1)S(1)}, u32[]{:S(2)}, u32[]{:S(2)}) collective-permute-start(bf16[2,2,16,16,128]{4,3,2,1,0:T(8,128)(2,1)} %get-tuple-element.12), channel_id=1, source_target_pairs={{1,0},{2,1},{3,2},{4,3},{5,4},{6,5},{7,6},{8,7},{9,8},{10,9},{11,1... | collective-permute-start | bytes 786440 | tf_op jit(solution)/shard_map/ppermute | solution.py:367
  21.6 0.0 collective-permute-start.4
  21.6 7.2 %collective-permute-start.5 = (bf16[2,2,16,16,128]{4,3,2,1,0:T(8,128)(2,1)}, bf16[2,2,16,16,128]{4,3,2,1,0:T(8,128)(2,1)S(1)}, u32[]{:S(2)}, u32[]{:S(2)}) collective-permute-start(bf16[2,2,16,16,128]{4,3,2,1,0:T(8,128)(2,1)} %get-tuple-element.11), channel_id=1, source_target_pairs={{1,0},{2,1},{3,2},{4,3},{5,4},{6,5},{7,6},{8,7},{9,8},{10,9},{11,1... | collective-permute-start | bytes 786440 | tf_op jit(solution)/shard_map/ppermute | solution.py:367
  28.8 0.0 collective-permute-start
  28.8 0.0 copy-done.9
  28.8 0.1 copy.7
  28.9 0.0 copy-done.8
  28.9 0.0 copy-done.4
  28.9 0.0 copy-start.2
  28.9 1.1 %copy-done.2 = bf16[1,6,128,512]{3,2,1,0:T(8,128)(2,1)S(1)} copy-done((bf16[1,6,128,512]{3,2,1,0:T(8,128)(2,1)S(1)}, bf16[1,6,128,512]{3,2,1,0:T(8,128)(2,1)}, u32[]{:S(2)}) %copy-start.2) | copy-done | bytes 786456
  30.0 0.0 copy-start
  30.1 1.7 %mixing.1.mixed = f32[6,128,512]{2,1,0:T(8,128)S(1)} custom-call(s32[128]{0:T(128)S(1)} %bitcast.34, f32[6,6]{1,0:T(8,128)S(1)} %fusion.3.mix_matrix, s32[128,512]{1,0:T(8,128)S(1)} %bitcast.30, bf16[6,128,512]{2,1,0:T(8,128)(2,1)S(1)} %bitcast.28), custom_call_target="tpu_custom_call" | custom-call | flops 1000000000 | bytes 4000000 | tf_op jit(solution)/shard_map/mixing/pallas_call | solution.py:156
  31.8 0.0 collective-permute-done.8.near_low
  31.8 7.2 %collective-permute-start.1 = (bf16[2,2,16,16,128]{4,3,2,1,0:T(8,128)(2,1)S(1)}, bf16[2,2,16,16,128]{4,3,2,1,0:T(8,128)(2,1)S(1)}, u32[]{:S(2)}, u32[]{:S(2)}) collective-permute-start(bf16[2,2,16,16,128]{4,3,2,1,0:T(8,128)(2,1)S(1)} %get-tuple-element.10), channel_id=1, source_target_pairs={{1,0},{2,1},{3,2},{4,3},{5,4},{6,5},{7,6},{8,7},{9,8},{10,9},{11,1... | collective-permute-start | bytes 786440 | tf_op jit(solution)/shard_map/ppermute | solution.py:367
  39.0 0.0 collective-permute-done.9.near_high
  39.0 0.1 collective-permute-start.10
  39.1 0.0 collective-permute-done.4.near_low
  39.2 7.2 %collective-permute-start.11 = (bf16[2,16,16,128]{3,2,1,0:T(8,128)(2,1)S(1)}, bf16[2,16,16,128]{3,2,1,0:T(8,128)(2,1)S(1)}, u32[]{:S(2)}, u32[]{:S(2)}) collective-permute-start(bf16[2,16,16,128]{3,2,1,0:T(8,128)(2,1)S(1)} %slice_bitcast_fusion), channel_id=1, source_target_pairs={{1,0},{2,1},{3,2},{4,3},{5,4},{6,5},{7,6},{8,7},{9,8},{10,9},{11,1... | collective-permute-start | bytes 393224 | tf_op jit(solution)/shard_map/ppermute | solution.py:369
  46.4 0.0 collective-permute-done.5.near_high
  46.4 0.1 collective-permute-start.6
  46.5 0.0 collective-permute-done.near_low
  46.5 7.2 %collective-permute-start.7 = (bf16[2,16,16,128]{3,2,1,0:T(8,128)(2,1)S(1)}, bf16[2,16,16,128]{3,2,1,0:T(8,128)(2,1)S(1)}, u32[]{:S(2)}, u32[]{:S(2)}) collective-permute-start(bf16[2,16,16,128]{3,2,1,0:T(8,128)(2,1)S(1)} %slice_bitcast_fusion.2), channel_id=1, source_target_pairs={{1,0},{2,1},{3,2},{4,3},{5,4},{6,5},{7,6},{8,7},{9,8},{10,9},{11,1... | collective-permute-start | bytes 393224 | tf_op jit(solution)/shard_map/ppermute | solution.py:369
  53.8 0.0 collective-permute-done.1.near_high
  53.8 0.1 collective-permute-start.2
  53.9 0.0 collective-permute-done.10.far_low
  53.9 7.2 %collective-permute-start.3 = (bf16[2,16,16,128]{3,2,1,0:T(8,128)(2,1)S(1)}, bf16[2,16,16,128]{3,2,1,0:T(8,128)(2,1)S(1)}, u32[]{:S(2)}, u32[]{:S(2)}) collective-permute-start(bf16[2,16,16,128]{3,2,1,0:T(8,128)(2,1)S(1)} %slice_bitcast_fusion.4), channel_id=1, source_target_pairs={{1,0},{2,1},{3,2},{4,3},{5,4},{6,5},{7,6},{8,7},{9,8},{10,9},{11,1... | collective-permute-start | bytes 393224 | tf_op jit(solution)/shard_map/ppermute | solution.py:369
  61.1 0.0 collective-permute-done.11.far_high
  61.1 0.0 copy-done
  61.1 3.7 %smooth.5.ready2 = bf16[128,32,256]{2,1,0:T(8,128)(2,1)S(1)} custom-call(bf16[256,512]{1,0:T(8,128)(2,1)S(1)} %copy-done, f32[2,6,16,16,128]{4,3,2,1,0:T(8,128)S(1)} %get-tuple-element.9.own, bf16[2,2,16,16,128]{4,3,2,1,0:T(8,128)(2,1)S(1)} %collective-permute-done.8.near_low, bf16[2,2,16,16,128]{4,3,2,1,0:T(8,128)(2,1)S(1)} %collective-permute-done.9.near_high, ...), custom_call_target="tpu_custom_call" | custom-call | flops 1000000000 | bytes 4000000 | tf_op jit(solution)/shard_map/smooth/pallas_call | solution.py:282
  64.8 0.0 collective-permute-done.6.far_low
  64.8 0.0 collective-permute-done.7.far_high
  64.8 3.7 %smooth.4.ready1 = bf16[128,32,256]{2,1,0:T(8,128)(2,1)S(1)} custom-call(bf16[256,512]{1,0:T(8,128)(2,1)S(1)} %copy-done, f32[2,6,16,16,128]{4,3,2,1,0:T(8,128)S(1)} %get-tuple-element.9.own, bf16[2,2,16,16,128]{4,3,2,1,0:T(8,128)(2,1)S(1)} %collective-permute-done.4.near_low, bf16[2,2,16,16,128]{4,3,2,1,0:T(8,128)(2,1)S(1)} %collective-permute-done.5.near_high, ...), custom_call_target="tpu_custom_call" | custom-call | flops 1000000000 | bytes 4000000 | tf_op jit(solution)/shard_map/smooth/pallas_call | solution.py:282
  68.6 0.0 copy-start.6
  68.6 0.0 collective-permute-done.2.far_low
  68.6 0.0 collective-permute-done.3.far_high
  68.6 3.7 %smooth.3.ready0 = bf16[128,32,256]{2,1,0:T(8,128)(2,1)S(1)} custom-call(bf16[256,512]{1,0:T(8,128)(2,1)S(1)} %copy-done, f32[2,6,16,16,128]{4,3,2,1,0:T(8,128)S(1)} %get-tuple-element.9.own, bf16[2,2,16,16,128]{4,3,2,1,0:T(8,128)(2,1)S(1)} %collective-permute-done.near_low, bf16[2,2,16,16,128]{4,3,2,1,0:T(8,128)(2,1)S(1)} %collective-permute-done.1.near_high, ...), custom_call_target="tpu_custom_call" | custom-call | flops 1000000000 | bytes 4000000 | tf_op jit(solution)/shard_map/smooth/pallas_call | solution.py:282
  72.3 0.0 copy-done.6
  72.3 8.9 %pick.1 = f32[3,128,512]{2,1,0:T(8,128)} custom-call(s32[128,512]{1,0:T(8,128)S(1)} %bitcast.32, bf16[128,32,256]{2,1,0:T(8,128)(2,1)S(1)} %smooth.3.ready0, bf16[128,32,256]{2,1,0:T(8,128)(2,1)S(1)} %smooth.4.ready1, bf16[128,32,256]{2,1,0:T(8,128)(2,1)S(1)} %smooth.5.ready2, f32[6,128,512]{2,1,0:T(8,128)S(1)} %mixing.1.mixed), custom_call_target="tpu_custom_call" | custom-call | flops 6000000000 | bytes 10000000 | tf_op jit(solution)/shard_map/pick/pallas_call | solution.py:342
  (7 shorter events, 0.1 us)
Async XLA Ops:
  0.0 28.9 %copy-start.8 = (s32[1,128]{1,0:T(1,128)S(1)}, s32[1,128]{1,0:T(1,128)}, u32[]{:S(2)}) copy-start(s32[1,128]{1,0:T(1,128)} %param.9) | copy-start | bytes 1540
  0.0 28.8 %copy-start.9 = (f32[6,6]{1,0:T(8,128)S(1)}, f32[6,6]{1,0:T(8,128)}, u32[]{:S(2)}) copy-start(f32[6,6]{1,0:T(8,128)} %param.10) | copy-start | bytes 436
  0.0 1.2 %copy-start.1 = (bf16[1,6,128,512]{3,2,1,0:T(8,128)(2,1)S(1)}, bf16[1,6,128,512]{3,2,1,0:T(8,128)(2,1)}, u32[]{:S(2)}) copy-start(bf16[1,6,128,512]{3,2,1,0:T(8,128)(2,1)} %param.8) | copy-start | bytes 2359300
  1.2 0.9 %copy-start.3 = (s32[1,128,512]{2,1,0:T(8,128)S(1)}, s32[1,128,512]{2,1,0:T(8,128)}, u32[]{:S(2)}) copy-start(s32[1,128,512]{2,1,0:T(8,128)} %param.7) | copy-start | bytes 786436
  2.1 0.9 %copy-start.5 = (s32[1,128,512]{2,1,0:T(8,128)S(1)}, s32[1,128,512]{2,1,0:T(8,128)}, u32[]{:S(2)}) copy-start(s32[1,128,512]{2,1,0:T(8,128)} %param.6) | copy-start | bytes 786436
  3.1 0.7 copy-start.7
  3.7 25.2 %copy-start.4 = (s32[1,128,512]{2,1,0:T(8,128)S(1)}, s32[1,128,512]{2,1,0:T(8,128)}, u32[]{:S(2)}) copy-start(s32[1,128,512]{2,1,0:T(8,128)} %param.7) | copy-start | bytes 786436
  13.2 18.5 %collective-permute-start.8 = (bf16[2,2,16,16,128]{4,3,2,1,0:T(8,128)(2,1)}, bf16[2,2,16,16,128]{4,3,2,1,0:T(8,128)(2,1)S(1)}, u32[]{:S(2)}, u32[]{:S(2)}) collective-permute-start(bf16[2,2,16,16,128]{4,3,2,1,0:T(8,128)(2,1)} %get-tuple-element.12), channel_id=1, source_target_pairs={{0,1},{1,2},{2,3},{3,4},{4,5},{5,6},{6,7},{7,8},{8,9},{9,10},{10,1... | collective-permute-start | bytes 786440 | tf_op jit(solution)/shard_map/ppermute | solution.py:366
  15.0 24.0 %collective-permute-start.9 = (bf16[2,2,16,16,128]{4,3,2,1,0:T(8,128)(2,1)}, bf16[2,2,16,16,128]{4,3,2,1,0:T(8,128)(2,1)S(1)}, u32[]{:S(2)}, u32[]{:S(2)}) collective-permute-start(bf16[2,2,16,16,128]{4,3,2,1,0:T(8,128)(2,1)} %get-tuple-element.12), channel_id=1, source_target_pairs={{1,0},{2,1},{3,2},{4,3},{5,4},{6,5},{7,6},{8,7},{9,8},{10,9},{11,1... | collective-permute-start | bytes 786440 | tf_op jit(solution)/shard_map/ppermute | solution.py:367
  21.6 17.5 %collective-permute-start.4 = (bf16[2,2,16,16,128]{4,3,2,1,0:T(8,128)(2,1)}, bf16[2,2,16,16,128]{4,3,2,1,0:T(8,128)(2,1)S(1)}, u32[]{:S(2)}, u32[]{:S(2)}) collective-permute-start(bf16[2,2,16,16,128]{4,3,2,1,0:T(8,128)(2,1)} %get-tuple-element.11), channel_id=1, source_target_pairs={{0,1},{1,2},{2,3},{3,4},{4,5},{5,6},{6,7},{7,8},{8,9},{9,10},{10,1... | collective-permute-start | bytes 786440 | tf_op jit(solution)/shard_map/ppermute | solution.py:366
  21.6 24.8 %collective-permute-start.5 = (bf16[2,2,16,16,128]{4,3,2,1,0:T(8,128)(2,1)}, bf16[2,2,16,16,128]{4,3,2,1,0:T(8,128)(2,1)S(1)}, u32[]{:S(2)}, u32[]{:S(2)}) collective-permute-start(bf16[2,2,16,16,128]{4,3,2,1,0:T(8,128)(2,1)} %get-tuple-element.11), channel_id=1, source_target_pairs={{1,0},{2,1},{3,2},{4,3},{5,4},{6,5},{7,6},{8,7},{9,8},{10,9},{11,1... | collective-permute-start | bytes 786440 | tf_op jit(solution)/shard_map/ppermute | solution.py:367
  28.8 17.7 %collective-permute-start = (bf16[2,2,16,16,128]{4,3,2,1,0:T(8,128)(2,1)S(1)}, bf16[2,2,16,16,128]{4,3,2,1,0:T(8,128)(2,1)S(1)}, u32[]{:S(2)}, u32[]{:S(2)}) collective-permute-start(bf16[2,2,16,16,128]{4,3,2,1,0:T(8,128)(2,1)S(1)} %get-tuple-element.10), channel_id=1, source_target_pairs={{0,1},{1,2},{2,3},{3,4},{4,5},{5,6},{6,7},{7,8},{8,9},{9,10},{10,1... | collective-permute-start | bytes 786440 | tf_op jit(solution)/shard_map/ppermute | solution.py:366
  28.9 1.1 %copy-start.2 = (bf16[1,6,128,512]{3,2,1,0:T(8,128)(2,1)S(1)}, bf16[1,6,128,512]{3,2,1,0:T(8,128)(2,1)}, u32[]{:S(2)}) copy-start(bf16[1,6,128,512]{3,2,1,0:T(8,128)(2,1)} %param.8) | copy-start | bytes 2359300
  30.0 31.1 %copy-start = (bf16[256,512]{1,0:T(8,128)(2,1)S(1)}, bf16[256,512]{1,0:T(8,128)(2,1)}, u32[]{:S(2)}) copy-start(bf16[256,512]{1,0:T(8,128)(2,1)} %constant.13.taps) | copy-start | bytes 786436
  31.8 22.0 %collective-permute-start.1 = (bf16[2,2,16,16,128]{4,3,2,1,0:T(8,128)(2,1)S(1)}, bf16[2,2,16,16,128]{4,3,2,1,0:T(8,128)(2,1)S(1)}, u32[]{:S(2)}, u32[]{:S(2)}) collective-permute-start(bf16[2,2,16,16,128]{4,3,2,1,0:T(8,128)(2,1)S(1)} %get-tuple-element.10), channel_id=1, source_target_pairs={{1,0},{2,1},{3,2},{4,3},{5,4},{6,5},{7,6},{8,7},{9,8},{10,9},{11,1... | collective-permute-start | bytes 786440 | tf_op jit(solution)/shard_map/ppermute | solution.py:367
  39.0 14.9 %collective-permute-start.10 = (bf16[2,16,16,128]{3,2,1,0:T(8,128)(2,1)S(1)}, bf16[2,16,16,128]{3,2,1,0:T(8,128)(2,1)S(1)}, u32[]{:S(2)}, u32[]{:S(2)}) collective-permute-start(bf16[2,16,16,128]{3,2,1,0:T(8,128)(2,1)S(1)} %slice_bitcast_fusion.1), channel_id=1, source_target_pairs={{0,1},{1,2},{2,3},{3,4},{4,5},{5,6},{6,7},{7,8},{8,9},{9,10},{10,1... | collective-permute-start | bytes 393224 | tf_op jit(solution)/shard_map/ppermute | solution.py:368
  39.2 22.0 %collective-permute-start.11 = (bf16[2,16,16,128]{3,2,1,0:T(8,128)(2,1)S(1)}, bf16[2,16,16,128]{3,2,1,0:T(8,128)(2,1)S(1)}, u32[]{:S(2)}, u32[]{:S(2)}) collective-permute-start(bf16[2,16,16,128]{3,2,1,0:T(8,128)(2,1)S(1)} %slice_bitcast_fusion), channel_id=1, source_target_pairs={{1,0},{2,1},{3,2},{4,3},{5,4},{6,5},{7,6},{8,7},{9,8},{10,9},{11,1... | collective-permute-start | bytes 393224 | tf_op jit(solution)/shard_map/ppermute | solution.py:369
  46.4 18.4 %collective-permute-start.6 = (bf16[2,16,16,128]{3,2,1,0:T(8,128)(2,1)S(1)}, bf16[2,16,16,128]{3,2,1,0:T(8,128)(2,1)S(1)}, u32[]{:S(2)}, u32[]{:S(2)}) collective-permute-start(bf16[2,16,16,128]{3,2,1,0:T(8,128)(2,1)S(1)} %slice_bitcast_fusion.3), channel_id=1, source_target_pairs={{0,1},{1,2},{2,3},{3,4},{4,5},{5,6},{6,7},{7,8},{8,9},{9,10},{10,1... | collective-permute-start | bytes 393224 | tf_op jit(solution)/shard_map/ppermute | solution.py:368
  46.5 18.3 %collective-permute-start.7 = (bf16[2,16,16,128]{3,2,1,0:T(8,128)(2,1)S(1)}, bf16[2,16,16,128]{3,2,1,0:T(8,128)(2,1)S(1)}, u32[]{:S(2)}, u32[]{:S(2)}) collective-permute-start(bf16[2,16,16,128]{3,2,1,0:T(8,128)(2,1)S(1)} %slice_bitcast_fusion.2), channel_id=1, source_target_pairs={{1,0},{2,1},{3,2},{4,3},{5,4},{6,5},{7,6},{8,7},{9,8},{10,9},{11,1... | collective-permute-start | bytes 393224 | tf_op jit(solution)/shard_map/ppermute | solution.py:369
  53.8 14.8 %collective-permute-start.2 = (bf16[2,16,16,128]{3,2,1,0:T(8,128)(2,1)S(1)}, bf16[2,16,16,128]{3,2,1,0:T(8,128)(2,1)S(1)}, u32[]{:S(2)}, u32[]{:S(2)}) collective-permute-start(bf16[2,16,16,128]{3,2,1,0:T(8,128)(2,1)S(1)} %slice_bitcast_fusion.5), channel_id=1, source_target_pairs={{0,1},{1,2},{2,3},{3,4},{4,5},{5,6},{6,7},{7,8},{8,9},{9,10},{10,1... | collective-permute-start | bytes 393224 | tf_op jit(solution)/shard_map/ppermute | solution.py:368
  53.9 14.7 %collective-permute-start.3 = (bf16[2,16,16,128]{3,2,1,0:T(8,128)(2,1)S(1)}, bf16[2,16,16,128]{3,2,1,0:T(8,128)(2,1)S(1)}, u32[]{:S(2)}, u32[]{:S(2)}) collective-permute-start(bf16[2,16,16,128]{3,2,1,0:T(8,128)(2,1)S(1)} %slice_bitcast_fusion.4), channel_id=1, source_target_pairs={{1,0},{2,1},{3,2},{4,3},{5,4},{6,5},{7,6},{8,7},{9,8},{10,9},{11,1... | collective-permute-start | bytes 393224 | tf_op jit(solution)/shard_map/ppermute | solution.py:369
  68.6 3.7 %copy-start.6 = (s32[1,128,512]{2,1,0:T(8,128)S(1)}, s32[1,128,512]{2,1,0:T(8,128)}, u32[]{:S(2)}) copy-start(s32[1,128,512]{2,1,0:T(8,128)} %param.6) | copy-start | bytes 786436

commit v4 on v3

--- a/solution.py
+++ b/solution.py
@@ -1,3 +1,5 @@
+import functools
+
 import jax
 import jax.numpy as jnp
 import numpy as np
@@ -6,15 +8,18 @@
 from jax.experimental.pallas import tpu as pltpu
 from jax.sharding import PartitionSpec as P
 
+
 SPECIES = 6
 ROWS = 8
 COLS = 16
 HALVES = 16
 LANES = 128
 SLOTS = 512
-CHUNKS = 3
-PER = SPECIES // CHUNKS
+SIZES = (4, 2)
+STARTS = (0, 4)
 GROUP = 8
+WIDE = COLS + 1
+SLOT = GROUP + 1
 MIB = 1 << 20
 
 raw_taps = (0.1353352832366127, 0.6065306597126334, 1.0)
@@ -56,9 +61,9 @@
     return limit
 
 
-def deposit_kernel(counts, cells_far, species_far, mix_far, own, sent0, sent1, sent2,
-                   cells, species, mix, w_s, d_s, sems):
-    sent = (sent0, sent1, sent2)
+def deposit_kernel(counts, cells_far, species_far, mix_far, own_far, sent0_far, sent1_far,
+                   cells, species, mix, own, sent0, sent1, w_s, d_s, sems, out_sems):
+    sent = [(sent0, k) for k in range(SIZES[0])] + [(sent1, k) for k in range(SIZES[1])]
 
     def fetches(r):
         rows = pl.ds(pl.multiple_of(r * COLS, COLS), COLS)
@@ -68,14 +73,21 @@
             pltpu.make_async_copy(mix_far.at[:, rows], mix.at[:, rows], sems.at[2, r]),
         )
 
+    def results(r):
+        part = pl.ds(2 * r, 2)
+        return [
+            pltpu.make_async_copy(near.at[:, :, part], far.at[:, :, part], out_sems.at[i, r])
+            for i, (near, far) in enumerate(((sent0, sent0_far), (sent1, sent1_far), (own, own_far)))
+        ]
+
     for r in range(ROWS):
         for copy in fetches(r):
             copy.start()
     zero = jnp.zeros((COLS, LANES), f32)
     for t in range(4):
         for k in (6, 7):
-            w_s[t, k * COLS:(k + 1) * COLS] = zero
-            w_s[t, (8 + k) * COLS:(9 + k) * COLS] = zero
+            w_s[t, k * WIDE:k * WIDE + COLS] = zero
+            w_s[t, (8 + k) * WIDE:(8 + k) * WIDE + COLS] = zero
 
     def one_row(r, carry):
         for copy in fetches(r):
@@ -86,27 +98,32 @@
         for t in range(4):
             upper = (cells[rows, pl.ds(t * LANES, LANES)] & 1) == 1
             for k, w in enumerate(weights_of(limit, t, rows, species, mix)):
-                w_s[t, k * COLS:(k + 1) * COLS] = jnp.where(upper, 0.0, w)
-                w_s[t, (8 + k) * COLS:(9 + k) * COLS] = jnp.where(upper, w, 0.0)
+                w_s[t, k * WIDE:k * WIDE + COLS] = jnp.where(upper, 0.0, w)
+                w_s[t, (8 + k) * WIDE:(8 + k) * WIDE + COLS] = jnp.where(upper, w, 0.0)
         for b in range(COLS):
             plane = cells[pl.ds(first + b, 1), :] >> 8
             table = onehot_of(plane & 127, 8)
-            w = jnp.concatenate([w_s[t, pl.ds(b, 16, stride=COLS)] for t in range(4)], axis=1).astype(bf16)
+            w = jnp.concatenate([w_s[t, pl.ds(b, 16, stride=WIDE)] for t in range(4)], axis=1).astype(bf16)
             second = jnp.broadcast_to(plane >> 7, (16, SLOTS)).astype(f32).astype(bf16) > 0.5
             none = jnp.zeros((16, SLOTS), bf16)
             halves = jnp.concatenate([jnp.where(second, none, w), jnp.where(second, w, none)], axis=0)
             dens = lax.dot_general(halves, table, (((1,), (1,)), ((), ())), preferred_element_type=f32)
-            d_s[0, pl.ds(b, 16, stride=COLS)] = dens[:16]
-            d_s[1, pl.ds(b, 16, stride=COLS)] = dens[16:]
+            d_s[0, pl.ds(b, 16, stride=WIDE)] = dens[:16]
+            d_s[1, pl.ds(b, 16, stride=WIDE)] = dens[16:]
         for z in range(2):
             for k in range(SPECIES):
                 for h in range(2):
-                    value = d_s[h, (z * 8 + k) * COLS:(z * 8 + k + 1) * COLS]
+                    value = d_s[h, (z * 8 + k) * WIDE:(z * 8 + k) * WIDE + COLS]
                     own[z, k, 2 * r + h] = value
-                    sent[k // PER][z, k % PER, 2 * r + h] = value.astype(bf16)
+                    sent[k][0][z, sent[k][1], 2 * r + h] = value.astype(bf16)
+        for copy in results(r):
+            copy.start()
         return carry
 
     lax.fori_loop(0, ROWS, one_row, 0)
+    for r in range(ROWS):
+        for copy in results(r):
+            copy.wait()
 
 
 VM = pltpu.MemorySpace.VMEM
@@ -118,19 +135,23 @@
     return pl.pallas_call(
         deposit_kernel,
         name="deposit",
-        in_specs=[pl.BlockSpec(memory_space=SM)] + [pl.BlockSpec(memory_space=pl.ANY)] * 3,
-        out_specs=[pl.BlockSpec(memory_space=VM)] * 4,
+        in_specs=[pl.BlockSpec(memory_space=SM)] + [pl.BlockSpec(memory_space=pltpu.MemorySpace.HBM)] * 3,
+        out_specs=[pl.BlockSpec(memory_space=pltpu.MemorySpace.HBM)] * 3,
         scratch_shapes=[
             pltpu.VMEM((ROWS * COLS, SLOTS), jnp.int32),
             pltpu.VMEM((ROWS * COLS, SLOTS), jnp.int32),
             pltpu.VMEM((SPECIES, ROWS * COLS, SLOTS), bf16),
-            pltpu.VMEM((4, 16 * COLS, LANES), f32),
-            pltpu.VMEM((2, 16 * COLS, LANES), f32),
+            pltpu.VMEM((2, SPECIES) + half, f32),
+            pltpu.VMEM((2, SIZES[0]) + half, bf16),
+            pltpu.VMEM((2, SIZES[1]) + half, bf16),
+            pltpu.VMEM((4, 16 * WIDE, LANES), f32),
+            pltpu.VMEM((2, 16 * WIDE, LANES), f32),
+            pltpu.SemaphoreType.DMA((3, ROWS)),
             pltpu.SemaphoreType.DMA((3, ROWS)),
         ],
         out_shape=[jax.ShapeDtypeStruct((2, SPECIES) + half, f32)]
-        + [jax.ShapeDtypeStruct((2, PER) + half, bf16)] * CHUNKS,
-        compiler_params=pltpu.CompilerParams(vmem_limit_bytes=16 * MIB),
+        + [jax.ShapeDtypeStruct((2, size) + half, bf16) for size in SIZES],
+        compiler_params=pltpu.CompilerParams(vmem_limit_bytes=60 * MIB),
         cost_estimate=pl.CostEstimate(flops=10**9, bytes_accessed=5 * 10**6, transcendentals=0),
     )(counts, cells, species, mix)
 
@@ -201,21 +222,23 @@
     return top, (v - top.astype(f32)).astype(bf16)
 
 
-def smooth_kernel(taps, own, near_low, near_high, far_low, far_high, ready, x_s, y_s, w_s, g_s):
+def smooth_kernel(size, even_ref, taps, own, near_a, near_b, far_a, far_b, ready, x_s, y_s, w_s, g_s):
     k = pl.program_id(0)
     lane = lax.broadcasted_iota(jnp.int32, (COLS, LANES), 1)
     col = lane & 15
     cu = 1.0 / (SMOOTH_SCALE * SLOPE_SCALE)
     cz = 0.5 / (SMOOTH_SCALE * SMOOTH_SCALE)
+    even = jnp.full((COLS, LANES), even_ref[0], jnp.int32) == 1
     for h in range(HALVES):
-        l2 = far_low[0, h].astype(f32)
-        a = near_low[0, 0, h].astype(f32)
-        b = near_low[1, 0, h].astype(f32)
+        def sides(a, b):
+            a, b = a.astype(f32), b.astype(f32)
+            return jnp.where(even, b, a), jnp.where(even, a, b)
+
+        l2, r2 = sides(far_a[0, h], far_b[0, h])
+        a, r0 = sides(near_a[0, 0, h], near_b[0, 0, h])
+        b, r1 = sides(near_a[1, 0, h], near_b[1, 0, h])
         o0 = own[0, 0, h]
         o1 = own[1, 0, h]
-        r0 = near_high[0, 0, h].astype(f32)
-        r1 = near_high[1, 0, h].astype(f32)
-        r2 = far_high[0, h].astype(f32)
         um = T2 * (l2 + o1) + T1 * (a + o0) + T0 * b
         u0 = T2 * (a + r0) + T1 * (b + o1) + T0 * o0
         u1 = T2 * (b + r1) + T1 * (o0 + r0) + T0 * o1
@@ -254,68 +277,71 @@
             w_s[1, p], table, preferred_element_type=f32
         )
         for h in range(HALVES):
-            g_s[h, pl.ds(pl.multiple_of((k * 8 + p) * COLS, COLS), COLS)] = out[h * COLS:(h + 1) * COLS]
+            g_s[h, pl.ds((k * 8 + p) * WIDE, COLS)] = out[h * COLS:(h + 1) * COLS]
 
     @pl.when(k == 0)
     def _():
-        zero = jnp.zeros((HALVES, 2 * COLS, LANES), f32)
-        for i in range(PER):
-            g_s[:, (i * 8 + 6) * COLS:(i * 8 + 8) * COLS] = zero
-
-    @pl.when(k == PER - 1)
+        zero = jnp.zeros((HALVES, 2 * WIDE, LANES), f32)
+        for i in range(size):
+            g_s[:, (i * 8 + 6) * WIDE:(i * 8 + 8) * WIDE] = zero
+
+    @pl.when(k == size - 1)
     def _():
         def one_row(r, carry):
             for q in range(COLS):
                 for h in range(2):
-                    top, rest = split(g_s[2 * r + h, pl.ds(q, 16, stride=COLS)])
-                    ready[r * COLS + q, :16, h * LANES:(h + 1) * LANES] = top
-                    ready[r * COLS + q, 16:, h * LANES:(h + 1) * LANES] = rest
+                    top, rest = split(g_s[2 * r + h, pl.ds(q, 8 * size, stride=WIDE)])
+                    ready[r * COLS + q, :8 * size, h * LANES:(h + 1) * LANES] = top
+                    ready[r * COLS + q, 8 * size:, h * LANES:(h + 1) * LANES] = rest
             return carry
 
         lax.fori_loop(0, ROWS, one_row, 0)
 
 
-def smooth(chunk, taps, own, near_low, near_high, far_low, far_high):
+def smooth(chunk, even, taps, own, near_a, near_b, far_a, far_b):
+    size, start = SIZES[chunk], STARTS[chunk]
     half = (HALVES, COLS, LANES)
     two = pl.BlockSpec((2, 1) + half, lambda k: (0, k, 0, 0, 0))
     one = pl.BlockSpec((1,) + half, lambda k: (k, 0, 0, 0))
     return pl.pallas_call(
-        smooth_kernel,
+        functools.partial(smooth_kernel, size),
         name="smooth",
-        grid=(PER,),
+        grid=(size,),
         in_specs=[
+            pl.BlockSpec(memory_space=SM),
             pl.BlockSpec((2 * LANES, 4 * LANES), lambda k: (0, 0)),
-            pl.BlockSpec((2, 1) + half, lambda k: (0, chunk * PER + k, 0, 0, 0)),
+            pl.BlockSpec((2, 1) + half, lambda k: (0, start + k, 0, 0, 0)),
             two,
             two,
             one,
             one,
         ],
-        out_specs=pl.BlockSpec((ROWS * COLS, 32, 2 * LANES), lambda k: (0, 0, 0)),
-        out_shape=jax.ShapeDtypeStruct((ROWS * COLS, 32, 2 * LANES), bf16),
+        out_specs=pl.BlockSpec((ROWS * COLS, 16 * size, 2 * LANES), lambda k: (0, 0, 0)),
+        out_shape=jax.ShapeDtypeStruct((ROWS * COLS, 16 * size, 2 * LANES), bf16),
         scratch_shapes=[
             pltpu.VMEM((2, 4, HALVES * COLS, 2 * LANES), bf16),
             pltpu.VMEM((6, HALVES * COLS, LANES), f32),
             pltpu.VMEM((2, 6, HALVES * COLS, 2 * LANES), bf16),
-            pltpu.VMEM((HALVES, PER * 8 * COLS, LANES), f32),
+            pltpu.VMEM((HALVES, size * 8 * WIDE, LANES), f32),
         ],
         compiler_params=pltpu.CompilerParams(vmem_limit_bytes=24 * MIB),
         cost_estimate=pl.CostEstimate(flops=10**9, bytes_accessed=4 * 10**6, transcendentals=0),
-    )(taps, own, near_low, near_high, far_low, far_high)
-
-
-def pick_kernel(cells, ready0, ready1, ready2, mixed, forces, got_s):
+    )(even, taps, own, near_a, near_b, far_a, far_b)
+
+
+def pick_kernel(cells, ready0, ready1, mixed, forces, got_s):
     def one_group(g, slot):
         first = pl.multiple_of(g * GROUP, GROUP)
         for b in range(GROUP):
             d = first + b
             table = onehot_of(cells[pl.ds(d, 1), :] >> 8, 16)
-            parts = [ready[d] for ready in (ready0, ready1, ready2)]
-            rows = jnp.concatenate([p[:16] for p in parts] + [p[16:] for p in parts], axis=0)
+            rows = jnp.concatenate(
+                [ready0[d, :32], ready1[d, :16], ready0[d, 32:], ready1[d, 16:]], axis=0
+            )
             got = jnp.dot(rows, table, preferred_element_type=f32)
             got = got[:48] + got[48:]
             for t in range(4):
-                got_s[slot, t, pl.ds(b, 48, stride=GROUP)] = got[:, t * LANES:(t + 1) * LANES]
+                got_s[slot, t, pl.ds(b, 48, stride=SLOT)] = got[:, t * LANES:(t + 1) * LANES]
         for t in range(4):
             lanes = slice(t * LANES, (t + 1) * LANES)
             upper = (cells[pl.ds(first, GROUP), lanes] & 1) == 1
@@ -323,29 +349,29 @@
             for a in range(3):
                 total = None
                 for k in range(SPECIES):
-                    row = ((k // PER) * 16 + (k % PER) * 8 + 2 * a) * GROUP
+                    row = (k * 8 + 2 * a) * SLOT
                     value = jnp.where(
-                        upper, got_s[slot, t, row + GROUP:row + 2 * GROUP], got_s[slot, t, row:row + GROUP]
+                        upper, got_s[slot, t, row + SLOT:row + SLOT + GROUP], got_s[slot, t, row:row + GROUP]
                     )
                     total = vs[k] * value if total is None else total + vs[k] * value
                 forces[a, pl.ds(first, GROUP), lanes] = total
 
-    def two_groups(i, carry):
-        one_group(2 * i, 0)
-        one_group(2 * i + 1, 1)
+    def four_groups(i, carry):
+        for j in range(4):
+            one_group(4 * i + j, j)
         return carry
 
-    lax.fori_loop(0, ROWS * COLS // GROUP // 2, two_groups, 0)
+    lax.fori_loop(0, ROWS * COLS // GROUP // 4, four_groups, 0)
 
 
 def pick(cells, ready, mixed):
     return pl.pallas_call(
         pick_kernel,
         name="pick",
-        in_specs=[pl.BlockSpec(memory_space=VM)] * 5,
+        in_specs=[pl.BlockSpec(memory_space=VM)] * 4,
         out_specs=pl.BlockSpec(memory_space=VM),
         out_shape=jax.ShapeDtypeStruct((3, ROWS * COLS, SLOTS), f32),
-        scratch_shapes=[pltpu.VMEM((2, 4, 48 * GROUP, LANES), f32)],
+        scratch_shapes=[pltpu.VMEM((4, 4, 48 * SLOT, LANES), f32)],
         compiler_params=pltpu.CompilerParams(vmem_limit_bytes=24 * MIB),
         cost_estimate=pl.CostEstimate(flops=6 * 10**9, bytes_accessed=10**7, transcendentals=0),
     )(cells, *ready, mixed)
@@ -354,20 +380,25 @@
 def body(send_cells, send_species, send_mix, send_counts, chi):
     axes = ("row", "col")
     count = lax.axis_size("row") * lax.axis_size("col")
-    up = [(i, (i + 1) % count) for i in range(count)]
-    down = [(j, i) for i, j in up]
+    swap_a = [(i, i ^ 1) for i in range(count)]
+    swap_b = [(i, (i + (1 if i % 2 else -1)) % count) for i in range(count)]
+    odd = lax.axis_index("col") % 2
+    even = (1 - odd).reshape(1)
     chis = 0.5 * (chi + chi.T) * (1.0 - jnp.eye(SPECIES, dtype=f32))
     mix_matrix = -0.5 * (chis + 1.0)
     cells, species, mix, counts = send_cells[0], send_species[0], send_mix[0], send_counts[0]
     own, *sent = deposit(counts, cells, species, mix)
     taps = tap_matrices()
     ready = []
-    for chunk in range(CHUNKS):
-        near_low = lax.ppermute(sent[chunk], axes, up)
-        near_high = lax.ppermute(sent[chunk], axes, down)
-        far_low = lax.ppermute(near_low[1], axes, up)
-        far_high = lax.ppermute(near_high[0], axes, down)
-        ready.append(smooth(chunk, taps, own, near_low, near_high, far_low, far_high))
+    for chunk in range(len(SIZES)):
+        def swap(value, pairs):
+            return lax.ppermute(value, axes, pairs)
+
+        near_a = swap(sent[chunk], swap_a)
+        near_b = swap(sent[chunk], swap_b)
+        far_a = swap(lax.dynamic_index_in_dim(near_b, 1 - odd, 0, False), swap_a)
+        far_b = swap(lax.dynamic_index_in_dim(near_a, odd, 0, False), swap_b)
+        ready.append(smooth(chunk, even, taps, own, near_a, near_b, far_a, far_b))
     mixed = mixing(counts, mix_matrix, species, mix)
     return pick(cells, ready, mixed)[None]
 

time: 81.4 us -> 69 us (0.85)
  starting transfers between devices: 44.7 us -> 19.7 us
  waiting for transfers between devices: 0.03 us -> 20.7 us
  local copies, waits for them, and re-layouts: 5.02 us -> 0.19 us
  Pallas kernels: 31.2 us -> 28.2 us
    ppermute x12 -> x8, starting transfers between devices: 44.7 us -> 19.7 us  [swap(): return lax.ppermute(value, axes, pairs)]
    ppermute x12 -> x8, waiting for transfers between devices: 0.03 us -> 20.7 us  [swap(): return lax.ppermute(value, axes, pairs)]
    unnamed x21 -> x15, local copies, waits for them, and re-layouts: 4.96 us -> 0.12 us
    pallas_call x1, Pallas kernels: 8.91 us -> 7.08 us  [pick(): pl.pallas_call(pick_kernel, name='pick', in_specs=[pl.BlockSpec(memory_sp...]
    pallas_call x3 -> x2, Pallas kernels: 11.1 us -> 9.7 us  [smooth(): pl.pallas_call(functools.partial(smooth_kernel, size), name='smooth', gri...]
  transfers between devices with their start and end apart: 12 -> 8, of which waited for: 0 -> 5; matrix products, arithmetic and copies ran while one was open for 0% -> 0% of each run, Pallas kernels for 11% -> 7%
where the time goes in v4:
time: 69 us; the launch traced here: 68.9 us
  Pallas kernels  28.2 us (41%)
  waiting for transfers between devices  20.7 us (30%)
  starting transfers between devices  19.7 us (29%)
    ppermute x8, waiting for transfers between devices, swap(): return lax.ppermute(value, axes, pairs)  20.7 us
    ppermute x8, starting transfers between devices, swap(): return lax.ppermute(value, axes, pairs)  19.7 us
    pallas_call x1, Pallas kernels, deposit(): pl.pallas_call(deposit_kernel, name='deposit', in_specs=[pl.BlockSpec(mem...  9.73 us
    pallas_call x2, Pallas kernels, smooth(): pl.pallas_call(functools.partial(smooth_kernel, size), name='smooth', gri...  9.7 us
    pallas_call x1, Pallas kernels, pick(): pl.pallas_call(pick_kernel, name='pick', in_specs=[pl.BlockSpec(memory_sp...  7.08 us
    pallas_call x1, Pallas kernels, mixing(): pl.pallas_call(mixing_kernel, name='mixing', in_specs=[pl.BlockSpec(memor...  1.7 us
  transfers between devices with their start and end apart: 8, of which 5 were waited for; matrix products, arithmetic and copies ran while one was open for 0% of the time, Pallas kernels for 7%

profile of v4, /device:TPU:0, one launch (start us, length us, event | category | flops | bytes accessed | tf_op | source)
XLA Modules:
  0.0 68.9 jit_solution(13217091516658272476)
XLA Ops:
  0.0 0.0 copy-start.6
  0.0 0.0 copy-start.2
  0.0 0.0 copy-start.3
  0.0 0.0 copy-start.5
  0.0 9.7 %deposit.1 = (f32[2,6,16,16,128]{4,3,2,1,0:T(8,128)}, bf16[2,4,16,16,128]{4,3,2,1,0:T(8,128)(2,1)}, bf16[2,2,16,16,128]{4,3,2,1,0:T(8,128)(2,1)}) custom-call(s32[128]{0:T(128)} %bitcast.30, s32[128,512]{1,0:T(8,128)} %bitcast.28, s32[128,512]{1,0:T(8,128)} %bitcast.26, bf16[6,128,512]{2,1,0:T(8,128)(2,1)} %bitcast.24), custom_call_target="tpu_custom_call" | custom-call | flops 1000000000 | bytes 5000000 | tf_op jit(solution)/shard_map/deposit/pallas_call | solution.py:135
  9.7 8.3 %collective-permute-start.1 = (bf16[2,4,16,16,128]{4,3,2,1,0:T(8,128)(2,1)}, bf16[2,4,16,16,128]{4,3,2,1,0:T(8,128)(2,1)S(1)}, u32[]{:S(2)}, u32[]{:S(2)}) collective-permute-start(bf16[2,4,16,16,128]{4,3,2,1,0:T(8,128)(2,1)} %get-tuple-element.9), channel_id=1, source_target_pairs={{0,127},{1,2},{2,1},{3,4},{4,3},{5,6},{6,5},{7,8},{8,7},{9,10},{10... | collective-permute-start | bytes 1572872 | tf_op jit(solution)/shard_map/ppermute | solution.py:395
  18.1 0.1 collective-permute-start.5
  18.2 0.0 collective-permute-start
  18.2 2.0 %collective-permute-start.4 = (bf16[2,2,16,16,128]{4,3,2,1,0:T(8,128)(2,1)}, bf16[2,2,16,16,128]{4,3,2,1,0:T(8,128)(2,1)S(1)}, u32[]{:S(2)}, u32[]{:S(2)}) collective-permute-start(bf16[2,2,16,16,128]{4,3,2,1,0:T(8,128)(2,1)} %get-tuple-element.10), channel_id=1, source_target_pairs={{0,1},{1,0},{2,3},{3,2},{4,5},{5,4},{6,7},{7,6},{8,9},{9,8},{10,11... | collective-permute-start | bytes 786440 | tf_op jit(solution)/shard_map/ppermute | solution.py:395
  20.2 0.0 copy-done.6
  20.2 0.1 copy.7
  20.3 9.3 %collective-permute-done.5.near_b = bf16[2,2,16,16,128]{4,3,2,1,0:T(8,128)(2,1)S(1)} collective-permute-done((bf16[2,2,16,16,128]{4,3,2,1,0:T(8,128)(2,1)}, bf16[2,2,16,16,128]{4,3,2,1,0:T(8,128)(2,1)S(1)}, u32[]{:S(2)}, u32[]{:S(2)}) %collective-permute-start.5) | collective-permute-done | bytes 262176 | tf_op jit(solution)/shard_map/ppermute | solution.py:395
  29.6 1.5 %collective-permute-start.6 = (bf16[2,16,16,128]{3,2,1,0:T(8,128)(2,1)S(1)}, bf16[2,16,16,128]{3,2,1,0:T(8,128)(2,1)S(1)}, u32[]{:S(2)}, u32[]{:S(2)}) collective-permute-start(bf16[2,16,16,128]{3,2,1,0:T(8,128)(2,1)S(1)} %dynamic-slice_bitcast_fusion.3), channel_id=1, source_target_pairs={{0,1},{1,0},{2,3},{3,2},{4,5},{5,4},{6,7},{7,6},{8,9},{9,8},{10,11... | collective-permute-start | bytes 393224 | tf_op jit(solution)/shard_map/ppermute | solution.py:395
  31.1 5.2 %collective-permute-done.4.near_a = bf16[2,2,16,16,128]{4,3,2,1,0:T(8,128)(2,1)S(1)} collective-permute-done((bf16[2,2,16,16,128]{4,3,2,1,0:T(8,128)(2,1)}, bf16[2,2,16,16,128]{4,3,2,1,0:T(8,128)(2,1)S(1)}, u32[]{:S(2)}, u32[]{:S(2)}) %collective-permute-start.4) | collective-permute-done | bytes 262176 | tf_op jit(solution)/shard_map/ppermute | solution.py:395
  36.3 7.5 %collective-permute-start.7 = (bf16[2,16,16,128]{3,2,1,0:T(8,128)(2,1)S(1)}, bf16[2,16,16,128]{3,2,1,0:T(8,128)(2,1)S(1)}, u32[]{:S(2)}, u32[]{:S(2)}) collective-permute-start(bf16[2,16,16,128]{3,2,1,0:T(8,128)(2,1)S(1)} %dynamic-slice_bitcast_fusion.2), channel_id=1, source_target_pairs={{0,127},{1,2},{2,1},{3,4},{4,3},{5,6},{6,5},{7,8},{8,7},{9,10},{10... | collective-permute-start | bytes 393224 | tf_op jit(solution)/shard_map/ppermute | solution.py:395
  43.8 0.0 collective-permute-done.1.near_b
  43.9 0.0 copy-start
  43.9 0.0 copy-start.1
  43.9 0.1 collective-permute-start.2
  44.0 0.0 collective-permute-done.near_a
  44.0 0.1 collective-permute-start.3
  44.2 0.0 copy-done.2
  44.2 0.0 copy-done.3
  44.2 0.0 copy-done.5
  44.2 1.7 %mixing.1.mixed = f32[6,128,512]{2,1,0:T(8,128)S(1)} custom-call(s32[128]{0:T(128)S(1)} %bitcast.31, f32[6,6]{1,0:T(8,128)S(1)} %fusion.3.mix_matrix, s32[128,512]{1,0:T(8,128)S(1)} %bitcast.27, bf16[6,128,512]{2,1,0:T(8,128)(2,1)S(1)} %bitcast.25), custom_call_target="tpu_custom_call" | custom-call | flops 1000000000 | bytes 4000000 | tf_op jit(solution)/shard_map/mixing/pallas_call | solution.py:177
  45.9 0.0 collective-permute-done.6.far_a
  45.9 0.7 collective-permute-done.7.far_b
  46.6 0.0 copy-done
  46.6 0.0 copy-done.1
  46.6 3.3 %smooth.3.ready1 = bf16[128,32,256]{2,1,0:T(8,128)(2,1)S(1)} custom-call(s32[1]{0:T(128)} %bitcast.1.even_ref, bf16[256,512]{1,0:T(8,128)(2,1)S(1)} %copy-done.1, f32[2,6,16,16,128]{4,3,2,1,0:T(8,128)S(1)} %copy-done, bf16[2,2,16,16,128]{4,3,2,1,0:T(8,128)(2,1)S(1)} %collective-permute-done.4.near_a, ...), custom_call_target="tpu_custom_call" | custom-call | flops 1000000000 | bytes 4000000 | tf_op jit(solution)/shard_map/smooth/pallas_call | solution.py:306
  49.8 0.0 copy-start.4
  49.8 0.8 %collective-permute-done.2.far_a = bf16[4,16,16,128]{3,2,1,0:T(8,128)(2,1)S(1)} collective-permute-done((bf16[4,16,16,128]{3,2,1,0:T(8,128)(2,1)S(1)}, bf16[4,16,16,128]{3,2,1,0:T(8,128)(2,1)S(1)}, u32[]{:S(2)}, u32[]{:S(2)}) %collective-permute-start.2) | collective-permute-done | bytes 262176 | tf_op jit(solution)/shard_map/ppermute | solution.py:395
  50.7 4.7 %collective-permute-done.3.far_b = bf16[4,16,16,128]{3,2,1,0:T(8,128)(2,1)S(1)} collective-permute-done((bf16[4,16,16,128]{3,2,1,0:T(8,128)(2,1)S(1)}, bf16[4,16,16,128]{3,2,1,0:T(8,128)(2,1)S(1)}, u32[]{:S(2)}, u32[]{:S(2)}) %collective-permute-start.3) | collective-permute-done | bytes 262176 | tf_op jit(solution)/shard_map/ppermute | solution.py:395
  55.3 6.5 %smooth.2.ready0 = bf16[128,64,256]{2,1,0:T(8,128)(2,1)S(1)} custom-call(s32[1]{0:T(128)} %bitcast.1.even_ref, bf16[256,512]{1,0:T(8,128)(2,1)S(1)} %copy-done.1, f32[2,6,16,16,128]{4,3,2,1,0:T(8,128)S(1)} %copy-done, bf16[2,4,16,16,128]{4,3,2,1,0:T(8,128)(2,1)S(1)} %collective-permute-done.near_a, ...), custom_call_target="tpu_custom_call" | custom-call | flops 1000000000 | bytes 4000000 | tf_op jit(solution)/shard_map/smooth/pallas_call | solution.py:306
  61.8 0.0 copy-done.4
  61.8 7.1 %pick.1 = f32[3,128,512]{2,1,0:T(8,128)} custom-call(s32[128,512]{1,0:T(8,128)S(1)} %bitcast.29, bf16[128,64,256]{2,1,0:T(8,128)(2,1)S(1)} %smooth.2.ready0, bf16[128,32,256]{2,1,0:T(8,128)(2,1)S(1)} %smooth.3.ready1, f32[6,128,512]{2,1,0:T(8,128)S(1)} %mixing.1.mixed), custom_call_target="tpu_custom_call" | custom-call | flops 6000000000 | bytes 10000000 | tf_op jit(solution)/shard_map/pick/pallas_call | solution.py:368
  (5 shorter events, 0.1 us)
Async XLA Ops:
  0.0 20.2 %copy-start.6 = (f32[6,6]{1,0:T(8,128)S(1)}, f32[6,6]{1,0:T(8,128)}, u32[]{:S(2)}) copy-start(f32[6,6]{1,0:T(8,128)} %param.10) | copy-start | bytes 436
  0.0 44.2 %copy-start.2 = (bf16[1,6,128,512]{3,2,1,0:T(8,128)(2,1)S(1)}, bf16[1,6,128,512]{3,2,1,0:T(8,128)(2,1)}, u32[]{:S(2)}) copy-start(bf16[1,6,128,512]{3,2,1,0:T(8,128)(2,1)} %param.8) | copy-start | bytes 2359300
  0.0 44.2 %copy-start.3 = (s32[1,128,512]{2,1,0:T(8,128)S(1)}, s32[1,128,512]{2,1,0:T(8,128)}, u32[]{:S(2)}) copy-start(s32[1,128,512]{2,1,0:T(8,128)} %param.7) | copy-start | bytes 786436
  0.0 44.2 %copy-start.5 = (s32[1,128]{1,0:T(1,128)S(1)}, s32[1,128]{1,0:T(1,128)}, u32[]{:S(2)}) copy-start(s32[1,128]{1,0:T(1,128)} %param.9) | copy-start | bytes 1540
  9.7 34.1 %collective-permute-start.1 = (bf16[2,4,16,16,128]{4,3,2,1,0:T(8,128)(2,1)}, bf16[2,4,16,16,128]{4,3,2,1,0:T(8,128)(2,1)S(1)}, u32[]{:S(2)}, u32[]{:S(2)}) collective-permute-start(bf16[2,4,16,16,128]{4,3,2,1,0:T(8,128)(2,1)} %get-tuple-element.9), channel_id=1, source_target_pairs={{0,127},{1,2},{2,1},{3,4},{4,3},{5,6},{6,5},{7,8},{8,7},{9,10},{10... | collective-permute-start | bytes 1572872 | tf_op jit(solution)/shard_map/ppermute | solution.py:395
  18.1 11.5 %collective-permute-start.5 = (bf16[2,2,16,16,128]{4,3,2,1,0:T(8,128)(2,1)}, bf16[2,2,16,16,128]{4,3,2,1,0:T(8,128)(2,1)S(1)}, u32[]{:S(2)}, u32[]{:S(2)}) collective-permute-start(bf16[2,2,16,16,128]{4,3,2,1,0:T(8,128)(2,1)} %get-tuple-element.10), channel_id=1, source_target_pairs={{0,127},{1,2},{2,1},{3,4},{4,3},{5,6},{6,5},{7,8},{8,7},{9,10},{10... | collective-permute-start | bytes 786440 | tf_op jit(solution)/shard_map/ppermute | solution.py:395
  18.2 25.8 %collective-permute-start = (bf16[2,4,16,16,128]{4,3,2,1,0:T(8,128)(2,1)}, bf16[2,4,16,16,128]{4,3,2,1,0:T(8,128)(2,1)S(1)}, u32[]{:S(2)}, u32[]{:S(2)}) collective-permute-start(bf16[2,4,16,16,128]{4,3,2,1,0:T(8,128)(2,1)} %get-tuple-element.9), channel_id=1, source_target_pairs={{0,1},{1,0},{2,3},{3,2},{4,5},{5,4},{6,7},{7,6},{8,9},{9,8},{10,11... | collective-permute-start | bytes 1572872 | tf_op jit(solution)/shard_map/ppermute | solution.py:395
  18.2 18.1 %collective-permute-start.4 = (bf16[2,2,16,16,128]{4,3,2,1,0:T(8,128)(2,1)}, bf16[2,2,16,16,128]{4,3,2,1,0:T(8,128)(2,1)S(1)}, u32[]{:S(2)}, u32[]{:S(2)}) collective-permute-start(bf16[2,2,16,16,128]{4,3,2,1,0:T(8,128)(2,1)} %get-tuple-element.10), channel_id=1, source_target_pairs={{0,1},{1,0},{2,3},{3,2},{4,5},{5,4},{6,7},{7,6},{8,9},{9,8},{10,11... | collective-permute-start | bytes 786440 | tf_op jit(solution)/shard_map/ppermute | solution.py:395
  29.6 16.3 %collective-permute-start.6 = (bf16[2,16,16,128]{3,2,1,0:T(8,128)(2,1)S(1)}, bf16[2,16,16,128]{3,2,1,0:T(8,128)(2,1)S(1)}, u32[]{:S(2)}, u32[]{:S(2)}) collective-permute-start(bf16[2,16,16,128]{3,2,1,0:T(8,128)(2,1)S(1)} %dynamic-slice_bitcast_fusion.3), channel_id=1, source_target_pairs={{0,1},{1,0},{2,3},{3,2},{4,5},{5,4},{6,7},{7,6},{8,9},{9,8},{10,11... | collective-permute-start | bytes 393224 | tf_op jit(solution)/shard_map/ppermute | solution.py:395
  36.3 10.3 %collective-permute-start.7 = (bf16[2,16,16,128]{3,2,1,0:T(8,128)(2,1)S(1)}, bf16[2,16,16,128]{3,2,1,0:T(8,128)(2,1)S(1)}, u32[]{:S(2)}, u32[]{:S(2)}) collective-permute-start(bf16[2,16,16,128]{3,2,1,0:T(8,128)(2,1)S(1)} %dynamic-slice_bitcast_fusion.2), channel_id=1, source_target_pairs={{0,127},{1,2},{2,1},{3,4},{4,3},{5,6},{6,5},{7,8},{8,7},{9,10},{10... | collective-permute-start | bytes 393224 | tf_op jit(solution)/shard_map/ppermute | solution.py:395
  43.9 2.7 %copy-start = (f32[2,6,16,16,128]{4,3,2,1,0:T(8,128)S(1)}, f32[2,6,16,16,128]{4,3,2,1,0:T(8,128)}, u32[]{:S(2)}) copy-start(f32[2,6,16,16,128]{4,3,2,1,0:T(8,128)} %get-tuple-element.8.own) | copy-start | bytes 4718596
  43.9 2.7 %copy-start.1 = (bf16[256,512]{1,0:T(8,128)(2,1)S(1)}, bf16[256,512]{1,0:T(8,128)(2,1)}, u32[]{:S(2)}) copy-start(bf16[256,512]{1,0:T(8,128)(2,1)} %constant.45.taps) | copy-start | bytes 786436
  43.9 6.8 %collective-permute-start.2 = (bf16[4,16,16,128]{3,2,1,0:T(8,128)(2,1)S(1)}, bf16[4,16,16,128]{3,2,1,0:T(8,128)(2,1)S(1)}, u32[]{:S(2)}, u32[]{:S(2)}) collective-permute-start(bf16[4,16,16,128]{3,2,1,0:T(8,128)(2,1)S(1)} %dynamic-slice_bitcast_fusion.1), channel_id=1, source_target_pairs={{0,1},{1,0},{2,3},{3,2},{4,5},{5,4},{6,7},{7,6},{8,9},{9,8},{10,11... | collective-permute-start | bytes 786440 | tf_op jit(solution)/shard_map/ppermute | solution.py:395
  44.0 11.3 %collective-permute-start.3 = (bf16[4,16,16,128]{3,2,1,0:T(8,128)(2,1)S(1)}, bf16[4,16,16,128]{3,2,1,0:T(8,128)(2,1)S(1)}, u32[]{:S(2)}, u32[]{:S(2)}) collective-permute-start(bf16[4,16,16,128]{3,2,1,0:T(8,128)(2,1)S(1)} %dynamic-slice_bitcast_fusion), channel_id=1, source_target_pairs={{0,127},{1,2},{2,1},{3,4},{4,3},{5,6},{6,5},{7,8},{8,7},{9,10},{10... | collective-permute-start | bytes 786440 | tf_op jit(solution)/shard_map/ppermute | solution.py:395
  49.8 12.0 %copy-start.4 = (s32[1,128,512]{2,1,0:T(8,128)S(1)}, s32[1,128,512]{2,1,0:T(8,128)}, u32[]{:S(2)}) copy-start(s32[1,128,512]{2,1,0:T(8,128)} %param.6) | copy-start | bytes 786436

commit v5 on v4

--- a/solution.py
+++ b/solution.py
@@ -21,6 +21,7 @@
 WIDE = COLS + 1
 SLOT = GROUP + 1
 MIB = 1 << 20
+LIMIT = 24
 
 raw_taps = (0.1353352832366127, 0.6065306597126334, 1.0)
 tap_total = raw_taps[2] + 2.0 * (raw_taps[0] + raw_taps[1])
@@ -30,11 +31,18 @@
 bf16 = jnp.bfloat16
 
 
-def onehot_of(row, count):
-    wide = jnp.broadcast_to(row, (16, SLOTS))
-    ids = lax.broadcasted_iota(jnp.int32, (16, SLOTS), 0)
-    inner = jnp.where((wide & 15) == ids, 1.0, 0.0).astype(bf16)
-    outer = (wide >> 4).astype(f32).astype(bf16)
+def digits_of(row):
+    wide = jnp.broadcast_to(row, (8, SLOTS))
+    low = (wide >> 8) & 15
+    ids = lax.broadcasted_iota(jnp.int32, (8, SLOTS), 0)
+    inner = jnp.concatenate(
+        [jnp.where(low == ids, 1.0, 0.0), jnp.where(low == ids + 8, 1.0, 0.0)], axis=0
+    ).astype(bf16)
+    high = (wide >> 12).astype(f32)
+    return inner, jnp.concatenate([high, high], axis=0).astype(bf16)
+
+
+def table_of(inner, outer, count):
     none = jnp.zeros((16, SLOTS), bf16)
     return jnp.concatenate(
         [jnp.where(outer == jnp.full((16, SLOTS), i, bf16), inner, none) for i in range(count)], axis=0
@@ -61,8 +69,8 @@
     return limit
 
 
-def deposit_kernel(counts, cells_far, species_far, mix_far, own_far, sent0_far, sent1_far,
-                   cells, species, mix, own, sent0, sent1, w_s, d_s, sems, out_sems):
+def deposit_kernel(counts_far, cells_far, species_far, mix_far, own_far, sent0_far, sent1_far,
+                   counts, cells, species, mix, own, sent0, sent1, w_s, d_s, sems, out_sems, count_sem):
     sent = [(sent0, k) for k in range(SIZES[0])] + [(sent1, k) for k in range(SIZES[1])]
 
     def fetches(r):
@@ -80,6 +88,8 @@
             for i, (near, far) in enumerate(((sent0, sent0_far), (sent1, sent1_far), (own, own_far)))
         ]
 
+    count_copy = pltpu.make_async_copy(counts_far, counts, count_sem)
+    count_copy.start()
     for r in range(ROWS):
         for copy in fetches(r):
             copy.start()
@@ -88,6 +98,8 @@
         for k in (6, 7):
             w_s[t, k * WIDE:k * WIDE + COLS] = zero
             w_s[t, (8 + k) * WIDE:(8 + k) * WIDE + COLS] = zero
+
+    count_copy.wait()
 
     def one_row(r, carry):
         for copy in fetches(r):
@@ -101,10 +113,10 @@
                 w_s[t, k * WIDE:k * WIDE + COLS] = jnp.where(upper, 0.0, w)
                 w_s[t, (8 + k) * WIDE:(8 + k) * WIDE + COLS] = jnp.where(upper, w, 0.0)
         for b in range(COLS):
-            plane = cells[pl.ds(first + b, 1), :] >> 8
-            table = onehot_of(plane & 127, 8)
+            inner, outer = digits_of(cells[pl.ds(first + b, 1), :])
+            second = outer > 7.5
+            table = table_of(inner, jnp.where(second, outer - 8.0, outer), 8)
             w = jnp.concatenate([w_s[t, pl.ds(b, 16, stride=WIDE)] for t in range(4)], axis=1).astype(bf16)
-            second = jnp.broadcast_to(plane >> 7, (16, SLOTS)).astype(f32).astype(bf16) > 0.5
             none = jnp.zeros((16, SLOTS), bf16)
             halves = jnp.concatenate([jnp.where(second, none, w), jnp.where(second, w, none)], axis=0)
             dens = lax.dot_general(halves, table, (((1,), (1,)), ((), ())), preferred_element_type=f32)
@@ -128,6 +140,7 @@
 
 VM = pltpu.MemorySpace.VMEM
 SM = pltpu.MemorySpace.SMEM
+FAR = pltpu.MemorySpace.HBM
 
 
 def deposit(counts, cells, species, mix):
@@ -135,9 +148,10 @@
     return pl.pallas_call(
         deposit_kernel,
         name="deposit",
-        in_specs=[pl.BlockSpec(memory_space=SM)] + [pl.BlockSpec(memory_space=pltpu.MemorySpace.HBM)] * 3,
-        out_specs=[pl.BlockSpec(memory_space=pltpu.MemorySpace.HBM)] * 3,
+        in_specs=[pl.BlockSpec(memory_space=FAR)] * 4,
+        out_specs=[pl.BlockSpec(memory_space=FAR)] * 3,
         scratch_shapes=[
+            pltpu.SMEM((ROWS * COLS,), jnp.int32),
             pltpu.VMEM((ROWS * COLS, SLOTS), jnp.int32),
             pltpu.VMEM((ROWS * COLS, SLOTS), jnp.int32),
             pltpu.VMEM((SPECIES, ROWS * COLS, SLOTS), bf16),
@@ -148,12 +162,13 @@
             pltpu.VMEM((2, 16 * WIDE, LANES), f32),
             pltpu.SemaphoreType.DMA((3, ROWS)),
             pltpu.SemaphoreType.DMA((3, ROWS)),
+            pltpu.SemaphoreType.DMA,
         ],
         out_shape=[jax.ShapeDtypeStruct((2, SPECIES) + half, f32)]
         + [jax.ShapeDtypeStruct((2, size) + half, bf16) for size in SIZES],
-        compiler_params=pltpu.CompilerParams(vmem_limit_bytes=60 * MIB),
+        compiler_params=pltpu.CompilerParams(vmem_limit_bytes=LIMIT * MIB),
         cost_estimate=pl.CostEstimate(flops=10**9, bytes_accessed=5 * 10**6, transcendentals=0),
-    )(counts, cells, species, mix)
+    )(*(pltpu.with_memory_space_constraint(v, FAR) for v in (counts, cells, species, mix)))
 
 
 def mixing_kernel(counts, mix_matrix, species, mix, mixed):
@@ -226,6 +241,7 @@
     k = pl.program_id(0)
     lane = lax.broadcasted_iota(jnp.int32, (COLS, LANES), 1)
     col = lane & 15
+    lower = lane.astype(f32).astype(bf16) < 64
     cu = 1.0 / (SMOOTH_SCALE * SLOPE_SCALE)
     cz = 0.5 / (SMOOTH_SCALE * SMOOTH_SCALE)
     even = jnp.full((COLS, LANES), even_ref[0], jnp.int32) == 1
@@ -260,18 +276,14 @@
         else:
             y_s[2 + i] = out
     for p in range(6):
+        pieces = [split(y_s[p, h * COLS:(h + 1) * COLS]) for h in range(HALVES)]
         for h in range(HALVES):
-            before = (h + HALVES - 1) % HALVES
-            after = (h + 1) % HALVES
-            v = y_s[p, h * COLS:(h + 1) * COLS]
-            around = jnp.where(
-                lane < 64,
-                y_s[p, after * COLS:(after + 1) * COLS],
-                y_s[p, before * COLS:(before + 1) * COLS],
-            )
-            for part, value in ((0, v), (1, around)):
-                for level, piece in enumerate(split(value)):
-                    w_s[level, p, h * COLS:(h + 1) * COLS, part * LANES:(part + 1) * LANES] = piece
+            rows = slice(h * COLS, (h + 1) * COLS)
+            for level in range(2):
+                w_s[level, p, rows, :LANES] = pieces[h][level]
+                w_s[level, p, rows, LANES:] = jnp.where(
+                    lower, pieces[(h + 1) % HALVES][level], pieces[(h - 1) % HALVES][level]
+                )
         table = taps[:, 3 * LANES:] if p < 2 else taps[:, 2 * LANES:3 * LANES]
         out = jnp.dot(w_s[0, p], table, preferred_element_type=f32) + jnp.dot(
             w_s[1, p], table, preferred_element_type=f32
@@ -334,7 +346,7 @@
         first = pl.multiple_of(g * GROUP, GROUP)
         for b in range(GROUP):
             d = first + b
-            table = onehot_of(cells[pl.ds(d, 1), :] >> 8, 16)
+            table = table_of(*digits_of(cells[pl.ds(d, 1), :]), 16)
             rows = jnp.concatenate(
                 [ready0[d, :32], ready1[d, :16], ready0[d, 32:], ready1[d, 16:]], axis=0
             )

time: 69 us -> 68.3 us (0.990)
  local copies, waits for them, and re-layouts: 0.19 us -> 1.31 us
  waiting for transfers between devices: 20.7 us -> 19.6 us
  Pallas kernels: 28.2 us -> 27.5 us
    unnamed x15 -> x13, local copies, waits for them, and re-layouts: 0.12 us -> 1.24 us
    ppermute x8, waiting for transfers between devices: 20.7 us -> 19.6 us  [swap(): return lax.ppermute(value, axes, pairs)]
  transfers between devices with their start and end apart: 8 -> 8, of which waited for: 5 -> 4; matrix products, arithmetic and copies ran while one was open for 0% -> 0% of each run, Pallas kernels for 7% -> 7%
where the time goes in v5:
time: 68.3 us; the launch traced here: 68.2 us
  Pallas kernels  27.5 us (40%)
  starting transfers between devices  19.7 us (29%)
  waiting for transfers between devices  19.6 us (29%)
  local copies, waits for them, and re-layouts  1.31 us (2%)
    ppermute x8, starting transfers between devices, swap(): return lax.ppermute(value, axes, pairs)  19.7 us
    ppermute x8, waiting for transfers between devices, swap(): return lax.ppermute(value, axes, pairs)  19.6 us
    pallas_call x2, Pallas kernels, smooth(): pl.pallas_call(functools.partial(smooth_kernel, size), name='smooth', gri...  9.5 us
    pallas_call x1, Pallas kernels, deposit(): pl.pallas_call(deposit_kernel, name='deposit', in_specs=[pl.BlockSpec(mem...  9.28 us
    pallas_call x1, Pallas kernels, pick(): pl.pallas_call(pick_kernel, name='pick', in_specs=[pl.BlockSpec(memory_sp...  7.01 us
    pallas_call x1, Pallas kernels, mixing(): pl.pallas_call(mixing_kernel, name='mixing', in_specs=[pl.BlockSpec(memor...  1.7 us
  transfers between devices with their start and end apart: 8, of which 4 were waited for; matrix products, arithmetic and copies ran while one was open for 0% of the time, Pallas kernels for 7%

profile of v5, /device:TPU:0, one launch (start us, length us, event | category | flops | bytes accessed | tf_op | source)
XLA Modules:
  0.0 68.2 jit_solution(8046572726572555158)
XLA Ops:
  0.0 0.0 copy-start.5
  0.0 0.0 copy-start.2
  0.0 0.0 copy-start.4
  0.0 9.3 %deposit.1 = (f32[2,6,16,16,128]{4,3,2,1,0:T(8,128)S(1)}, bf16[2,4,16,16,128]{4,3,2,1,0:T(8,128)(2,1)}, bf16[2,2,16,16,128]{4,3,2,1,0:T(8,128)(2,1)}) custom-call(s32[128]{0:T(128)} %bitcast.30, s32[128,512]{1,0:T(8,128)} %bitcast.28, s32[128,512]{1,0:T(8,128)} %bitcast.26, bf16[6,128,512]{2,1,0:T(8,128)(2,1)} %bitcast.24), custom_call_target="tpu_custom_call" | custom-call | flops 1000000000 | bytes 5000000 | tf_op jit(solution)/shard_map/deposit/pallas_call | solution.py:148
  9.3 8.3 %collective-permute-start.1 = (bf16[2,4,16,16,128]{4,3,2,1,0:T(8,128)(2,1)}, bf16[2,4,16,16,128]{4,3,2,1,0:T(8,128)(2,1)S(1)}, u32[]{:S(2)}, u32[]{:S(2)}) collective-permute-start(bf16[2,4,16,16,128]{4,3,2,1,0:T(8,128)(2,1)} %get-tuple-element.9), channel_id=1, source_target_pairs={{0,127},{1,2},{2,1},{3,4},{4,3},{5,6},{6,5},{7,8},{8,7},{9,10},{10... | collective-permute-start | bytes 1572872 | tf_op jit(solution)/shard_map/ppermute | solution.py:407
  17.6 0.1 collective-permute-start.5
  17.7 0.0 collective-permute-start
  17.7 2.0 %collective-permute-start.4 = (bf16[2,2,16,16,128]{4,3,2,1,0:T(8,128)(2,1)}, bf16[2,2,16,16,128]{4,3,2,1,0:T(8,128)(2,1)S(1)}, u32[]{:S(2)}, u32[]{:S(2)}) collective-permute-start(bf16[2,2,16,16,128]{4,3,2,1,0:T(8,128)(2,1)} %get-tuple-element.10), channel_id=1, source_target_pairs={{0,1},{1,0},{2,3},{3,2},{4,5},{5,4},{6,7},{7,6},{8,9},{9,8},{10,11... | collective-permute-start | bytes 786440 | tf_op jit(solution)/shard_map/ppermute | solution.py:407
  19.7 0.0 copy-done.5
  19.7 0.1 copy.7
  19.8 9.3 %collective-permute-done.5.near_b = bf16[2,2,16,16,128]{4,3,2,1,0:T(8,128)(2,1)S(1)} collective-permute-done((bf16[2,2,16,16,128]{4,3,2,1,0:T(8,128)(2,1)}, bf16[2,2,16,16,128]{4,3,2,1,0:T(8,128)(2,1)S(1)}, u32[]{:S(2)}, u32[]{:S(2)}) %collective-permute-start.5) | collective-permute-done | bytes 262176 | tf_op jit(solution)/shard_map/ppermute | solution.py:407
  29.2 1.5 %collective-permute-start.6 = (bf16[2,16,16,128]{3,2,1,0:T(8,128)(2,1)S(1)}, bf16[2,16,16,128]{3,2,1,0:T(8,128)(2,1)S(1)}, u32[]{:S(2)}, u32[]{:S(2)}) collective-permute-start(bf16[2,16,16,128]{3,2,1,0:T(8,128)(2,1)S(1)} %dynamic-slice_bitcast_fusion.3), channel_id=1, source_target_pairs={{0,1},{1,0},{2,3},{3,2},{4,5},{5,4},{6,7},{7,6},{8,9},{9,8},{10,11... | collective-permute-start | bytes 393224 | tf_op jit(solution)/shard_map/ppermute | solution.py:407
  30.7 5.2 %collective-permute-done.4.near_a = bf16[2,2,16,16,128]{4,3,2,1,0:T(8,128)(2,1)S(1)} collective-permute-done((bf16[2,2,16,16,128]{4,3,2,1,0:T(8,128)(2,1)}, bf16[2,2,16,16,128]{4,3,2,1,0:T(8,128)(2,1)S(1)}, u32[]{:S(2)}, u32[]{:S(2)}) %collective-permute-start.4) | collective-permute-done | bytes 262176 | tf_op jit(solution)/shard_map/ppermute | solution.py:407
  35.9 7.5 %collective-permute-start.7 = (bf16[2,16,16,128]{3,2,1,0:T(8,128)(2,1)S(1)}, bf16[2,16,16,128]{3,2,1,0:T(8,128)(2,1)S(1)}, u32[]{:S(2)}, u32[]{:S(2)}) collective-permute-start(bf16[2,16,16,128]{3,2,1,0:T(8,128)(2,1)S(1)} %dynamic-slice_bitcast_fusion.2), channel_id=1, source_target_pairs={{0,127},{1,2},{2,1},{3,4},{4,3},{5,6},{6,5},{7,8},{8,7},{9,10},{10... | collective-permute-start | bytes 393224 | tf_op jit(solution)/shard_map/ppermute | solution.py:407
  43.4 0.0 collective-permute-done.1.near_b
  43.4 0.0 copy-start
  43.4 0.1 collective-permute-start.2
  43.5 0.0 collective-permute-done.near_a
  43.6 0.1 collective-permute-start.3
  43.7 0.0 copy-done.2
  43.7 0.0 copy-done.4
  43.7 0.0 copy-start.1
  43.7 1.1 %copy-done.1 = bf16[1,6,128,512]{3,2,1,0:T(8,128)(2,1)S(1)} copy-done((bf16[1,6,128,512]{3,2,1,0:T(8,128)(2,1)S(1)}, bf16[1,6,128,512]{3,2,1,0:T(8,128)(2,1)}, u32[]{:S(2)}) %copy-start.1) | copy-done | bytes 786456
  44.8 1.7 %mixing.1.mixed = f32[6,128,512]{2,1,0:T(8,128)S(1)} custom-call(s32[128]{0:T(128)S(1)} %bitcast.31, f32[6,6]{1,0:T(8,128)S(1)} %fusion.3.mix_matrix, s32[128,512]{1,0:T(8,128)S(1)} %bitcast.27, bf16[6,128,512]{2,1,0:T(8,128)(2,1)S(1)} %bitcast.25), custom_call_target="tpu_custom_call" | custom-call | flops 1000000000 | bytes 4000000 | tf_op jit(solution)/shard_map/mixing/pallas_call | solution.py:192
  46.5 0.0 collective-permute-done.6.far_a
  46.6 0.0 collective-permute-done.7.far_b
  46.6 0.0 copy-done
  46.6 3.2 %smooth.3.ready1 = bf16[128,32,256]{2,1,0:T(8,128)(2,1)S(1)} custom-call(s32[1]{0:T(128)} %bitcast.1.even_ref, bf16[256,512]{1,0:T(8,128)(2,1)S(1)} %copy-done, f32[2,6,16,16,128]{4,3,2,1,0:T(8,128)S(1)} %get-tuple-element.8.own, bf16[2,2,16,16,128]{4,3,2,1,0:T(8,128)(2,1)S(1)} %collective-permute-done.4.near_a, ...), custom_call_target="tpu_custom_call" | custom-call | flops 1000000000 | bytes 4000000 | tf_op jit(solution)/shard_map/smooth/pallas_call | solution.py:318
  49.8 0.0 copy-start.3
  49.8 0.4 collective-permute-done.2.far_a
  50.2 4.7 %collective-permute-done.3.far_b = bf16[4,16,16,128]{3,2,1,0:T(8,128)(2,1)S(1)} collective-permute-done((bf16[4,16,16,128]{3,2,1,0:T(8,128)(2,1)S(1)}, bf16[4,16,16,128]{3,2,1,0:T(8,128)(2,1)S(1)}, u32[]{:S(2)}, u32[]{:S(2)}) %collective-permute-start.3) | collective-permute-done | bytes 262176 | tf_op jit(solution)/shard_map/ppermute | solution.py:407
  54.9 6.3 %smooth.2.ready0 = bf16[128,64,256]{2,1,0:T(8,128)(2,1)S(1)} custom-call(s32[1]{0:T(128)} %bitcast.1.even_ref, bf16[256,512]{1,0:T(8,128)(2,1)S(1)} %copy-done, f32[2,6,16,16,128]{4,3,2,1,0:T(8,128)S(1)} %get-tuple-element.8.own, bf16[2,4,16,16,128]{4,3,2,1,0:T(8,128)(2,1)S(1)} %collective-permute-done.near_a, ...), custom_call_target="tpu_custom_call" | custom-call | flops 1000000000 | bytes 4000000 | tf_op jit(solution)/shard_map/smooth/pallas_call | solution.py:318
  61.2 0.0 copy-done.3
  61.2 7.0 %pick.1 = f32[3,128,512]{2,1,0:T(8,128)} custom-call(s32[128,512]{1,0:T(8,128)S(1)} %bitcast.29, bf16[128,64,256]{2,1,0:T(8,128)(2,1)S(1)} %smooth.2.ready0, bf16[128,32,256]{2,1,0:T(8,128)(2,1)S(1)} %smooth.3.ready1, f32[6,128,512]{2,1,0:T(8,128)S(1)} %mixing.1.mixed), custom_call_target="tpu_custom_call" | custom-call | flops 6000000000 | bytes 10000000 | tf_op jit(solution)/shard_map/pick/pallas_call | solution.py:380
  (5 shorter events, 0.1 us)
Async XLA Ops:
  0.0 19.7 %copy-start.5 = (f32[6,6]{1,0:T(8,128)S(1)}, f32[6,6]{1,0:T(8,128)}, u32[]{:S(2)}) copy-start(f32[6,6]{1,0:T(8,128)} %param.10) | copy-start | bytes 436
  0.0 43.7 %copy-start.2 = (s32[1,128,512]{2,1,0:T(8,128)S(1)}, s32[1,128,512]{2,1,0:T(8,128)}, u32[]{:S(2)}) copy-start(s32[1,128,512]{2,1,0:T(8,128)} %param.7) | copy-start | bytes 786436
  0.0 43.7 %copy-start.4 = (s32[1,128]{1,0:T(1,128)S(1)}, s32[1,128]{1,0:T(1,128)}, u32[]{:S(2)}) copy-start(s32[1,128]{1,0:T(1,128)} %param.9) | copy-start | bytes 1540
  9.3 34.1 %collective-permute-start.1 = (bf16[2,4,16,16,128]{4,3,2,1,0:T(8,128)(2,1)}, bf16[2,4,16,16,128]{4,3,2,1,0:T(8,128)(2,1)S(1)}, u32[]{:S(2)}, u32[]{:S(2)}) collective-permute-start(bf16[2,4,16,16,128]{4,3,2,1,0:T(8,128)(2,1)} %get-tuple-element.9), channel_id=1, source_target_pairs={{0,127},{1,2},{2,1},{3,4},{4,3},{5,6},{6,5},{7,8},{8,7},{9,10},{10... | collective-permute-start | bytes 1572872 | tf_op jit(solution)/shard_map/ppermute | solution.py:407
  17.6 11.5 %collective-permute-start.5 = (bf16[2,2,16,16,128]{4,3,2,1,0:T(8,128)(2,1)}, bf16[2,2,16,16,128]{4,3,2,1,0:T(8,128)(2,1)S(1)}, u32[]{:S(2)}, u32[]{:S(2)}) collective-permute-start(bf16[2,2,16,16,128]{4,3,2,1,0:T(8,128)(2,1)} %get-tuple-element.10), channel_id=1, source_target_pairs={{0,127},{1,2},{2,1},{3,4},{4,3},{5,6},{6,5},{7,8},{8,7},{9,10},{10... | collective-permute-start | bytes 786440 | tf_op jit(solution)/shard_map/ppermute | solution.py:407
  17.7 25.8 %collective-permute-start = (bf16[2,4,16,16,128]{4,3,2,1,0:T(8,128)(2,1)}, bf16[2,4,16,16,128]{4,3,2,1,0:T(8,128)(2,1)S(1)}, u32[]{:S(2)}, u32[]{:S(2)}) collective-permute-start(bf16[2,4,16,16,128]{4,3,2,1,0:T(8,128)(2,1)} %get-tuple-element.9), channel_id=1, source_target_pairs={{0,1},{1,0},{2,3},{3,2},{4,5},{5,4},{6,7},{7,6},{8,9},{9,8},{10,11... | collective-permute-start | bytes 1572872 | tf_op jit(solution)/shard_map/ppermute | solution.py:407
  17.7 18.1 %collective-permute-start.4 = (bf16[2,2,16,16,128]{4,3,2,1,0:T(8,128)(2,1)}, bf16[2,2,16,16,128]{4,3,2,1,0:T(8,128)(2,1)S(1)}, u32[]{:S(2)}, u32[]{:S(2)}) collective-permute-start(bf16[2,2,16,16,128]{4,3,2,1,0:T(8,128)(2,1)} %get-tuple-element.10), channel_id=1, source_target_pairs={{0,1},{1,0},{2,3},{3,2},{4,5},{5,4},{6,7},{7,6},{8,9},{9,8},{10,11... | collective-permute-start | bytes 786440 | tf_op jit(solution)/shard_map/ppermute | solution.py:407
  29.2 17.4 %collective-permute-start.6 = (bf16[2,16,16,128]{3,2,1,0:T(8,128)(2,1)S(1)}, bf16[2,16,16,128]{3,2,1,0:T(8,128)(2,1)S(1)}, u32[]{:S(2)}, u32[]{:S(2)}) collective-permute-start(bf16[2,16,16,128]{3,2,1,0:T(8,128)(2,1)S(1)} %dynamic-slice_bitcast_fusion.3), channel_id=1, source_target_pairs={{0,1},{1,0},{2,3},{3,2},{4,5},{5,4},{6,7},{7,6},{8,9},{9,8},{10,11... | collective-permute-start | bytes 393224 | tf_op jit(solution)/shard_map/ppermute | solution.py:407
  35.9 10.7 %collective-permute-start.7 = (bf16[2,16,16,128]{3,2,1,0:T(8,128)(2,1)S(1)}, bf16[2,16,16,128]{3,2,1,0:T(8,128)(2,1)S(1)}, u32[]{:S(2)}, u32[]{:S(2)}) collective-permute-start(bf16[2,16,16,128]{3,2,1,0:T(8,128)(2,1)S(1)} %dynamic-slice_bitcast_fusion.2), channel_id=1, source_target_pairs={{0,127},{1,2},{2,1},{3,4},{4,3},{5,6},{6,5},{7,8},{8,7},{9,10},{10... | collective-permute-start | bytes 393224 | tf_op jit(solution)/shard_map/ppermute | solution.py:407
  43.4 3.2 %copy-start = (bf16[256,512]{1,0:T(8,128)(2,1)S(1)}, bf16[256,512]{1,0:T(8,128)(2,1)}, u32[]{:S(2)}) copy-start(bf16[256,512]{1,0:T(8,128)(2,1)} %constant.45.taps) | copy-start | bytes 786436
  43.4 6.8 %collective-permute-start.2 = (bf16[4,16,16,128]{3,2,1,0:T(8,128)(2,1)S(1)}, bf16[4,16,16,128]{3,2,1,0:T(8,128)(2,1)S(1)}, u32[]{:S(2)}, u32[]{:S(2)}) collective-permute-start(bf16[4,16,16,128]{3,2,1,0:T(8,128)(2,1)S(1)} %dynamic-slice_bitcast_fusion.1), channel_id=1, source_target_pairs={{0,1},{1,0},{2,3},{3,2},{4,5},{5,4},{6,7},{7,6},{8,9},{9,8},{10,11... | collective-permute-start | bytes 786440 | tf_op jit(solution)/shard_map/ppermute | solution.py:407
  43.6 11.3 %collective-permute-start.3 = (bf16[4,16,16,128]{3,2,1,0:T(8,128)(2,1)S(1)}, bf16[4,16,16,128]{3,2,1,0:T(8,128)(2,1)S(1)}, u32[]{:S(2)}, u32[]{:S(2)}) collective-permute-start(bf16[4,16,16,128]{3,2,1,0:T(8,128)(2,1)S(1)} %dynamic-slice_bitcast_fusion), channel_id=1, source_target_pairs={{0,127},{1,2},{2,1},{3,4},{4,3},{5,6},{6,5},{7,8},{8,7},{9,10},{10... | collective-permute-start | bytes 786440 | tf_op jit(solution)/shard_map/ppermute | solution.py:407
  43.7 1.1 %copy-start.1 = (bf16[1,6,128,512]{3,2,1,0:T(8,128)(2,1)S(1)}, bf16[1,6,128,512]{3,2,1,0:T(8,128)(2,1)}, u32[]{:S(2)}) copy-start(bf16[1,6,128,512]{3,2,1,0:T(8,128)(2,1)} %param.8) | copy-start | bytes 2359300
  49.8 11.4 %copy-start.3 = (s32[1,128,512]{2,1,0:T(8,128)S(1)}, s32[1,128,512]{2,1,0:T(8,128)}, u32[]{:S(2)}) copy-start(s32[1,128,512]{2,1,0:T(8,128)} %param.6) | copy-start | bytes 786436

commit v6 on v5

--- a/solution.py
+++ b/solution.py
@@ -237,7 +237,12 @@
     return top, (v - top.astype(f32)).astype(bf16)
 
 
-def smooth_kernel(size, even_ref, taps, own, near_a, near_b, far_a, far_b, ready, x_s, y_s, w_s, g_s):
+def smooth_kernel(size, planes, even_ref, taps, own, near_a, near_b, *refs):
+    flat, slopes = 0 in planes, 2 in planes
+    far_a, far_b = refs[:2] if slopes else (None, None)
+    ready, x_s, y_s, w_s, g_s = refs[-5:]
+    outs = (0, 1, 2, 3) * flat + (4, 5) * slopes
+    rows_of = rows_per_species(planes)
     k = pl.program_id(0)
     lane = lax.broadcasted_iota(jnp.int32, (COLS, LANES), 1)
     col = lane & 15
@@ -250,110 +255,133 @@
             a, b = a.astype(f32), b.astype(f32)
             return jnp.where(even, b, a), jnp.where(even, a, b)
 
-        l2, r2 = sides(far_a[0, h], far_b[0, h])
         a, r0 = sides(near_a[0, 0, h], near_b[0, 0, h])
         b, r1 = sides(near_a[1, 0, h], near_b[1, 0, h])
         o0 = own[0, 0, h]
         o1 = own[1, 0, h]
-        um = T2 * (l2 + o1) + T1 * (a + o0) + T0 * b
         u0 = T2 * (a + r0) + T1 * (b + o1) + T0 * o0
         u1 = T2 * (b + r1) + T1 * (o0 + r0) + T0 * o1
-        up = T2 * (o0 + r2) + T1 * (o1 + r1) + T0 * r0
-        for i, v in enumerate((cu * u0, cu * u1, cz * (u1 - um), cz * (up - u0))):
+        values = {}
+        if flat:
+            values.update({0: cu * u0, 1: cu * u1})
+        if slopes:
+            l2, r2 = sides(far_a[0, h], far_b[0, h])
+            um = T2 * (l2 + o1) + T1 * (a + o0) + T0 * b
+            up = T2 * (o0 + r2) + T1 * (o1 + r1) + T0 * r0
+            values.update({2: cz * (u1 - um), 3: cz * (up - u0)})
+        for i, plane in enumerate(planes):
+            v = values[plane]
             around = jnp.where(col < 8, pltpu.roll(v, COLS - 1, 0), pltpu.roll(v, 1, 0))
             for part, value in ((0, v), (1, around)):
                 for level, piece in enumerate(split(value)):
                     x_s[level, i, h * COLS:(h + 1) * COLS, part * LANES:(part + 1) * LANES] = piece
-    for i in range(4):
-        width = 2 * LANES if i < 2 else LANES
-        table = taps[:, :width]
+    for i, plane in enumerate(planes):
+        table = taps[:, :2 * LANES] if plane < 2 else taps[:, :LANES]
         out = jnp.dot(x_s[0, i], table, preferred_element_type=f32) + jnp.dot(
             x_s[1, i], table, preferred_element_type=f32
         )
-        if i < 2:
-            y_s[i] = out[:, :LANES]
-            y_s[2 + i] = out[:, LANES:]
+        if plane < 2:
+            y_s[outs.index(plane)] = out[:, :LANES]
+            y_s[outs.index(2 + plane)] = out[:, LANES:]
         else:
-            y_s[2 + i] = out
-    for p in range(6):
-        pieces = [split(y_s[p, h * COLS:(h + 1) * COLS]) for h in range(HALVES)]
+            y_s[outs.index(2 + plane)] = out
+    for i, p in enumerate(outs):
+        pieces = [split(y_s[i, h * COLS:(h + 1) * COLS]) for h in range(HALVES)]
         for h in range(HALVES):
             rows = slice(h * COLS, (h + 1) * COLS)
             for level in range(2):
-                w_s[level, p, rows, :LANES] = pieces[h][level]
-                w_s[level, p, rows, LANES:] = jnp.where(
+                w_s[level, i, rows, :LANES] = pieces[h][level]
+                w_s[level, i, rows, LANES:] = jnp.where(
                     lower, pieces[(h + 1) % HALVES][level], pieces[(h - 1) % HALVES][level]
                 )
         table = taps[:, 3 * LANES:] if p < 2 else taps[:, 2 * LANES:3 * LANES]
-        out = jnp.dot(w_s[0, p], table, preferred_element_type=f32) + jnp.dot(
-            w_s[1, p], table, preferred_element_type=f32
+        out = jnp.dot(w_s[0, i], table, preferred_element_type=f32) + jnp.dot(
+            w_s[1, i], table, preferred_element_type=f32
         )
         for h in range(HALVES):
-            g_s[h, pl.ds((k * 8 + p) * WIDE, COLS)] = out[h * COLS:(h + 1) * COLS]
-
-    @pl.when(k == 0)
-    def _():
-        zero = jnp.zeros((HALVES, 2 * WIDE, LANES), f32)
-        for i in range(size):
-            g_s[:, (i * 8 + 6) * WIDE:(i * 8 + 8) * WIDE] = zero
+            g_s[h, pl.ds((k * rows_of + i) * WIDE, COLS)] = out[h * COLS:(h + 1) * COLS]
+
+    if rows_of > len(outs):
+        @pl.when(k == 0)
+        def _():
+            zero = jnp.zeros((HALVES, (rows_of - len(outs)) * WIDE, LANES), f32)
+            for i in range(size):
+                g_s[:, (i * rows_of + len(outs)) * WIDE:(i + 1) * rows_of * WIDE] = zero
 
     @pl.when(k == size - 1)
     def _():
+        count = rows_of * size
+
         def one_row(r, carry):
             for q in range(COLS):
                 for h in range(2):
-                    top, rest = split(g_s[2 * r + h, pl.ds(q, 8 * size, stride=WIDE)])
-                    ready[r * COLS + q, :8 * size, h * LANES:(h + 1) * LANES] = top
-                    ready[r * COLS + q, 8 * size:, h * LANES:(h + 1) * LANES] = rest
+                    value = g_s[2 * r + h, pl.ds(q, count, stride=WIDE)]
+                    top = value.astype(bf16).astype(f32)
+                    ready[r * COLS + q, :, h * LANES:(h + 1) * LANES] = jnp.concatenate(
+                        [top, value - top], axis=0
+                    ).astype(bf16)
             return carry
 
         lax.fori_loop(0, ROWS, one_row, 0)
 
 
-def smooth(chunk, even, taps, own, near_a, near_b, far_a, far_b):
+def rows_per_species(planes):
+    return {(0, 1): 4, (2, 3): 2, (0, 1, 2, 3): 8}[planes]
+
+
+def smooth(chunk, planes, even, taps, own, *halos):
     size, start = SIZES[chunk], STARTS[chunk]
     half = (HALVES, COLS, LANES)
+    count = rows_per_species(planes) * size
+    outs = sum(2 if plane < 2 else 1 for plane in planes)
     two = pl.BlockSpec((2, 1) + half, lambda k: (0, k, 0, 0, 0))
     one = pl.BlockSpec((1,) + half, lambda k: (k, 0, 0, 0))
     return pl.pallas_call(
-        functools.partial(smooth_kernel, size),
+        functools.partial(smooth_kernel, size, planes),
         name="smooth",
         grid=(size,),
         in_specs=[
             pl.BlockSpec(memory_space=SM),
             pl.BlockSpec((2 * LANES, 4 * LANES), lambda k: (0, 0)),
             pl.BlockSpec((2, 1) + half, lambda k: (0, start + k, 0, 0, 0)),
-            two,
-            two,
-            one,
-            one,
-        ],
-        out_specs=pl.BlockSpec((ROWS * COLS, 16 * size, 2 * LANES), lambda k: (0, 0, 0)),
-        out_shape=jax.ShapeDtypeStruct((ROWS * COLS, 16 * size, 2 * LANES), bf16),
+        ]
+        + ([two, two, one, one] if 2 in planes else [two, two]),
+        out_specs=pl.BlockSpec((ROWS * COLS, 2 * count, 2 * LANES), lambda k: (0, 0, 0)),
+        out_shape=jax.ShapeDtypeStruct((ROWS * COLS, 2 * count, 2 * LANES), bf16),
         scratch_shapes=[
-            pltpu.VMEM((2, 4, HALVES * COLS, 2 * LANES), bf16),
-            pltpu.VMEM((6, HALVES * COLS, LANES), f32),
-            pltpu.VMEM((2, 6, HALVES * COLS, 2 * LANES), bf16),
-            pltpu.VMEM((HALVES, size * 8 * WIDE, LANES), f32),
+            pltpu.VMEM((2, len(planes), HALVES * COLS, 2 * LANES), bf16),
+            pltpu.VMEM((outs, HALVES * COLS, LANES), f32),
+            pltpu.VMEM((2, outs, HALVES * COLS, 2 * LANES), bf16),
+            pltpu.VMEM((HALVES, count * WIDE, LANES), f32),
         ],
         compiler_params=pltpu.CompilerParams(vmem_limit_bytes=24 * MIB),
         cost_estimate=pl.CostEstimate(flops=10**9, bytes_accessed=4 * 10**6, transcendentals=0),
-    )(even, taps, own, near_a, near_b, far_a, far_b)
-
-
-def pick_kernel(cells, ready0, ready1, mixed, forces, got_s):
+    )(even, taps, own, *halos)
+
+
+FLAT = (0, 1)
+SLOPES = (2, 3)
+
+
+def row_of(k, p):
+    if k < 4:
+        return k * 4 + p if p < 4 else 16 + k * 2 + p - 4
+    return 24 + (k - 4) * 8 + p
+
+
+def pick_kernel(cells, flat0, slopes0, ready1, mixed, forces, got_s):
     def one_group(g, slot):
         first = pl.multiple_of(g * GROUP, GROUP)
         for b in range(GROUP):
             d = first + b
             table = table_of(*digits_of(cells[pl.ds(d, 1), :]), 16)
-            rows = jnp.concatenate(
-                [ready0[d, :32], ready1[d, :16], ready0[d, 32:], ready1[d, 16:]], axis=0
+            rows = jnp.concatenate([flat0[d], slopes0[d], ready1[d]], axis=0)
+            got = jnp.dot(rows, table, preferred_element_type=f32)
+            got = jnp.concatenate(
+                [got[:16] + got[16:32], got[32:40] + got[40:48], got[48:64] + got[64:]], axis=0
             )
-            got = jnp.dot(rows, table, preferred_element_type=f32)
-            got = got[:48] + got[48:]
             for t in range(4):
-                got_s[slot, t, pl.ds(b, 48, stride=SLOT)] = got[:, t * LANES:(t + 1) * LANES]
+                got_s[slot, t, pl.ds(b, 40, stride=SLOT)] = got[:, t * LANES:(t + 1) * LANES]
         for t in range(4):
             lanes = slice(t * LANES, (t + 1) * LANES)
             upper = (cells[pl.ds(first, GROUP), lanes] & 1) == 1
@@ -361,10 +389,10 @@
             for a in range(3):
                 total = None
                 for k in range(SPECIES):
-                    row = (k * 8 + 2 * a) * SLOT
-                    value = jnp.where(
-                        upper, got_s[slot, t, row + SLOT:row + SLOT + GROUP], got_s[slot, t, row:row + GROUP]
+                    low, high = (
+                        got_s[slot, t, pl.ds(row_of(k, 2 * a + z) * SLOT, GROUP)] for z in range(2)
                     )
+                    value = jnp.where(upper, high, low)
                     total = vs[k] * value if total is None else total + vs[k] * value
                 forces[a, pl.ds(first, GROUP), lanes] = total
 
@@ -380,10 +408,10 @@
     return pl.pallas_call(
         pick_kernel,
         name="pick",
-        in_specs=[pl.BlockSpec(memory_space=VM)] * 4,
+        in_specs=[pl.BlockSpec(memory_space=VM)] * 5,
         out_specs=pl.BlockSpec(memory_space=VM),
         out_shape=jax.ShapeDtypeStruct((3, ROWS * COLS, SLOTS), f32),
-        scratch_shapes=[pltpu.VMEM((4, 4, 48 * SLOT, LANES), f32)],
+        scratch_shapes=[pltpu.VMEM((4, 4, 40 * SLOT, LANES), f32)],
         compiler_params=pltpu.CompilerParams(vmem_limit_bytes=24 * MIB),
         cost_estimate=pl.CostEstimate(flops=6 * 10**9, bytes_accessed=10**7, transcendentals=0),
     )(cells, *ready, mixed)
@@ -410,7 +438,11 @@
         near_b = swap(sent[chunk], swap_b)
         far_a = swap(lax.dynamic_index_in_dim(near_b, 1 - odd, 0, False), swap_a)
         far_b = swap(lax.dynamic_index_in_dim(near_a, odd, 0, False), swap_b)
-        ready.append(smooth(chunk, even, taps, own, near_a, near_b, far_a, far_b))
+        if chunk == 0:
+            ready.append(smooth(chunk, FLAT, even, taps, own, near_a, near_b))
+            ready.append(smooth(chunk, SLOPES, even, taps, own, near_a, near_b, far_a, far_b))
+        else:
+            ready.append(smooth(chunk, FLAT + SLOPES, even, taps, own, near_a, near_b, far_a, far_b))
     mixed = mixing(counts, mix_matrix, species, mix)
     return pick(cells, ready, mixed)[None]
 

time: 68.3 us -> 67.4 us (0.987)
  the two profiles are of different devices: /device:TPU:0 before, /device:TPU:1 now
where the time goes in v6:
time: 67.4 us; the launch traced here: 67.2 us
  Pallas kernels  29.3 us (43%)
  waiting for transfers between devices  19.6 us (29%)
  starting transfers between devices  16.8 us (25%)
  local copies, waits for them, and re-layouts  1.32 us (2%)
    ppermute x8, waiting for transfers between devices, swap(): return lax.ppermute(value, axes, pairs)  19.6 us
    ppermute x8, starting transfers between devices, swap(): return lax.ppermute(value, axes, pairs)  16.8 us
    pallas_call x3, Pallas kernels, smooth(): pl.pallas_call(functools.partial(smooth_kernel, size, planes), name='smoo...  11.3 us
    pallas_call x1, Pallas kernels, deposit(): pl.pallas_call(deposit_kernel, name='deposit', in_specs=[pl.BlockSpec(mem...  9.28 us
    pallas_call x1, Pallas kernels, pick(): pl.pallas_call(pick_kernel, name='pick', in_specs=[pl.BlockSpec(memory_sp...  7.01 us
    pallas_call x1, Pallas kernels, mixing(): pl.pallas_call(mixing_kernel, name='mixing', in_specs=[pl.BlockSpec(memor...  1.7 us
  transfers between devices with their start and end apart: 8, of which 2 were waited for; matrix products, arithmetic and copies ran while one was open for 0% of the time, Pallas kernels for 14%

profile of v6, /device:TPU:1, one launch (start us, length us, event | category | flops | bytes accessed | tf_op | source)
XLA Modules:
  0.0 67.2 jit_solution(7025199507255423045)
XLA Ops:
  0.0 0.0 copy-start.5
  0.0 0.0 copy-start.2
  0.0 0.0 copy-start.4
  0.0 9.3 %deposit.1 = (f32[2,6,16,16,128]{4,3,2,1,0:T(8,128)S(1)}, bf16[2,4,16,16,128]{4,3,2,1,0:T(8,128)(2,1)}, bf16[2,2,16,16,128]{4,3,2,1,0:T(8,128)(2,1)}) custom-call(s32[128]{0:T(128)} %bitcast.30, s32[128,512]{1,0:T(8,128)} %bitcast.28, s32[128,512]{1,0:T(8,128)} %bitcast.26, bf16[6,128,512]{2,1,0:T(8,128)(2,1)} %bitcast.24), custom_call_target="tpu_custom_call" | custom-call | flops 1000000000 | bytes 5000000 | tf_op jit(solution)/shard_map/deposit/pallas_call | solution.py:148
  9.3 7.7 %collective-permute-start.1 = (bf16[2,4,16,16,128]{4,3,2,1,0:T(8,128)(2,1)}, bf16[2,4,16,16,128]{4,3,2,1,0:T(8,128)(2,1)S(1)}, u32[]{:S(2)}, u32[]{:S(2)}) collective-permute-start(bf16[2,4,16,16,128]{4,3,2,1,0:T(8,128)(2,1)} %get-tuple-element.9), channel_id=1, source_target_pairs={{0,127},{1,2},{2,1},{3,4},{4,3},{5,6},{6,5},{7,8},{8,7},{9,10},{10... | collective-permute-start | bytes 1572872 | tf_op jit(solution)/shard_map/ppermute | solution.py:435
  17.0 0.1 collective-permute-start.5
  17.1 0.0 collective-permute-start
  17.1 1.5 %collective-permute-start.4 = (bf16[2,2,16,16,128]{4,3,2,1,0:T(8,128)(2,1)}, bf16[2,2,16,16,128]{4,3,2,1,0:T(8,128)(2,1)S(1)}, u32[]{:S(2)}, u32[]{:S(2)}) collective-permute-start(bf16[2,2,16,16,128]{4,3,2,1,0:T(8,128)(2,1)} %get-tuple-element.10), channel_id=1, source_target_pairs={{0,1},{1,0},{2,3},{3,2},{4,5},{5,4},{6,7},{7,6},{8,9},{9,8},{10,11... | collective-permute-start | bytes 786440 | tf_op jit(solution)/shard_map/ppermute | solution.py:435
  18.5 0.0 copy-done.5
  18.5 0.1 copy.7
  18.6 16.6 %collective-permute-done.5.near_b = bf16[2,2,16,16,128]{4,3,2,1,0:T(8,128)(2,1)S(1)} collective-permute-done((bf16[2,2,16,16,128]{4,3,2,1,0:T(8,128)(2,1)}, bf16[2,2,16,16,128]{4,3,2,1,0:T(8,128)(2,1)S(1)}, u32[]{:S(2)}, u32[]{:S(2)}) %collective-permute-start.5) | collective-permute-done | bytes 262176 | tf_op jit(solution)/shard_map/ppermute | solution.py:435
  35.3 0.1 collective-permute-start.6
  35.4 0.0 collective-permute-done.4.near_a
  35.4 7.3 %collective-permute-start.7 = (bf16[2,16,16,128]{3,2,1,0:T(8,128)(2,1)S(1)}, bf16[2,16,16,128]{3,2,1,0:T(8,128)(2,1)S(1)}, u32[]{:S(2)}, u32[]{:S(2)}) collective-permute-start(bf16[2,16,16,128]{3,2,1,0:T(8,128)(2,1)S(1)} %dynamic-slice_bitcast_fusion.2), channel_id=1, source_target_pairs={{0,127},{1,2},{2,1},{3,4},{4,3},{5,6},{6,5},{7,8},{8,7},{9,10},{10... | collective-permute-start | bytes 393224 | tf_op jit(solution)/shard_map/ppermute | solution.py:435
  42.7 0.0 collective-permute-done.1.near_b
  42.8 0.0 copy-start
  42.8 0.1 collective-permute-start.2
  42.9 0.0 collective-permute-done.near_a
  42.9 0.1 collective-permute-start.3
  43.0 0.0 copy-done.2
  43.0 0.0 copy-done.4
  43.0 0.0 copy-start.1
  43.0 1.1 %copy-done.1 = bf16[1,6,128,512]{3,2,1,0:T(8,128)(2,1)S(1)} copy-done((bf16[1,6,128,512]{3,2,1,0:T(8,128)(2,1)S(1)}, bf16[1,6,128,512]{3,2,1,0:T(8,128)(2,1)}, u32[]{:S(2)}) %copy-start.1) | copy-done | bytes 786456
  44.2 1.7 %mixing.1.mixed = f32[6,128,512]{2,1,0:T(8,128)S(1)} custom-call(s32[128]{0:T(128)S(1)} %bitcast.31, f32[6,6]{1,0:T(8,128)S(1)} %fusion.3.mix_matrix, s32[128,512]{1,0:T(8,128)S(1)} %bitcast.27, bf16[6,128,512]{2,1,0:T(8,128)(2,1)S(1)} %bitcast.25), custom_call_target="tpu_custom_call" | custom-call | flops 1000000000 | bytes 4000000 | tf_op jit(solution)/shard_map/mixing/pallas_call | solution.py:192
  45.9 0.0 collective-permute-done.6.refs_0_
  45.9 3.0 %collective-permute-done.7.refs_1_ = bf16[2,16,16,128]{3,2,1,0:T(8,128)(2,1)S(1)} collective-permute-done((bf16[2,16,16,128]{3,2,1,0:T(8,128)(2,1)S(1)}, bf16[2,16,16,128]{3,2,1,0:T(8,128)(2,1)S(1)}, u32[]{:S(2)}, u32[]{:S(2)}) %collective-permute-start.7) | collective-permute-done | bytes 131104 | tf_op jit(solution)/shard_map/ppermute | solution.py:435
  48.9 0.0 copy-done
  48.9 3.2 %smooth.5.ready1 = bf16[128,32,256]{2,1,0:T(8,128)(2,1)S(1)} custom-call(s32[1]{0:T(128)} %bitcast.1.even_ref, bf16[256,512]{1,0:T(8,128)(2,1)S(1)} %copy-done, f32[2,6,16,16,128]{4,3,2,1,0:T(8,128)S(1)} %get-tuple-element.8.own, bf16[2,2,16,16,128]{4,3,2,1,0:T(8,128)(2,1)S(1)} %collective-permute-done.4.near_a, ...), custom_call_target="tpu_custom_call" | custom-call | flops 1000000000 | bytes 4000000 | tf_op jit(solution)/shard_map/smooth/pallas_call | solution.py:339
  52.1 4.5 %smooth.3.flat0 = bf16[128,32,256]{2,1,0:T(8,128)(2,1)S(1)} custom-call(s32[1]{0:T(128)} %bitcast.1.even_ref, bf16[256,512]{1,0:T(8,128)(2,1)S(1)} %copy-done, f32[2,6,16,16,128]{4,3,2,1,0:T(8,128)S(1)} %get-tuple-element.8.own, bf16[2,4,16,16,128]{4,3,2,1,0:T(8,128)(2,1)S(1)} %collective-permute-done.near_a, ...), custom_call_target="tpu_custom_call" | custom-call | flops 1000000000 | bytes 4000000 | tf_op jit(solution)/shard_map/smooth/pallas_call | solution.py:339
  56.6 0.0 copy-start.3
  56.6 0.0 collective-permute-done.2.refs_0_
  56.6 0.0 collective-permute-done.3.refs_1_
  56.6 3.6 %smooth.4.slopes0 = bf16[128,16,256]{2,1,0:T(8,128)(2,1)S(1)} custom-call(s32[1]{0:T(128)} %bitcast.1.even_ref, bf16[256,512]{1,0:T(8,128)(2,1)S(1)} %copy-done, f32[2,6,16,16,128]{4,3,2,1,0:T(8,128)S(1)} %get-tuple-element.8.own, bf16[2,4,16,16,128]{4,3,2,1,0:T(8,128)(2,1)S(1)} %collective-permute-done.near_a, ...), custom_call_target="tpu_custom_call" | custom-call | flops 1000000000 | bytes 4000000 | tf_op jit(solution)/shard_map/smooth/pallas_call | solution.py:339
  60.2 0.0 copy-done.3
  60.2 7.0 %pick.1 = f32[3,128,512]{2,1,0:T(8,128)} custom-call(s32[128,512]{1,0:T(8,128)S(1)} %bitcast.29, bf16[128,32,256]{2,1,0:T(8,128)(2,1)S(1)} %smooth.3.flat0, bf16[128,16,256]{2,1,0:T(8,128)(2,1)S(1)} %smooth.4.slopes0, bf16[128,32,256]{2,1,0:T(8,128)(2,1)S(1)} %smooth.5.ready1, f32[6,128,512]{2,1,0:T(8,128)S(1)} %mixing.1.mixed), custom_call_target="tpu_custom_call" | custom-call | flops 6000000000 | bytes 10000000 | tf_op jit(solution)/shard_map/pick/pallas_call | solution.py:408
  (5 shorter events, 0.1 us)
Async XLA Ops:
  0.0 18.5 %copy-start.5 = (f32[6,6]{1,0:T(8,128)S(1)}, f32[6,6]{1,0:T(8,128)}, u32[]{:S(2)}) copy-start(f32[6,6]{1,0:T(8,128)} %param.10) | copy-start | bytes 436
  0.0 43.0 %copy-start.2 = (s32[1,128,512]{2,1,0:T(8,128)S(1)}, s32[1,128,512]{2,1,0:T(8,128)}, u32[]{:S(2)}) copy-start(s32[1,128,512]{2,1,0:T(8,128)} %param.7) | copy-start | bytes 786436
  0.0 43.0 %copy-start.4 = (s32[1,128]{1,0:T(1,128)S(1)}, s32[1,128]{1,0:T(1,128)}, u32[]{:S(2)}) copy-start(s32[1,128]{1,0:T(1,128)} %param.9) | copy-start | bytes 1540
  9.3 33.4 %collective-permute-start.1 = (bf16[2,4,16,16,128]{4,3,2,1,0:T(8,128)(2,1)}, bf16[2,4,16,16,128]{4,3,2,1,0:T(8,128)(2,1)S(1)}, u32[]{:S(2)}, u32[]{:S(2)}) collective-permute-start(bf16[2,4,16,16,128]{4,3,2,1,0:T(8,128)(2,1)} %get-tuple-element.9), channel_id=1, source_target_pairs={{0,127},{1,2},{2,1},{3,4},{4,3},{5,6},{6,5},{7,8},{8,7},{9,10},{10... | collective-permute-start | bytes 1572872 | tf_op jit(solution)/shard_map/ppermute | solution.py:435
  17.0 18.3 %collective-permute-start.5 = (bf16[2,2,16,16,128]{4,3,2,1,0:T(8,128)(2,1)}, bf16[2,2,16,16,128]{4,3,2,1,0:T(8,128)(2,1)S(1)}, u32[]{:S(2)}, u32[]{:S(2)}) collective-permute-start(bf16[2,2,16,16,128]{4,3,2,1,0:T(8,128)(2,1)} %get-tuple-element.10), channel_id=1, source_target_pairs={{0,127},{1,2},{2,1},{3,4},{4,3},{5,6},{6,5},{7,8},{8,7},{9,10},{10... | collective-permute-start | bytes 786440 | tf_op jit(solution)/shard_map/ppermute | solution.py:435
  17.1 25.8 %collective-permute-start = (bf16[2,4,16,16,128]{4,3,2,1,0:T(8,128)(2,1)}, bf16[2,4,16,16,128]{4,3,2,1,0:T(8,128)(2,1)S(1)}, u32[]{:S(2)}, u32[]{:S(2)}) collective-permute-start(bf16[2,4,16,16,128]{4,3,2,1,0:T(8,128)(2,1)} %get-tuple-element.9), channel_id=1, source_target_pairs={{0,1},{1,0},{2,3},{3,2},{4,5},{5,4},{6,7},{7,6},{8,9},{9,8},{10,11... | collective-permute-start | bytes 1572872 | tf_op jit(solution)/shard_map/ppermute | solution.py:435
  17.1 18.3 %collective-permute-start.4 = (bf16[2,2,16,16,128]{4,3,2,1,0:T(8,128)(2,1)}, bf16[2,2,16,16,128]{4,3,2,1,0:T(8,128)(2,1)S(1)}, u32[]{:S(2)}, u32[]{:S(2)}) collective-permute-start(bf16[2,2,16,16,128]{4,3,2,1,0:T(8,128)(2,1)} %get-tuple-element.10), channel_id=1, source_target_pairs={{0,1},{1,0},{2,3},{3,2},{4,5},{5,4},{6,7},{7,6},{8,9},{9,8},{10,11... | collective-permute-start | bytes 786440 | tf_op jit(solution)/shard_map/ppermute | solution.py:435
  35.3 10.6 %collective-permute-start.6 = (bf16[2,16,16,128]{3,2,1,0:T(8,128)(2,1)S(1)}, bf16[2,16,16,128]{3,2,1,0:T(8,128)(2,1)S(1)}, u32[]{:S(2)}, u32[]{:S(2)}) collective-permute-start(bf16[2,16,16,128]{3,2,1,0:T(8,128)(2,1)S(1)} %dynamic-slice_bitcast_fusion.3), channel_id=1, source_target_pairs={{0,1},{1,0},{2,3},{3,2},{4,5},{5,4},{6,7},{7,6},{8,9},{9,8},{10,11... | collective-permute-start | bytes 393224 | tf_op jit(solution)/shard_map/ppermute | solution.py:435
  35.4 13.5 %collective-permute-start.7 = (bf16[2,16,16,128]{3,2,1,0:T(8,128)(2,1)S(1)}, bf16[2,16,16,128]{3,2,1,0:T(8,128)(2,1)S(1)}, u32[]{:S(2)}, u32[]{:S(2)}) collective-permute-start(bf16[2,16,16,128]{3,2,1,0:T(8,128)(2,1)S(1)} %dynamic-slice_bitcast_fusion.2), channel_id=1, source_target_pairs={{0,127},{1,2},{2,1},{3,4},{4,3},{5,6},{6,5},{7,8},{8,7},{9,10},{10... | collective-permute-start | bytes 393224 | tf_op jit(solution)/shard_map/ppermute | solution.py:435
  42.8 6.1 %copy-start = (bf16[256,512]{1,0:T(8,128)(2,1)S(1)}, bf16[256,512]{1,0:T(8,128)(2,1)}, u32[]{:S(2)}) copy-start(bf16[256,512]{1,0:T(8,128)(2,1)} %constant.45.taps) | copy-start | bytes 786436
  42.8 13.8 %collective-permute-start.2 = (bf16[4,16,16,128]{3,2,1,0:T(8,128)(2,1)S(1)}, bf16[4,16,16,128]{3,2,1,0:T(8,128)(2,1)S(1)}, u32[]{:S(2)}, u32[]{:S(2)}) collective-permute-start(bf16[4,16,16,128]{3,2,1,0:T(8,128)(2,1)S(1)} %dynamic-slice_bitcast_fusion.1), channel_id=1, source_target_pairs={{0,1},{1,0},{2,3},{3,2},{4,5},{5,4},{6,7},{7,6},{8,9},{9,8},{10,11... | collective-permute-start | bytes 786440 | tf_op jit(solution)/shard_map/ppermute | solution.py:435
  42.9 13.7 %collective-permute-start.3 = (bf16[4,16,16,128]{3,2,1,0:T(8,128)(2,1)S(1)}, bf16[4,16,16,128]{3,2,1,0:T(8,128)(2,1)S(1)}, u32[]{:S(2)}, u32[]{:S(2)}) collective-permute-start(bf16[4,16,16,128]{3,2,1,0:T(8,128)(2,1)S(1)} %dynamic-slice_bitcast_fusion), channel_id=1, source_target_pairs={{0,127},{1,2},{2,1},{3,4},{4,3},{5,6},{6,5},{7,8},{8,7},{9,10},{10... | collective-permute-start | bytes 786440 | tf_op jit(solution)/shard_map/ppermute | solution.py:435
  43.0 1.1 %copy-start.1 = (bf16[1,6,128,512]{3,2,1,0:T(8,128)(2,1)S(1)}, bf16[1,6,128,512]{3,2,1,0:T(8,128)(2,1)}, u32[]{:S(2)}) copy-start(bf16[1,6,128,512]{3,2,1,0:T(8,128)(2,1)} %param.8) | copy-start | bytes 2359300
  56.6 3.6 %copy-start.3 = (s32[1,128,512]{2,1,0:T(8,128)S(1)}, s32[1,128,512]{2,1,0:T(8,128)}, u32[]{:S(2)}) copy-start(s32[1,128,512]{2,1,0:T(8,128)} %param.6) | copy-start | bytes 786436

commit v7 on v6

--- a/solution.py
+++ b/solution.py
@@ -15,8 +15,6 @@
 HALVES = 16
 LANES = 128
 SLOTS = 512
-SIZES = (4, 2)
-STARTS = (0, 4)
 GROUP = 8
 WIDE = COLS + 1
 SLOT = GROUP + 1
@@ -69,9 +67,8 @@
     return limit
 
 
-def deposit_kernel(counts_far, cells_far, species_far, mix_far, own_far, sent0_far, sent1_far,
-                   counts, cells, species, mix, own, sent0, sent1, w_s, d_s, sems, out_sems, count_sem):
-    sent = [(sent0, k) for k in range(SIZES[0])] + [(sent1, k) for k in range(SIZES[1])]
+def deposit_kernel(counts_far, cells_far, species_far, mix_far, own_far, sent_far,
+                   counts, cells, species, mix, own, sent, w_s, d_s, sems, out_sems, count_sem):
 
     def fetches(r):
         rows = pl.ds(pl.multiple_of(r * COLS, COLS), COLS)
@@ -85,7 +82,7 @@
         part = pl.ds(2 * r, 2)
         return [
             pltpu.make_async_copy(near.at[:, :, part], far.at[:, :, part], out_sems.at[i, r])
-            for i, (near, far) in enumerate(((sent0, sent0_far), (sent1, sent1_far), (own, own_far)))
+            for i, (near, far) in enumerate(((sent, sent_far), (own, own_far)))
         ]
 
     count_copy = pltpu.make_async_copy(counts_far, counts, count_sem)
@@ -127,7 +124,7 @@
                 for h in range(2):
                     value = d_s[h, (z * 8 + k) * WIDE:(z * 8 + k) * WIDE + COLS]
                     own[z, k, 2 * r + h] = value
-                    sent[k][0][z, sent[k][1], 2 * r + h] = value.astype(bf16)
+                    sent[z, k, 2 * r + h] = value.astype(bf16)
         for copy in results(r):
             copy.start()
         return carry
@@ -149,23 +146,21 @@
         deposit_kernel,
         name="deposit",
         in_specs=[pl.BlockSpec(memory_space=FAR)] * 4,
-        out_specs=[pl.BlockSpec(memory_space=FAR)] * 3,
+        out_specs=[pl.BlockSpec(memory_space=FAR)] * 2,
         scratch_shapes=[
             pltpu.SMEM((ROWS * COLS,), jnp.int32),
             pltpu.VMEM((ROWS * COLS, SLOTS), jnp.int32),
             pltpu.VMEM((ROWS * COLS, SLOTS), jnp.int32),
             pltpu.VMEM((SPECIES, ROWS * COLS, SLOTS), bf16),
             pltpu.VMEM((2, SPECIES) + half, f32),
-            pltpu.VMEM((2, SIZES[0]) + half, bf16),
-            pltpu.VMEM((2, SIZES[1]) + half, bf16),
+            pltpu.VMEM((2, SPECIES) + half, bf16),
             pltpu.VMEM((4, 16 * WIDE, LANES), f32),
             pltpu.VMEM((2, 16 * WIDE, LANES), f32),
             pltpu.SemaphoreType.DMA((3, ROWS)),
-            pltpu.SemaphoreType.DMA((3, ROWS)),
+            pltpu.SemaphoreType.DMA((2, ROWS)),
             pltpu.SemaphoreType.DMA,
         ],
-        out_shape=[jax.ShapeDtypeStruct((2, SPECIES) + half, f32)]
-        + [jax.ShapeDtypeStruct((2, size) + half, bf16) for size in SIZES],
+        out_shape=[jax.ShapeDtypeStruct((2, SPECIES) + half, dtype) for dtype in (f32, bf16)],
         compiler_params=pltpu.CompilerParams(vmem_limit_bytes=LIMIT * MIB),
         cost_estimate=pl.CostEstimate(flops=10**9, bytes_accessed=5 * 10**6, transcendentals=0),
     )(*(pltpu.with_memory_space_constraint(v, FAR) for v in (counts, cells, species, mix)))
@@ -237,12 +232,12 @@
     return top, (v - top.astype(f32)).astype(bf16)
 
 
-def smooth_kernel(size, planes, even_ref, taps, own, near_a, near_b, *refs):
+def smooth_kernel(planes, even_ref, taps, own, near_a, near_b, *refs):
     flat, slopes = 0 in planes, 2 in planes
     far_a, far_b = refs[:2] if slopes else (None, None)
     ready, x_s, y_s, w_s, g_s = refs[-5:]
     outs = (0, 1, 2, 3) * flat + (4, 5) * slopes
-    rows_of = rows_per_species(planes)
+    rows_of, count = ROWS_OF[planes]
     k = pl.program_id(0)
     lane = lax.broadcasted_iota(jnp.int32, (COLS, LANES), 1)
     col = lane & 15
@@ -301,17 +296,15 @@
         for h in range(HALVES):
             g_s[h, pl.ds((k * rows_of + i) * WIDE, COLS)] = out[h * COLS:(h + 1) * COLS]
 
-    if rows_of > len(outs):
+    if count > rows_of * SPECIES:
         @pl.when(k == 0)
         def _():
-            zero = jnp.zeros((HALVES, (rows_of - len(outs)) * WIDE, LANES), f32)
-            for i in range(size):
-                g_s[:, (i * rows_of + len(outs)) * WIDE:(i + 1) * rows_of * WIDE] = zero
-
-    @pl.when(k == size - 1)
+            g_s[:, rows_of * SPECIES * WIDE:] = jnp.zeros(
+                (HALVES, (count - rows_of * SPECIES) * WIDE, LANES), f32
+            )
+
+    @pl.when(k == SPECIES - 1)
     def _():
-        count = rows_of * size
-
         def one_row(r, carry):
             for q in range(COLS):
                 for h in range(2):
@@ -325,25 +318,25 @@
         lax.fori_loop(0, ROWS, one_row, 0)
 
 
-def rows_per_species(planes):
-    return {(0, 1): 4, (2, 3): 2, (0, 1, 2, 3): 8}[planes]
-
-
-def smooth(chunk, planes, even, taps, own, *halos):
-    size, start = SIZES[chunk], STARTS[chunk]
+FLAT = (0, 1)
+SLOPES = (2, 3)
+ROWS_OF = {FLAT: (4, 24), SLOPES: (2, 16)}
+
+
+def smooth(planes, even, taps, own, *halos):
+    _, count = ROWS_OF[planes]
     half = (HALVES, COLS, LANES)
-    count = rows_per_species(planes) * size
     outs = sum(2 if plane < 2 else 1 for plane in planes)
     two = pl.BlockSpec((2, 1) + half, lambda k: (0, k, 0, 0, 0))
     one = pl.BlockSpec((1,) + half, lambda k: (k, 0, 0, 0))
     return pl.pallas_call(
-        functools.partial(smooth_kernel, size, planes),
+        functools.partial(smooth_kernel, planes),
         name="smooth",
-        grid=(size,),
+        grid=(SPECIES,),
         in_specs=[
             pl.BlockSpec(memory_space=SM),
             pl.BlockSpec((2 * LANES, 4 * LANES), lambda k: (0, 0)),
-            pl.BlockSpec((2, 1) + half, lambda k: (0, start + k, 0, 0, 0)),
+            pl.BlockSpec((2, 1) + half, lambda k: (0, k, 0, 0, 0)),
         ]
         + ([two, two, one, one] if 2 in planes else [two, two]),
         out_specs=pl.BlockSpec((ROWS * COLS, 2 * count, 2 * LANES), lambda k: (0, 0, 0)),
@@ -359,27 +352,19 @@
     )(even, taps, own, *halos)
 
 
-FLAT = (0, 1)
-SLOPES = (2, 3)
-
-
 def row_of(k, p):
-    if k < 4:
-        return k * 4 + p if p < 4 else 16 + k * 2 + p - 4
-    return 24 + (k - 4) * 8 + p
-
-
-def pick_kernel(cells, flat0, slopes0, ready1, mixed, forces, got_s):
+    return k * 4 + p if p < 4 else 24 + k * 2 + p - 4
+
+
+def pick_kernel(cells, flat, slopes, mixed, forces, got_s):
     def one_group(g, slot):
         first = pl.multiple_of(g * GROUP, GROUP)
         for b in range(GROUP):
             d = first + b
             table = table_of(*digits_of(cells[pl.ds(d, 1), :]), 16)
-            rows = jnp.concatenate([flat0[d], slopes0[d], ready1[d]], axis=0)
+            rows = jnp.concatenate([flat[d], slopes[d]], axis=0)
             got = jnp.dot(rows, table, preferred_element_type=f32)
-            got = jnp.concatenate(
-                [got[:16] + got[16:32], got[32:40] + got[40:48], got[48:64] + got[64:]], axis=0
-            )
+            got = jnp.concatenate([got[:24] + got[24:48], got[48:64] + got[64:]], axis=0)
             for t in range(4):
                 got_s[slot, t, pl.ds(b, 40, stride=SLOT)] = got[:, t * LANES:(t + 1) * LANES]
         for t in range(4):
@@ -408,7 +393,7 @@
     return pl.pallas_call(
         pick_kernel,
         name="pick",
-        in_specs=[pl.BlockSpec(memory_space=VM)] * 5,
+        in_specs=[pl.BlockSpec(memory_space=VM)] * 4,
         out_specs=pl.BlockSpec(memory_space=VM),
         out_shape=jax.ShapeDtypeStruct((3, ROWS * COLS, SLOTS), f32),
         scratch_shapes=[pltpu.VMEM((4, 4, 40 * SLOT, LANES), f32)],
@@ -427,24 +412,20 @@
     chis = 0.5 * (chi + chi.T) * (1.0 - jnp.eye(SPECIES, dtype=f32))
     mix_matrix = -0.5 * (chis + 1.0)
     cells, species, mix, counts = send_cells[0], send_species[0], send_mix[0], send_counts[0]
-    own, *sent = deposit(counts, cells, species, mix)
+    own, sent = deposit(counts, cells, species, mix)
     taps = tap_matrices()
-    ready = []
-    for chunk in range(len(SIZES)):
-        def swap(value, pairs):
-            return lax.ppermute(value, axes, pairs)
-
-        near_a = swap(sent[chunk], swap_a)
-        near_b = swap(sent[chunk], swap_b)
-        far_a = swap(lax.dynamic_index_in_dim(near_b, 1 - odd, 0, False), swap_a)
-        far_b = swap(lax.dynamic_index_in_dim(near_a, odd, 0, False), swap_b)
-        if chunk == 0:
-            ready.append(smooth(chunk, FLAT, even, taps, own, near_a, near_b))
-            ready.append(smooth(chunk, SLOPES, even, taps, own, near_a, near_b, far_a, far_b))
-        else:
-            ready.append(smooth(chunk, FLAT + SLOPES, even, taps, own, near_a, near_b, far_a, far_b))
+
+    def swap(value, pairs):
+        return lax.ppermute(value, axes, pairs)
+
+    near_a = swap(sent, swap_a)
+    near_b = swap(sent, swap_b)
+    far_a = swap(lax.dynamic_index_in_dim(near_b, 1 - odd, 0, False), swap_a)
+    far_b = swap(lax.dynamic_index_in_dim(near_a, odd, 0, False), swap_b)
+    flat = smooth(FLAT, even, taps, own, near_a, near_b)
+    slopes = smooth(SLOPES, even, taps, own, near_a, near_b, far_a, far_b)
     mixed = mixing(counts, mix_matrix, species, mix)
-    return pick(cells, ready, mixed)[None]
+    return pick(cells, (flat, slopes), mixed)[None]
 
 
 def solution(mesh):

time: 67.4 us -> 63.4 us (0.941)
  starting transfers between devices: 16.8 us -> 12.9 us
  waiting for transfers between devices: 19.6 us -> 18.3 us
  Pallas kernels: 29.3 us -> 30.4 us
    ppermute x8 -> x4, starting transfers between devices: 16.8 us -> 12.9 us  [swap(): return lax.ppermute(value, axes, pairs)]
    ppermute x8 -> x4, waiting for transfers between devices: 19.6 us -> 18.3 us  [swap(): return lax.ppermute(value, axes, pairs)]
    pallas_call x3 -> x2, Pallas kernels: 11.3 us -> 12.2 us  [smooth(): pl.pallas_call(functools.partial(smooth_kernel, planes), name='smooth', g...]
  transfers between devices with their start and end apart: 8 -> 4, of which waited for: 2 -> 1; matrix products, arithmetic and copies ran while one was open for 0% -> 0% of each run, Pallas kernels for 14% -> 13%
where the time goes in v7:
time: 63.4 us; the launch traced here: 63 us
  Pallas kernels  30.4 us (48%)
  waiting for transfers between devices  18.3 us (29%)
  starting transfers between devices  12.9 us (20%)
  local copies, waits for them, and re-layouts  1.31 us (2%)
    ppermute x4, waiting for transfers between devices, swap(): return lax.ppermute(value, axes, pairs)  18.3 us
    ppermute x4, starting transfers between devices, swap(): return lax.ppermute(value, axes, pairs)  12.9 us
    pallas_call x2, Pallas kernels, smooth(): pl.pallas_call(functools.partial(smooth_kernel, planes), name='smooth', g...  12.2 us
    pallas_call x1, Pallas kernels, deposit(): pl.pallas_call(deposit_kernel, name='deposit', in_specs=[pl.BlockSpec(mem...  9.22 us
    pallas_call x1, Pallas kernels, pick(): pl.pallas_call(pick_kernel, name='pick', in_specs=[pl.BlockSpec(memory_sp...  7.26 us
    pallas_call x1, Pallas kernels, mixing(): pl.pallas_call(mixing_kernel, name='mixing', in_specs=[pl.BlockSpec(memor...  1.7 us
  transfers between devices with their start and end apart: 4, of which 1 were waited for; matrix products, arithmetic and copies ran while one was open for 0% of the time, Pallas kernels for 13%

profile of v7, /device:TPU:1, one launch (start us, length us, event | category | flops | bytes accessed | tf_op | source)
XLA Modules:
  0.0 63.0 jit_solution(15449672390756539278)
XLA Ops:
  0.0 0.0 copy-start.5
  0.0 0.0 copy-start.2
  0.0 0.0 copy-start.4
  0.0 9.2 %deposit.1 = (f32[2,6,16,16,128]{4,3,2,1,0:T(8,128)S(1)}, bf16[2,6,16,16,128]{4,3,2,1,0:T(8,128)(2,1)}) custom-call(s32[128]{0:T(128)} %bitcast.26, s32[128,512]{1,0:T(8,128)} %bitcast.24, s32[128,512]{1,0:T(8,128)} %bitcast.22, bf16[6,128,512]{2,1,0:T(8,128)(2,1)} %bitcast.20), custom_call_target="tpu_custom_call" | custom-call | flops 1000000000 | bytes 5000000 | tf_op jit(solution)/shard_map/deposit/pallas_call | solution.py:145
  9.2 7.7 %collective-permute-start.1 = (bf16[2,6,16,16,128]{4,3,2,1,0:T(8,128)(2,1)}, bf16[2,6,16,16,128]{4,3,2,1,0:T(8,128)(2,1)S(1)}, u32[]{:S(2)}, u32[]{:S(2)}) collective-permute-start(bf16[2,6,16,16,128]{4,3,2,1,0:T(8,128)(2,1)} %get-tuple-element.8), channel_id=1, source_target_pairs={{0,127},{1,2},{2,1},{3,4},{4,3},{5,6},{6,5},{7,8},{8,7},{9,10},{10... | collective-permute-start | bytes 2359304 | tf_op jit(solution)/shard_map/ppermute | solution.py:419
  16.9 0.0 collective-permute-start
  16.9 0.0 copy-done.5
  16.9 0.1 copy.7
  17.0 18.2 %collective-permute-done.1.near_b = bf16[2,6,16,16,128]{4,3,2,1,0:T(8,128)(2,1)S(1)} collective-permute-done((bf16[2,6,16,16,128]{4,3,2,1,0:T(8,128)(2,1)}, bf16[2,6,16,16,128]{4,3,2,1,0:T(8,128)(2,1)S(1)}, u32[]{:S(2)}, u32[]{:S(2)}) %collective-permute-start.1) | collective-permute-done | bytes 786464 | tf_op jit(solution)/shard_map/ppermute | solution.py:419
  35.2 0.0 copy-start
  35.3 0.1 collective-permute-start.2
  35.4 0.0 collective-permute-done.near_a
  35.4 5.1 %collective-permute-start.3 = (bf16[6,16,16,128]{3,2,1,0:T(8,128)(2,1)S(1)}, bf16[6,16,16,128]{3,2,1,0:T(8,128)(2,1)S(1)}, u32[]{:S(2)}, u32[]{:S(2)}) collective-permute-start(bf16[6,16,16,128]{3,2,1,0:T(8,128)(2,1)S(1)} %dynamic-slice_bitcast_fusion), channel_id=1, source_target_pairs={{0,127},{1,2},{2,1},{3,4},{4,3},{5,6},{6,5},{7,8},{8,7},{9,10},{10... | collective-permute-start | bytes 1179656 | tf_op jit(solution)/shard_map/ppermute | solution.py:419
  40.6 0.0 copy-done.2
  40.6 0.0 copy-done.4
  40.6 0.0 copy-start.1
  40.6 1.1 %copy-done.1 = bf16[1,6,128,512]{3,2,1,0:T(8,128)(2,1)S(1)} copy-done((bf16[1,6,128,512]{3,2,1,0:T(8,128)(2,1)S(1)}, bf16[1,6,128,512]{3,2,1,0:T(8,128)(2,1)}, u32[]{:S(2)}) %copy-start.1) | copy-done | bytes 786456
  41.7 1.7 %mixing.1.mixed = f32[6,128,512]{2,1,0:T(8,128)S(1)} custom-call(s32[128]{0:T(128)S(1)} %bitcast.27, f32[6,6]{1,0:T(8,128)S(1)} %fusion.3.mix_matrix, s32[128,512]{1,0:T(8,128)S(1)} %bitcast.23, bf16[6,128,512]{2,1,0:T(8,128)(2,1)S(1)} %bitcast.21), custom_call_target="tpu_custom_call" | custom-call | flops 1000000000 | bytes 4000000 | tf_op jit(solution)/shard_map/mixing/pallas_call | solution.py:187
  43.4 0.0 copy-done
  43.4 6.7 %smooth.2.flat = bf16[128,48,256]{2,1,0:T(8,128)(2,1)S(1)} custom-call(s32[1]{0:T(128)} %bitcast.1.even_ref, bf16[256,512]{1,0:T(8,128)(2,1)S(1)} %copy-done, f32[2,6,16,16,128]{4,3,2,1,0:T(8,128)S(1)} %get-tuple-element.7.own, bf16[2,6,16,16,128]{4,3,2,1,0:T(8,128)(2,1)S(1)} %collective-permute-done.near_a, ...), custom_call_target="tpu_custom_call" | custom-call | flops 1000000000 | bytes 4000000 | tf_op jit(solution)/shard_map/smooth/pallas_call | solution.py:332
  50.2 0.0 copy-start.3
  50.2 0.0 collective-permute-done.2.refs_0_
  50.2 0.0 collective-permute-done.3.refs_1_
  50.2 5.5 %smooth.3.slopes = bf16[128,32,256]{2,1,0:T(8,128)(2,1)S(1)} custom-call(s32[1]{0:T(128)} %bitcast.1.even_ref, bf16[256,512]{1,0:T(8,128)(2,1)S(1)} %copy-done, f32[2,6,16,16,128]{4,3,2,1,0:T(8,128)S(1)} %get-tuple-element.7.own, bf16[2,6,16,16,128]{4,3,2,1,0:T(8,128)(2,1)S(1)} %collective-permute-done.near_a, ...), custom_call_target="tpu_custom_call" | custom-call | flops 1000000000 | bytes 4000000 | tf_op jit(solution)/shard_map/smooth/pallas_call | solution.py:332
  55.7 0.0 copy-done.3
  55.7 7.3 %pick.1 = f32[3,128,512]{2,1,0:T(8,128)} custom-call(s32[128,512]{1,0:T(8,128)S(1)} %bitcast.25, bf16[128,48,256]{2,1,0:T(8,128)(2,1)S(1)} %smooth.2.flat, bf16[128,32,256]{2,1,0:T(8,128)(2,1)S(1)} %smooth.3.slopes, f32[6,128,512]{2,1,0:T(8,128)S(1)} %mixing.1.mixed), custom_call_target="tpu_custom_call" | custom-call | flops 6000000000 | bytes 10000000 | tf_op jit(solution)/shard_map/pick/pallas_call | solution.py:393
  (3 shorter events, 0.1 us)
Async XLA Ops:
  0.0 16.9 %copy-start.5 = (f32[6,6]{1,0:T(8,128)S(1)}, f32[6,6]{1,0:T(8,128)}, u32[]{:S(2)}) copy-start(f32[6,6]{1,0:T(8,128)} %param.10) | copy-start | bytes 436
  0.0 40.6 %copy-start.2 = (s32[1,128,512]{2,1,0:T(8,128)S(1)}, s32[1,128,512]{2,1,0:T(8,128)}, u32[]{:S(2)}) copy-start(s32[1,128,512]{2,1,0:T(8,128)} %param.7) | copy-start | bytes 786436
  0.0 40.6 %copy-start.4 = (s32[1,128]{1,0:T(1,128)S(1)}, s32[1,128]{1,0:T(1,128)}, u32[]{:S(2)}) copy-start(s32[1,128]{1,0:T(1,128)} %param.9) | copy-start | bytes 1540
  9.2 26.0 %collective-permute-start.1 = (bf16[2,6,16,16,128]{4,3,2,1,0:T(8,128)(2,1)}, bf16[2,6,16,16,128]{4,3,2,1,0:T(8,128)(2,1)S(1)}, u32[]{:S(2)}, u32[]{:S(2)}) collective-permute-start(bf16[2,6,16,16,128]{4,3,2,1,0:T(8,128)(2,1)} %get-tuple-element.8), channel_id=1, source_target_pairs={{0,127},{1,2},{2,1},{3,4},{4,3},{5,6},{6,5},{7,8},{8,7},{9,10},{10... | collective-permute-start | bytes 2359304 | tf_op jit(solution)/shard_map/ppermute | solution.py:419
  16.9 18.4 %collective-permute-start = (bf16[2,6,16,16,128]{4,3,2,1,0:T(8,128)(2,1)}, bf16[2,6,16,16,128]{4,3,2,1,0:T(8,128)(2,1)S(1)}, u32[]{:S(2)}, u32[]{:S(2)}) collective-permute-start(bf16[2,6,16,16,128]{4,3,2,1,0:T(8,128)(2,1)} %get-tuple-element.8), channel_id=1, source_target_pairs={{0,1},{1,0},{2,3},{3,2},{4,5},{5,4},{6,7},{7,6},{8,9},{9,8},{10,11... | collective-permute-start | bytes 2359304 | tf_op jit(solution)/shard_map/ppermute | solution.py:419
  35.2 8.2 %copy-start = (bf16[256,512]{1,0:T(8,128)(2,1)S(1)}, bf16[256,512]{1,0:T(8,128)(2,1)}, u32[]{:S(2)}) copy-start(bf16[256,512]{1,0:T(8,128)(2,1)} %constant.39.taps) | copy-start | bytes 786436
  35.3 14.9 %collective-permute-start.2 = (bf16[6,16,16,128]{3,2,1,0:T(8,128)(2,1)S(1)}, bf16[6,16,16,128]{3,2,1,0:T(8,128)(2,1)S(1)}, u32[]{:S(2)}, u32[]{:S(2)}) collective-permute-start(bf16[6,16,16,128]{3,2,1,0:T(8,128)(2,1)S(1)} %dynamic-slice_bitcast_fusion.1), channel_id=1, source_target_pairs={{0,1},{1,0},{2,3},{3,2},{4,5},{5,4},{6,7},{7,6},{8,9},{9,8},{10,11... | collective-permute-start | bytes 1179656 | tf_op jit(solution)/shard_map/ppermute | solution.py:419
  35.4 14.8 %collective-permute-start.3 = (bf16[6,16,16,128]{3,2,1,0:T(8,128)(2,1)S(1)}, bf16[6,16,16,128]{3,2,1,0:T(8,128)(2,1)S(1)}, u32[]{:S(2)}, u32[]{:S(2)}) collective-permute-start(bf16[6,16,16,128]{3,2,1,0:T(8,128)(2,1)S(1)} %dynamic-slice_bitcast_fusion), channel_id=1, source_target_pairs={{0,127},{1,2},{2,1},{3,4},{4,3},{5,6},{6,5},{7,8},{8,7},{9,10},{10... | collective-permute-start | bytes 1179656 | tf_op jit(solution)/shard_map/ppermute | solution.py:419
  40.6 1.1 %copy-start.1 = (bf16[1,6,128,512]{3,2,1,0:T(8,128)(2,1)S(1)}, bf16[1,6,128,512]{3,2,1,0:T(8,128)(2,1)}, u32[]{:S(2)}) copy-start(bf16[1,6,128,512]{3,2,1,0:T(8,128)(2,1)} %param.8) | copy-start | bytes 2359300
  50.2 5.6 %copy-start.3 = (s32[1,128,512]{2,1,0:T(8,128)S(1)}, s32[1,128,512]{2,1,0:T(8,128)}, u32[]{:S(2)}) copy-start(s32[1,128,512]{2,1,0:T(8,128)} %param.6) | copy-start | bytes 786436
